TPU v7x, 512 devices: a whole 4x8x8 slice. The times are simulated.
512 devices in a mesh: gx: 8 (over z_hi, x), gy: 8 (over y), gz: 8 (over z_lo, core).
Axes of the slice: x: 4, y: 8, z: 8 (z_hi: 2, z_lo: 4; z = z_hi * 4 + z_lo), core: 2. Of those that a mesh axis runs over, the one named last changes fastest.
Arguments:
- features: float32 [2048, 64, 512], P(('gx', 'gy', 'gz')), may hold values from -6 to 6
- preact: float32 [2048, 64, 512], P(('gx', 'gy', 'gz')), may hold values from -10 to 10
- cotangent: float32 [2048, 64, 512], P(('gx', 'gy', 'gz')), may hold values from -6 to 6
- kernel: float32 [27, 64, 64], replicated, may hold values from -0.15625 to 0.15625
- active: int32 [2048, 512], P(('gx', 'gy', 'gz')), may hold values from 0 to 1, as said below
- owner_dir: int32 [2048, 27], P(('gx', 'gy', 'gz')), may hold values from 0 to 27, as said below
- owner_slot: int32 [2048, 27], P(('gx', 'gy', 'gz')), may hold values from 0 to 3, as said below
- send_list: int32 [1536], P(('gx', 'gy', 'gz')), may hold values from 0 to 4, as said below
Outputs:
- input_grad: float32 [2048, 64, 512], P(('gx', 'gy', 'gz'))
- kernel_grad: float32 [27, 64, 64], replicated
- bias_grad: float32 [64], replicated
Inputs may be any that keep to these rules, and one draw needn't show every extreme that they name: `owner_dir`: 27 where the neighbouring block is empty or the stored entry is unused; 13 for a block of the same partition; else the offset of the owner's grid position, 9 (dx + 1) + 3 (dy + 1) + (dz + 1), with dx, dy, dz each -1, 0 or 1. A named partition always exists and lists the block in its send list. `owner_slot`: own stored index where owner_dir is 13, position in the owner's send list where owner_dir names another partition, 0 where it is 27. `send_list`: each partition's 3 entries hold, increasing, the distinct stored indices of its occupied blocks in the partition's outer layer of blocks (on faces, edges or corners), each of which touches another partition, then 4 for unused entries; some partition fills all 3. 1 for active voxels of an occupied stored block, 0 elsewhere; unused stored entries are 0 throughout; some partition has all 4 entries occupied.
All inputs are finite; a program needn't handle non-finite values.
Results may differ from a plain program's by a relative error of at most 0.0001.
Values sent between devices are 32-bit elements; how exact they have to be, the bound alone decides.
No kernel may reach another device: no remote copies, remote signals or barrier semaphores. Data moves between devices by JAX's collectives and lax.ppermute only.
A program may use at most 64 MiB of HBM per device.

v0:
```python
import jax
import jax.numpy as jnp
from jax import lax
from jax.sharding import PartitionSpec as P

BS = 8


def padded_2(cells, sides, width):
    for axis, dim in sides:
        count = lax.axis_size(axis)
        ends = count - 1
        head = lax.slice_in_dim(cells, 0, width, axis=dim)
        tail = lax.slice_in_dim(cells, cells.shape[dim] - width, cells.shape[dim], axis=dim)
        cells = jnp.concatenate(
            [
                lax.ppermute(tail, axis, [(i, (i + 1) % count) for i in range(ends)]),
                cells,
                lax.ppermute(head, axis, [((i + 1) % count, i) for i in range(ends)]),
            ],
            axis=dim,
        )
    return cells


def silu_slope(preact):
    sigmoid_value = jax.nn.sigmoid(preact)
    return sigmoid_value * (1.0 + preact * (1.0 - sigmoid_value))


def shifted_stack(padded, direction, extent):
    windows = []
    for offset_x in (-1, 0, 1):
        for offset_y in (-1, 0, 1):
            for offset_z in (-1, 0, 1):
                begin_x = 1 + direction * offset_x
                begin_y = 1 + direction * offset_y
                begin_z = 1 + direction * offset_z
                window = padded[
                    :,
                    begin_x : begin_x + extent,
                    begin_y : begin_y + extent,
                    begin_z : begin_z + extent,
                ]
                windows.append(window.reshape(padded.shape[0], extent**3))
    return jnp.stack(windows)


def slice_length(heading, extent):
    length = 1
    for move in heading:
        length = length * (extent if move == 0 else 1)
    return length


def cut_slice(cubes, heading, extent):
    ranges = [
        slice(extent - 1, extent) if move == 1 else slice(0, 1) if move == -1 else slice(0, extent)
        for move in heading
    ]
    portion = cubes[:, :, ranges[0], ranges[1], ranges[2]]
    return portion.reshape(cubes.shape[0], cubes.shape[1], -1)


def remote_piece(sheet_row, owner_offset, block_offset, extent):
    sheet_side = tuple((-move for move in owner_offset))
    block_side = tuple((-move for move in block_offset))
    lengths = tuple((extent if move == 0 else 1 for move in sheet_side))
    shaped = sheet_row.reshape((sheet_row.shape[0],) + lengths)
    ranges = []
    for sheet_move, block_move in zip(sheet_side, block_side):
        if sheet_move == 0 and block_move == 1:
            ranges.append(slice(extent - 1, extent))
        elif sheet_move == 0 and block_move == -1:
            ranges.append(slice(0, 1))
        else:
            ranges.append(slice(None))
    return shaped[:, ranges[0], ranges[1], ranges[2]]


def options_along(move):
    return (0,) if move == 0 else (0, move)


def gather_cube(own_cubes, sheets, targets, slots, extent, listed):
    anchor = jnp.zeros((), jnp.int32)
    blocks, width = (own_cubes.shape[0], own_cubes.shape[1])
    remote_row = jnp.clip(slots, 0, listed - 1)
    own_row = jnp.clip(slots, 0, blocks - 1)
    layers = []
    for place_x in range(3):
        strips = []
        for place_y in range(3):
            pieces = []
            for place_z in range(3):
                places = (place_x, place_y, place_z)
                block_offset = (place_x - 1, place_y - 1, place_z - 1)
                index = place_x * 9 + place_y * 3 + place_z
                begins = [anchor + (extent - 1 if where_at == 0 else 0) for where_at in places]
                lengths = [extent if where_at == 1 else 1 for where_at in places]
                code_here = targets[index]
                own_part = lax.dynamic_slice(
                    own_cubes, [own_row[index], anchor] + begins, [1, width] + lengths
                )[0]
                piece = jnp.where(code_here == 13, own_part, jnp.zeros_like(own_part))
                for move_x in options_along(block_offset[0]):
                    for move_y in options_along(block_offset[1]):
                        for move_z in options_along(block_offset[2]):
                            owner_offset = (move_x, move_y, move_z)
                            if owner_offset == (0, 0, 0):
                                continue
                            code = 9 * (move_x + 1) + 3 * (move_y + 1) + (move_z + 1)
                            sheet_row = lax.dynamic_index_in_dim(
                                sheets[owner_offset], remote_row[index], 0, keepdims=False
                            )
                            piece = jnp.where(
                                code_here == code,
                                remote_piece(sheet_row, owner_offset, block_offset, extent),
                                piece,
                            )
                pieces.append(piece)
            strips.append(jnp.concatenate(pieces, axis=3))
        layers.append(jnp.concatenate(strips, axis=2))
    return jnp.concatenate(layers, axis=1)


def shards(features, preact, cotangent, kernel, active, owner_dir, owner_slot, send_list):
    blocks, channels, volume = features.shape
    extent = BS
    listed = send_list.shape[0]
    voxel_mask = active.astype(jnp.float32)[:, None, :]
    gradient = cotangent * silu_slope(preact) * voxel_mask
    masked_input = features * voxel_mask
    keep_mask = (send_list < blocks).astype(jnp.float32)[:, None, None]
    picked = jnp.minimum(send_list, blocks - 1)
    grad_pack = gradient[picked] * keep_mask
    payload = jnp.concatenate([grad_pack, masked_input[picked] * keep_mask], axis=1)
    own_all = jnp.concatenate([gradient, masked_input], axis=1)
    width_all = payload.shape[1]
    cubes = payload.reshape(listed, width_all, extent, extent, extent)
    own_cubes = own_all.reshape(blocks, width_all, extent, extent, extent)
    headings = [
        (move_x, move_y, move_z)
        for move_x in (-1, 0, 1)
        for move_y in (-1, 0, 1)
        for move_z in (-1, 0, 1)
    ]
    centre = (0, 0, 0)
    sheets = {}
    layers = []
    for heading in headings:
        if heading == centre:
            layers.append(jnp.zeros((listed, width_all, extent * extent), jnp.float32))
        else:
            portion = cut_slice(cubes, heading, extent)
            layers.append(
                jnp.pad(portion, ((0, 0), (0, 0), (0, extent * extent - portion.shape[2])))
            )
    packed = jnp.stack(layers).reshape((3, 3, 3, listed, width_all, extent * extent))
    grown = padded_2(packed, (("gx", 0), ("gy", 1), ("gz", 2)), 1)
    for offset in headings:
        if offset != centre:
            backward = tuple((-move for move in offset))
            sheet = grown[2 + 2 * offset[0], 2 + 2 * offset[1], 2 + 2 * offset[2]]
            sheets[offset] = sheet[:, :, : slice_length(backward, extent)]

    def visit_block(running, inputs):
        kernel_partial, bias_partial = running
        targets, slots, own_grad, own_input, own_mask = inputs
        whole_cube = gather_cube(own_cubes, sheets, targets, slots, extent, listed)
        grad_windows = shifted_stack(whole_cube[:channels], -1, extent)
        block_result = (
            jnp.einsum("kio,kov->iv", kernel, grad_windows, precision=lax.Precision.HIGHEST)
            * own_mask
        )
        input_windows = shifted_stack(whole_cube[channels:], 1, extent)
        kernel_partial = kernel_partial + jnp.einsum(
            "kiv,ov->kio", input_windows, own_grad, precision=lax.Precision.HIGHEST
        )
        bias_partial = bias_partial + jnp.sum(own_grad, axis=1)
        return ((kernel_partial, bias_partial), block_result)

    initial = (
        jnp.zeros((27, channels, channels), jnp.float32),
        jnp.zeros((channels,), jnp.float32),
    )
    (kernel_partial, bias_partial), input_grad = lax.scan(
        visit_block, initial, (owner_dir, owner_slot, gradient, masked_input, voxel_mask)
    )
    kernel_total, bias_total = lax.psum((kernel_partial, bias_partial), ("gx", "gy", "gz"))
    scaling = (volume * blocks * lax.axis_size(("gx", "gy", "gz"))) ** (-0.5)
    return (input_grad, kernel_total * scaling, bias_total * scaling)


def solution(mesh):
    placed = (
        P(("gx", "gy", "gz"), None, None),
        P(("gx", "gy", "gz"), None, None),
        P(("gx", "gy", "gz"), None, None),
        P(),
        P(("gx", "gy", "gz"), None),
        P(("gx", "gy", "gz"), None),
        P(("gx", "gy", "gz"), None),
        P(("gx", "gy", "gz")),
    )
    return jax.shard_map(
        shards,
        mesh=mesh,
        in_specs=placed,
        out_specs=(P(("gx", "gy", "gz"), None, None), P(), P()),
        check_vma=False,
    )
```

profile of v0, /device:TPU:1, one launch (start us, length us, event | category | flops | bytes accessed | tf_op | source)
XLA Modules:
  0.0 2031.1 jit_solution(9067910962077913569)
XLA Ops:
  25.3 4.6 collective-permute-start
  29.9 10.2 collective-permute-done.1
  42.7 9.1 collective-permute-start.2
  53.1 28.4 %collective-permute-done.2 = f32[5,1,3,3,128,64]{4,5,3,2,1,0:T(8,128)S(1)} collective-permute-done((f32[5,1,3,3,128,64]{4,5,3,2,1,0:T(8,128)S(1)}, f32[5,1,3,3,128,64]{4,5,3,2,1,0:T(8,128)S(1)}, u32[]{:S(2)}, u32[]{:S(2)}) %collective-permute-start.2) | collective-permute-done | bytes 1474592 | tf_op jit(solution)/shard_map/ppermute | solution.py:17
  81.5 3.9 collective-permute-done.3
  85.5 2.7 pad_maximum_fusion.6
  88.2 4.8 collective-permute-start.5
  93.1 3.9 collective-permute-start.4
  104.3 18.6 collective-permute-done.5
  134.7 1583.7 %while.15 = (s32[]{:T(128)}, f32[27,64,64]{2,1,0:T(8,128)}, f32[64]{0:T(128)}, f32[4,64,512]{2,1,0:T(8,128)}, s32[4,27]{1,0:T(4,128)}, /*index=5*/s32[4,27]{1,0:...) while((s32[]{:T(128)}, f32[27,64,64]{2,1,0:T(8,128)}, ...), condition=%wide.region_2.3_spmd.clone, body=%wide.region_0.2_spmd.clone.sunk | while | flops 1361610112 | bytes 96052456 | solution.py:187
  373.9 2.5 fusion.234
  483.0 5.2 convolution_add_fusion.2
  527.0 3.1 fusion.240
  770.0 2.5 fusion.234
  879.1 5.2 convolution_add_fusion.2
  923.1 3.1 fusion.240
  1166.2 2.5 fusion.234
  1275.2 5.2 convolution_add_fusion.2
  1319.2 3.1 fusion.240
  1562.2 2.5 fusion.234
  1671.3 5.2 convolution_add_fusion.2
  1715.3 3.1 fusion.240
  1718.5 129.9 %psum.15 = f32[64]{0:T(128)S(1)} all-reduce(f32[64]{0:T(128)} %get-tuple-element.189), channel_id=1, replica_groups=mesh['gx'=8,'gy'=8,'gz'=8] {'gx','gy','gz'}, use_global_device_ids=true, to_apply=%region_4.5 | all-reduce | flops 64 | bytes 512 | tf_op jit(solution)/shard_map/psum | solution.py:190
  1848.9 173.2 %all-reduce.22.cloned.1.call-done = f32[27,64,64]{2,1,0:T(8,128)} async-done(((f32[27,64,64]{2,1,0:T(8,128)}), f32[27,64,64]{2,1,0:T(8,128)}) %all-reduce.22.cloned.1.call-update) | async-done | bytes 442384 | tf_op jit(solution)/shard_map/psum | solution.py:190
  (1305 shorter events, 878.3 us)
Async XLA Ops:
  7.2 2014.9 %all-reduce.22.cloned.1.call-start = ((), (), s32[]{:S(2)}) async-start(), calls=%async_computation | async-start | bytes 1769472 | tf_op jit(solution)/shard_map/psum | solution.py:190
  22.7 17.4 collective-permute-start.1
  25.3 17.0 collective-permute-start
  42.7 38.9 %collective-permute-start.2 = (f32[5,1,3,3,128,64]{4,5,3,2,1,0:T(8,128)S(1)}, f32[5,1,3,3,128,64]{4,5,3,2,1,0:T(8,128)S(1)}, u32[]{:S(2)}, u32[]{:S(2)}) collective-permute-start(f32[5,1,3,3,128,64]{4,5,3,2,1,0:T(8,128)S(1)} %get-tuple-element.752), channel_id=1, source_target_pairs={{0,8},{8,16},{16,24},{24,32},{32,40},{40,48},{48,56},{1,9},{9,17},... | collective-permute-start | bytes 4423688 | tf_op jit(solution)/shard_map/ppermute | solution.py:17
  51.8 33.7 %collective-permute-start.3 = (f32[5,1,3,3,128,64]{4,5,3,2,1,0:T(8,128)S(1)}, f32[5,1,3,3,128,64]{4,5,3,2,1,0:T(8,128)S(1)}, u32[]{:S(2)}, u32[]{:S(2)}) collective-permute-start(f32[5,1,3,3,128,64]{4,5,3,2,1,0:T(8,128)S(1)} %get-tuple-element.753), channel_id=1, source_target_pairs={{8,0},{16,8},{24,16},{32,24},{40,32},{48,40},{56,48},{9,1},{17,9},... | collective-permute-start | bytes 4423688 | tf_op jit(solution)/shard_map/ppermute | solution.py:19
  88.2 34.7 %collective-permute-start.5 = (f32[5,5,1,3,128,64]{4,5,3,2,1,0:T(8,128)}, f32[5,5,1,3,128,64]{4,5,3,2,1,0:T(8,128)}, u32[]{:S(2)}, u32[]{:S(2)}) collective-permute-start(f32[5,5,1,3,128,64]{4,5,3,2,1,0:T(8,128)} %get-tuple-element.750), channel_id=1, source_target_pairs={{1,0},{2,1},{3,2},{4,3},{5,4},{6,5},{7,6},{9,8},{10,9},{11,10},{12... | collective-permute-start | bytes 7372808 | tf_op jit(solution)/shard_map/ppermute | solution.py:19
  93.1 35.8 %collective-permute-start.4 = (f32[5,5,1,3,128,64]{4,5,3,2,1,0:T(8,128)}, f32[5,5,1,3,128,64]{4,5,3,2,1,0:T(8,128)}, u32[]{:S(2)}, u32[]{:S(2)}) collective-permute-start(f32[5,5,1,3,128,64]{4,5,3,2,1,0:T(8,128)} %get-tuple-element.751), channel_id=1, source_target_pairs={{0,1},{1,2},{2,3},{3,4},{4,5},{5,6},{6,7},{8,9},{9,10},{10,11},{11... | collective-permute-start | bytes 7372808 | tf_op jit(solution)/shard_map/ppermute | solution.py:17
  134.7 195.9 %copy-start.9 = (f32[3,128,64]{1,2,0:T(8,128)}, f32[3,128,64]{1,2,0:T(8,128)S(1)}, u32[]{:S(2)}) copy-start(f32[3,128,64]{1,2,0:T(8,128)S(1)} %get-tuple-element.1654) | copy-start | bytes 294916 | tf_op jit(solution)/shard_map/while
  134.7 195.9 %copy-start.11 = (f32[3,128,64]{1,2,0:T(8,128)}, f32[3,128,64]{1,2,0:T(8,128)S(1)}, u32[]{:S(2)}) copy-start(f32[3,128,64]{1,2,0:T(8,128)S(1)} %get-tuple-element.1664) | copy-start | bytes 294916 | tf_op jit(solution)/shard_map/while
  134.8 204.1 %copy-start.36 = (f32[3,128,8]{1,2,0:T(8,128)}, f32[3,128,8]{1,2,0:T(8,128)S(1)}, u32[]{:S(2)}) copy-start(f32[3,128,8]{1,2,0:T(8,128)S(1)} %get-tuple-element.1650) | copy-start | bytes 36868 | tf_op jit(solution)/shard_map/while
  134.8 205.5 %copy-start.7 = (f32[3,128,64]{1,2,0:T(8,128)}, f32[3,128,64]{1,2,0:T(8,128)S(1)}, u32[]{:S(2)}) copy-start(f32[3,128,64]{1,2,0:T(8,128)S(1)} %get-tuple-element.1652) | copy-start | bytes 294916 | tf_op jit(solution)/shard_map/while
  530.2 196.6 %copy-start.9 = (f32[3,128,64]{1,2,0:T(8,128)}, f32[3,128,64]{1,2,0:T(8,128)S(1)}, u32[]{:S(2)}) copy-start(f32[3,128,64]{1,2,0:T(8,128)S(1)} %get-tuple-element.1654) | copy-start | bytes 294916 | tf_op jit(solution)/shard_map/while
  530.2 196.6 %copy-start.11 = (f32[3,128,64]{1,2,0:T(8,128)}, f32[3,128,64]{1,2,0:T(8,128)S(1)}, u32[]{:S(2)}) copy-start(f32[3,128,64]{1,2,0:T(8,128)S(1)} %get-tuple-element.1664) | copy-start | bytes 294916 | tf_op jit(solution)/shard_map/while
  530.2 204.8 %copy-start.36 = (f32[3,128,8]{1,2,0:T(8,128)}, f32[3,128,8]{1,2,0:T(8,128)S(1)}, u32[]{:S(2)}) copy-start(f32[3,128,8]{1,2,0:T(8,128)S(1)} %get-tuple-element.1650) | copy-start | bytes 36868 | tf_op jit(solution)/shard_map/while
  530.2 206.2 %copy-start.7 = (f32[3,128,64]{1,2,0:T(8,128)}, f32[3,128,64]{1,2,0:T(8,128)S(1)}, u32[]{:S(2)}) copy-start(f32[3,128,64]{1,2,0:T(8,128)S(1)} %get-tuple-element.1652) | copy-start | bytes 294916 | tf_op jit(solution)/shard_map/while
  926.2 195.1 %copy-start.13 = (f32[3,128,64]{1,2,0:T(8,128)}, f32[3,128,64]{1,2,0:T(8,128)S(1)}, u32[]{:S(2)}) copy-start(f32[3,128,64]{1,2,0:T(8,128)S(1)} %get-tuple-element.1660) | copy-start | bytes 294916 | tf_op jit(solution)/shard_map/while
  926.3 196.6 %copy-start.9 = (f32[3,128,64]{1,2,0:T(8,128)}, f32[3,128,64]{1,2,0:T(8,128)S(1)}, u32[]{:S(2)}) copy-start(f32[3,128,64]{1,2,0:T(8,128)S(1)} %get-tuple-element.1654) | copy-start | bytes 294916 | tf_op jit(solution)/shard_map/while
  926.3 196.6 %copy-start.11 = (f32[3,128,64]{1,2,0:T(8,128)}, f32[3,128,64]{1,2,0:T(8,128)S(1)}, u32[]{:S(2)}) copy-start(f32[3,128,64]{1,2,0:T(8,128)S(1)} %get-tuple-element.1664) | copy-start | bytes 294916 | tf_op jit(solution)/shard_map/while
  926.3 204.8 %copy-start.36 = (f32[3,128,8]{1,2,0:T(8,128)}, f32[3,128,8]{1,2,0:T(8,128)S(1)}, u32[]{:S(2)}) copy-start(f32[3,128,8]{1,2,0:T(8,128)S(1)} %get-tuple-element.1650) | copy-start | bytes 36868 | tf_op jit(solution)/shard_map/while
  926.3 206.2 %copy-start.7 = (f32[3,128,64]{1,2,0:T(8,128)}, f32[3,128,64]{1,2,0:T(8,128)S(1)}, u32[]{:S(2)}) copy-start(f32[3,128,64]{1,2,0:T(8,128)S(1)} %get-tuple-element.1652) | copy-start | bytes 294916 | tf_op jit(solution)/shard_map/while
  1322.4 196.6 %copy-start.9 = (f32[3,128,64]{1,2,0:T(8,128)}, f32[3,128,64]{1,2,0:T(8,128)S(1)}, u32[]{:S(2)}) copy-start(f32[3,128,64]{1,2,0:T(8,128)S(1)} %get-tuple-element.1654) | copy-start | bytes 294916 | tf_op jit(solution)/shard_map/while
  1322.4 196.6 %copy-start.11 = (f32[3,128,64]{1,2,0:T(8,128)}, f32[3,128,64]{1,2,0:T(8,128)S(1)}, u32[]{:S(2)}) copy-start(f32[3,128,64]{1,2,0:T(8,128)S(1)} %get-tuple-element.1664) | copy-start | bytes 294916 | tf_op jit(solution)/shard_map/while
  1322.4 204.8 %copy-start.36 = (f32[3,128,8]{1,2,0:T(8,128)}, f32[3,128,8]{1,2,0:T(8,128)S(1)}, u32[]{:S(2)}) copy-start(f32[3,128,8]{1,2,0:T(8,128)S(1)} %get-tuple-element.1650) | copy-start | bytes 36868 | tf_op jit(solution)/shard_map/while
  1322.4 206.1 %copy-start.7 = (f32[3,128,64]{1,2,0:T(8,128)}, f32[3,128,64]{1,2,0:T(8,128)S(1)}, u32[]{:S(2)}) copy-start(f32[3,128,64]{1,2,0:T(8,128)S(1)} %get-tuple-element.1652) | copy-start | bytes 294916 | tf_op jit(solution)/shard_map/while
  (127 other events, 3432.2 us)
Sparse Core Ops, SparseCore 0:
  1718.6 303.3 all-reduce.21
where the time goes:
time: 2060 us; the launch traced here: 2030 us
  local copies, waits for them, and re-layouts  816 us (40%)
  loops' own time  706 us (34%)
  waiting for transfers between devices  237 us (12%)
  blocking collectives  130 us (6%)
  other arithmetic  70.3 us (3%)
  matrix products  33.2 us (2%)
  starting transfers between devices  25.1 us (1%)
    another operation x1, loops' own time, shards(): lax.scan(visit_block, initial, (owner_dir, owner_slot, gradient, masked_i...  706 us
    reshape x216, local copies, waits for them, and re-layouts, shifted_stack(): return jnp.stack(windows)  273 us
    slice x236, local copies, waits for them, and re-layouts, shifted_stack(): padded[:, begin_x:begin_x + extent, begin_y:begin_y + extent, begin_z:beg...  234 us
    while x496, local copies, waits for them, and re-layouts  215 us
    psum x1, waiting for transfers between devices, shards(): lax.psum((kernel_partial, bias_partial), ('gx', 'gy', 'gz'))  173 us
    psum x1, blocking collectives, shards(): lax.psum((kernel_partial, bias_partial), ('gx', 'gy', 'gz'))  130 us
  transfers between devices with their start and end apart: 7, of which 6 were waited for; matrix products, arithmetic and copies ran while one was open for 1% of the time, Pallas kernels for 0%

commit v1 on v0

v1 whole, which is shorter than its diff:
```python
import functools

import jax
import jax.numpy as jnp
import numpy as np
from jax import lax
from jax.experimental import pallas as pl
from jax.experimental.pallas import tpu as pltpu
from jax.sharding import Mesh, PartitionSpec as P

F32 = jnp.float32
BF16 = jnp.bfloat16
BS = 8
VOL = 512
LANES = 128
PAY = 1024
AX = ("gx", "gy", "zl", "core")
AXZ = ("zl", "core")

FACE = 64


def layout_of(blocks, listed):
    own = blocks * VOL
    face = listed * FACE
    edge = listed * BS
    corner = -(-listed // 8) * 8
    y_rows = face + 2 * edge
    z_rows = face + 4 * edge + 4 * corner
    starts = [own]
    for size in (face, face, y_rows, y_rows, z_rows):
        starts.append(starts[-1] + size)
    total = starts[-1] + z_rows
    return dict(face=face, edge=edge, corner=corner, y_rows=y_rows, z_rows=z_rows,
                starts=starts, total=total)


def log2(n):
    return int(n).bit_length() - 1


def piece_table(blocks, listed):
    lay = layout_of(blocks, listed)
    face, edge, corner, starts = lay["face"], lay["edge"], lay["corner"], lay["starts"]
    table = np.zeros((27, 28), np.int32)
    for o in range(27):
        off = (o // 9 - 1, o // 3 % 3 - 1, o % 3 - 1)
        if off == (0, 0, 0):
            continue
        fixed = [7 if v == -1 else 0 for v in off]
        axis = 0 if off[0] else (1 if off[1] else 2)
        plane = [i for i in range(3) if i != axis]
        for d in range(27):
            own = (d // 9 - 1, d // 3 % 3 - 1, d % 3 - 1)
            if any(v != 0 and v != w for v, w in zip(own, off)):
                continue
            side = [(v + 1) // 2 for v in own]
            if own == (0, 0, 0):
                base, mult, strides = 0, VOL, {0: 64, 1: 8, 2: 1}
            elif own[2]:
                base = starts[4 + side[2]]
                if own[0] and own[1]:
                    base += face + 4 * edge + corner * (side[1] * 2 + side[0])
                    mult, strides = 1, {}
                elif own[0]:
                    base += face + edge * side[0]
                    mult, strides = 8, {1: 1}
                elif own[1]:
                    base += face + 2 * edge + edge * side[1]
                    mult, strides = 8, {0: 1}
                else:
                    mult, strides = 64, {0: 8, 1: 1}
            elif own[1]:
                base = starts[2 + side[1]]
                if own[0]:
                    base += face + edge * side[0]
                    mult, strides = 8, {2: 1}
                else:
                    mult, strides = 64, {0: 8, 2: 1}
            else:
                base = starts[side[0]]
                mult, strides = 64, {1: 8, 2: 1}
            for i in range(3):
                if off[i] != 0:
                    base += fixed[i] * strides.get(i, 0)
            s1 = strides[plane[0]] if off[plane[0]] == 0 else 1
            s2 = strides[plane[1]] if off[plane[1]] == 0 else 1
            table[o, d] = base | log2(mult) << 12 | log2(s1) << 16 | log2(s2) << 20
    return table.reshape(-1)


def split_hl(value, mask):
    high = value.astype(BF16).astype(F32)
    return jnp.where(mask, high, value - high)


def prep_kernel(send, cot, pre, act, gd, xs, ys, zs):
    blocks = cot.shape[0]
    listed = send.shape[0]
    for b in range(blocks):
        p = pre[b]
        s = 1.0 / (1.0 + jnp.exp(-p))
        m = act[b : b + 1, :].astype(F32)
        g = cot[b] * (s * (1.0 + p * (1.0 - s))) * m
        gd[b * VOL : (b + 1) * VOL, :] = jnp.concatenate([g, g], axis=0).T
    for i in range(listed):
        r0 = pl.multiple_of(jnp.minimum(send[i], blocks - 1) * VOL, VOL)
        for side in range(2):
            f = 7 * side
            xs[side, i * 64 : (i + 1) * 64, :] = gd[pl.ds(r0 + f * 64, 64), :]
            for x in range(8):
                ys[side, i * 64 + x * 8 : i * 64 + x * 8 + 8, :] = gd[pl.ds(r0 + x * 64 + f * 8, 8), :]
            zs[side, i * 64 : (i + 1) * 64, :] = gd[pl.ds(r0 + f, 64, stride=8), :]


def pack_y_kernel(ys, rx0, rx1, out0, out1):
    face = ys.shape[1]
    listed = face // 64
    for side, out in ((0, out0), (1, out1)):
        f = 7 * side
        out[0:face, :] = ys[side]
        for j, rx in enumerate((rx0, rx1)):
            for s in range(listed):
                row = face + (j * listed + s) * 8
                out[row : row + 8, :] = rx[s * 64 + f * 8 : s * 64 + f * 8 + 8, :]


def pack_z_kernel(zs, rx0, rx1, ry0, ry1, out0, out1):
    face = zs.shape[1]
    listed = face // 64
    edge = listed * 8
    corner = -(-listed // 8) * 8
    for side, out in ((0, out0), (1, out1)):
        f = 7 * side
        out[0:face, :] = zs[side]
        for j, src in enumerate((rx0, rx1, ry0, ry1)):
            row = face + j * edge
            out[row : row + edge, :] = src[pl.ds(f, edge, stride=8), :]
        for j, src in enumerate((ry0, ry1)):
            for i in range(2):
                row = face + 4 * edge + corner * (2 * j + i)
                out[row : row + corner, :] = jnp.zeros((corner, LANES), F32)
                for s in range(listed):
                    at = face + i * edge + s * 8 + f
                    out[row + s : row + s + 1, :] = src[at : at + 1, :]


def main_kernel(gd, feat, act, kern, at, p, kg, rt, bias, z):
    b = pl.program_id(0)
    lane = lax.broadcasted_iota(jnp.int32, (VOL, LANES), 1) < 64

    @pl.when(b == 0)
    def _():
        kg[...] = jnp.zeros(kg.shape, F32)
        bias[...] = jnp.zeros(bias.shape, F32)
        for k in range(27):
            kx, c = k // 9, k % 9
            w = kern[k]
            wd = jnp.concatenate([w, w], axis=1)
            high = wd.astype(BF16)
            low = (wd - high.astype(F32)).astype(BF16)
            rt[kx * 128 : kx * 128 + 64, c * 128 : (c + 1) * 128] = high
            rt[kx * 128 + 64 : kx * 128 + 128, c * 128 : (c + 1) * 128] = low

    g = gd[...]
    bias[0:1, :] += jnp.sum(g, axis=0, keepdims=True)
    hl = split_hl(g, lane)
    row = lax.broadcasted_iota(jnp.int32, (VOL, LANES), 0)
    vy = (row // 8) % 8
    vz = row % 8
    for kz in (-1, 0, 1):
        if kz == 0:
            sz = hl
        elif kz == 1:
            sz = jnp.where(vz >= 1, pltpu.roll(hl, 1, 0), 0.0)
        else:
            sz = jnp.where(vz <= 6, pltpu.roll(hl, VOL - 1, 0), 0.0)
        for ky in (-1, 0, 1):
            if ky == 0:
                sy = sz
            elif ky == 1:
                sy = jnp.where(vy >= 1, pltpu.roll(sz, 8, 0), 0.0)
            else:
                sy = jnp.where(vy <= 6, pltpu.roll(sz, VOL - 8, 0), 0.0)
            c = (ky + 1) * 3 + kz + 1
            z[:, c * 128 : (c + 1) * 128] = sy.astype(BF16)

    f = feat[0] * act[pl.ds(b, 1), :].astype(F32)
    ff = jnp.concatenate([f, f], axis=0)
    half = lax.broadcasted_iota(jnp.int32, (LANES, VOL), 0) < 64
    a = split_hl(ff, half)
    at[...] = a.T
    zero = jnp.zeros((LANES, 64), F32)
    up = jnp.concatenate([zero, a[:, : VOL - 64]], axis=1)
    down = jnp.concatenate([a[:, 64:], zero], axis=1)
    a3 = jnp.concatenate([up, a, down], axis=0).astype(BF16)
    kg[...] += jnp.dot(a3, z[...], preferred_element_type=F32)
    p3 = lax.dot_general(z[...], rt[...], (((1,), (1,)), ((), ())), preferred_element_type=F32)
    p[...] = p3[:, 128:256]
    p[64:VOL, :] += p3[: VOL - 64, 256:384]
    p[0 : VOL - 64, :] += p3[64:, 0:128]


def nt(a, b):
    return lax.dot_general(a, b, (((1,), (1,)), ((), ())), preferred_element_type=F32)


def tn(a, b):
    return lax.dot_general(a, b, (((0,), (0,)), ((), ())), preferred_element_type=F32)


def plane_pieces(axis, sign):
    out = []
    for o in range(27):
        off = (o // 9 - 1, o // 3 % 3 - 1, o % 3 - 1)
        if off[axis] == sign and all(off[i] == 0 for i in range(axis)):
            r, q = [off[i] for i in range(3) if i != axis]
            out.append((o, r, q))
    return out


def halo_kernel(scale, od, os_, tb, core, gd, rx0, rx1, ry0, ry1, rz0, rz1, at, rt, kgm, bias, p, act,
                mine, other, ig, src, pb, pw, kg, pa, pay):
    blocks = od.shape[0]
    row = 0
    for ref in (gd, rx0, rx1, ry0, ry1, rz0, rz1):
        src[row : row + ref.shape[0], :] = ref[...]
        row += ref.shape[0]
    kg[...] = kgm[...]
    pa[...] = p[...]
    lane64 = lax.broadcasted_iota(jnp.int32, (64, LANES), 1) < 64

    def plane(b, axis, sign):
        face = 0 if sign == -1 else 7
        pb[...] = jnp.zeros(pb.shape, F32)
        for o, r, q in plane_pieces(axis, sign):
            d = od[b, o]

            @pl.when(d != 27)
            def _(o=o, r=r, q=q, d=d):
                code = tb[o * 28 + d]
                base = (code & 4095) + (os_[b, o] << ((code >> 12) & 15))
                sr = (code >> 16) & 15
                sq = (code >> 20) & 15
                for i in range(8 if r == 0 else 1):
                    for j in range(8 if q == 0 else 1):
                        at_r = i + 1 if r == 0 else (0 if r == -1 else 9)
                        at_q = 8 + j if q == 0 else (7 if q == -1 else 16)
                        row = base + (i << sr) + (j << sq)
                        pb[at_r, at_q : at_q + 1, :] = src[pl.ds(row, 1), :]

        for kr in (-1, 0, 1):
            for kq in (-1, 0, 1):
                win = pb[1 - kr : 9 - kr, 8 - kq : 16 - kq, :].reshape(64, LANES)
                c = (kr + 1) * 3 + kq + 1
                pw[:, c * 128 : (c + 1) * 128] = split_hl(win, lane64).astype(BF16)
        r0 = b * VOL
        k = 1 - sign
        if axis == 0:
            rows = pl.ds(pl.multiple_of(r0 + face * 64, 64), 64)
            ap = at[rows, :].astype(BF16)
            span = slice(k * 128, (k + 1) * 128)
            kg[span, :] += tn(ap, pw[...])
            pa[rows, :] += nt(pw[...], rt[span, :])
        elif axis == 1:
            starts = [pl.multiple_of(r0 + x * 64 + face * 8, 8) for x in range(8)]
            ap = jnp.concatenate([at[pl.ds(s, 8), :] for s in starts], axis=0).astype(BF16)
            acc = jnp.zeros((64, LANES), F32)
            cols = slice(k * 384, (k + 1) * 384)
            for i in range(3):
                part = pw[:, i * 384 : (i + 1) * 384]
                kg[i * 128 : (i + 1) * 128, cols] += tn(ap, part)
                acc = acc + nt(part, rt[i * 128 : (i + 1) * 128, cols])
            for x, s in enumerate(starts):
                pa[pl.ds(s, 8), :] += acc[x * 8 : x * 8 + 8, :]
        else:
            rows = pl.ds(r0 + face, 64, stride=8)
            ap = at[rows, :].astype(BF16)
            acc = jnp.zeros((64, LANES), F32)
            for i in range(3):
                for j in range(3):
                    part = pw[:, (i * 3 + j) * 128 : (i * 3 + j + 1) * 128]
                    cols = slice((j * 3 + k) * 128, (j * 3 + k + 1) * 128)
                    kg[i * 128 : (i + 1) * 128, cols] += tn(ap, part)
                    acc = acc + nt(part, rt[i * 128 : (i + 1) * 128, cols])
            pa[rows, :] = pa[rows, :] + acc

    def block(b, carry):
        for axis in range(3):
            for sign in (-1, 1):
                found = od[b, plane_pieces(axis, sign)[0][0]] != 27
                for o, _, _ in plane_pieces(axis, sign)[1:]:
                    found = found | (od[b, o] != 27)

                @pl.when(found)
                def _(axis=axis, sign=sign):
                    plane(b, axis, sign)

        return carry

    lax.fori_loop(0, blocks, block, 0)

    for n in range(28):
        t, odd = n // 2, n % 2
        if n < 27:
            kx, c = n // 9, n % 9
            lo, hi = c * 128, (c + 1) * 128
            u = kg[kx * 128 : kx * 128 + 64, lo:hi] + kg[kx * 128 + 64 : kx * 128 + 128, lo:hi]
            u = u + pltpu.roll(u, 64, 1)
        else:
            first = lax.broadcasted_iota(jnp.int32, (64, LANES), 0) == 0
            u = jnp.where(first, jnp.broadcast_to(bias[0:1, :], (64, LANES)), 0.0)
        if odd:
            pay[t * 64 : (t + 1) * 64, :] = jnp.where(lane64, held, u) * scale
        held = u
    pay[14 * 64 :, :] = jnp.zeros((PAY - 14 * 64, LANES), F32)
    me = core[0]
    mine[...] = pay[pl.ds(pl.multiple_of(me * (PAY // 2), PAY // 2), PAY // 2), :]
    other[...] = pay[pl.ds(pl.multiple_of((1 - me) * (PAY // 2), PAY // 2), PAY // 2), :]
    for b in range(blocks):
        og = pa[b * VOL : (b + 1) * VOL, :]
        og = (og + pltpu.roll(og, 64, 1)).T
        ig[b] = og[:64, :] * act[b : b + 1, :].astype(F32)


def unpack_kernel(core, mine, other, kout, bout, pay):
    me = core[0]
    pay[pl.ds(pl.multiple_of(me * (PAY // 2), PAY // 2), PAY // 2), :] = mine[...]
    pay[pl.ds(pl.multiple_of((1 - me) * (PAY // 2), PAY // 2), PAY // 2), :] = other[...]
    for t in range(14):
        tile = pay[t * 64 : (t + 1) * 64, :]
        turned = pltpu.roll(tile, 64, 1)
        kout[2 * t] = tile[:, :64]
        if t < 13:
            kout[2 * t + 1] = turned[:, :64]
        else:
            bout[...] = turned[0:1, :64]


VM = pl.BlockSpec(memory_space=pltpu.VMEM)
SM = pl.BlockSpec(memory_space=pltpu.SMEM)


def sds(shape, dtype=F32):
    return jax.ShapeDtypeStruct(shape, dtype)


def both_ways(low, high, axis):
    n = lax.axis_size(axis)
    up = lax.ppermute(high, axis, [(i, i + 1) for i in range(n - 1)])
    down = lax.ppermute(low, axis, [(i + 1, i) for i in range(n - 1)])
    return up, down


def shards(features, preact, cotangent, kernel, active, owner_dir, owner_slot, send_list):
    blocks, channels, volume = features.shape
    listed = send_list.shape[0]
    lay = layout_of(blocks, listed)
    face, yr, zr = lay["face"], lay["y_rows"], lay["z_rows"]
    devices = lax.axis_size(AX)
    me = lax.axis_index("core").astype(jnp.int32)
    core = me.reshape(1)
    scale = float((volume * blocks * devices) ** -0.5)

    gd, xs, ys, zs = pl.pallas_call(
        prep_kernel,
        out_shape=(sds((blocks * VOL, LANES)),) + (sds((2, face, LANES)),) * 3,
        in_specs=[SM, VM, VM, VM],
        out_specs=(VM,) * 4,
        name="prep",
    )(send_list, cotangent, preact, active)

    rx0, rx1 = both_ways(xs[0], xs[1], "gx")

    full = lambda shape: pl.BlockSpec(shape, lambda b: (0,) * len(shape))
    at, p, kgm, rt, bias = pl.pallas_call(
        main_kernel,
        grid=(blocks,),
        in_specs=[
            pl.BlockSpec((VOL, LANES), lambda b: (b, 0)),
            pl.BlockSpec((1, channels, VOL), lambda b: (b, 0, 0)),
            full((blocks, VOL)),
            full((27, channels, channels)),
        ],
        out_specs=(
            pl.BlockSpec((VOL, LANES), lambda b: (b, 0)),
            pl.BlockSpec((VOL, LANES), lambda b: (b, 0)),
            full((384, 1152)),
            full((384, 1152)),
            full((8, LANES)),
        ),
        out_shape=(
            sds((blocks * VOL, LANES)),
            sds((blocks * VOL, LANES)),
            sds((384, 1152)),
            sds((384, 1152), BF16),
            sds((8, LANES)),
        ),
        scratch_shapes=[pltpu.VMEM((VOL, 1152), BF16)],
        name="interior",
    )(gd, features, active, kernel)

    ys0, ys1 = pl.pallas_call(
        pack_y_kernel, out_shape=(sds((yr, LANES)),) * 2, in_specs=[VM] * 3, out_specs=(VM,) * 2,
        name="pack_y",
    )(ys, rx0, rx1)
    ry0, ry1 = both_ways(ys0, ys1, "gy")
    zs0, zs1 = pl.pallas_call(
        pack_z_kernel, out_shape=(sds((zr, LANES)),) * 2, in_specs=[VM] * 5, out_specs=(VM,) * 2,
        name="pack_z",
    )(zs, rx0, rx1, ry0, ry1)
    rz0, rz1 = both_ways(zs0, zs1, AXZ)

    table = jnp.asarray(piece_table(blocks, listed))
    mine, other, input_grad = pl.pallas_call(
        functools.partial(halo_kernel, scale),
        out_shape=(sds((PAY // 2, LANES)), sds((PAY // 2, LANES)), sds((blocks, channels, VOL))),
        in_specs=[SM] * 4 + [VM] * 13,
        out_specs=(VM,) * 3,
        scratch_shapes=[
            pltpu.VMEM((lay["total"], LANES), F32),
            pltpu.VMEM((10, 24, LANES), F32),
            pltpu.VMEM((64, 1152), BF16),
            pltpu.VMEM((384, 1152), F32),
            pltpu.VMEM((blocks * VOL, LANES), F32),
            pltpu.VMEM((PAY, LANES), F32),
        ],
        name="halo",
    )(owner_dir, owner_slot, table, core, gd, rx0, rx1, ry0, ry1, rz0, rz1, at, rt, kgm, bias, p, active)

    swap = [(0, 1), (1, 0)]
    peers_ax = ("gx", "gy", "zl")
    peers = lax.axis_size(peers_ax)
    half = mine + lax.ppermute(other, "core", swap)
    spread = lax.all_to_all(half.reshape(peers, PAY // 2 // peers, LANES), peers_ax, 0, 0, tiled=True)
    share = jnp.sum(spread, axis=0)
    copies = jnp.broadcast_to(share[None], spread.shape)
    whole = lax.all_to_all(copies, peers_ax, 0, 0, tiled=True).reshape(PAY // 2, LANES)
    rest = lax.ppermute(whole, "core", swap)

    kernel_grad, bias_grad = pl.pallas_call(
        unpack_kernel,
        out_shape=(sds((27, channels, channels)), sds((1, channels))),
        in_specs=[SM, VM, VM],
        out_specs=(VM,) * 2,
        scratch_shapes=[pltpu.VMEM((PAY, LANES), F32)],
        name="unpack",
    )(core, whole, rest)
    return input_grad, kernel_grad, bias_grad.reshape(channels)


def solution(mesh):
    shape = mesh.devices.shape
    fine = Mesh(mesh.devices.reshape(shape[0], shape[1], shape[2] // 2, 2), AX)
    placed = (
        P(AX, None, None),
        P(AX, None, None),
        P(AX, None, None),
        P(),
        P(AX, None),
        P(AX, None),
        P(AX, None),
        P(AX),
    )
    return jax.shard_map(
        shards,
        mesh=fine,
        in_specs=placed,
        out_specs=(P(AX, None, None), P(), P()),
        check_vma=False,
    )
```

time: 2060 us -> 132 us (0.06); the launches traced: 2030 us -> 131 us
  local copies, waits for them, and re-layouts: 816 us -> 3.74 us
  loops' own time: 706 us -> 0 us
  waiting for transfers between devices: 237 us -> 9 us
  other arithmetic: 70.3 us -> 1.27 us
  blocking collectives: 130 us -> 64.7 us
  matrix products: 33.2 us -> 0 us
  Pallas kernels: 0 us -> 23.9 us
    another operation x1 -> x0, loops' own time: 706 us -> none  [shards(): lax.scan(visit_block, initial, (owner_dir, owner_slot, gradient, masked_i...]
    reshape x232 -> x0, local copies, waits for them, and re-layouts: 285 us -> none  [the longest x216 273 us: shifted_stack(): return jnp.stack(windows)]
    slice x316 -> x0, local copies, waits for them, and re-layouts: 261 us -> none  [the longest x236 234 us: shifted_stack(): padded[:, begin_x:begin_x + extent, begin_y:begin_y + extent, begin_z:beg...]
    while x496 -> x0, local copies, waits for them, and re-layouts: 215 us -> none
    psum x1 -> x0, waiting for transfers between devices: 173 us -> none  [shards(): lax.psum((kernel_partial, bias_partial), ('gx', 'gy', 'gz'))]
    psum x1 -> x0, blocking collectives: 130 us -> none  [shards(): lax.psum((kernel_partial, bias_partial), ('gx', 'gy', 'gz'))]
    all_to_all x0 -> x2, blocking collectives: none -> 64.7 us  [the longest x1 42 us: shards(): lax.all_to_all(half.reshape(peers, PAY // 2 // peers, LANES), peers_ax, 0...]
    ppermute x6 -> x8, waiting for transfers between devices: 63.4 us -> 9 us  [the longest x3 3.73 us: both_ways(): down = lax.ppermute(low, axis, [(i + 1, i) for i in range(n - 1)])]
  transfers between devices with their start and end apart: 7 -> 8, of which waited for: 6 -> 6; matrix products, arithmetic and copies ran while one was open for 1% -> 0% of each run, Pallas kernels for 0% -> 7%
where the time goes in v1:
time: 132 us; the launch traced here: 131 us
  blocking collectives  64.7 us (49%)
  starting transfers between devices  27.5 us (21%)
  Pallas kernels  23.9 us (18%)
  waiting for transfers between devices  9 us (7%)
  local copies, waits for them, and re-layouts  3.74 us (3%)
    all_to_all x1, blocking collectives, shards(): lax.all_to_all(half.reshape(peers, PAY // 2 // peers, LANES), peers_ax, 0...  42 us
    all_to_all x1, blocking collectives, shards(): lax.all_to_all(copies, peers_ax, 0, 0, tiled=True).reshape(PAY // 2, LANES)  22.8 us
    ppermute x3, starting transfers between devices, both_ways(): up = lax.ppermute(high, axis, [(i, i + 1) for i in range(n - 1)])  15.1 us
    pallas_call x1, Pallas kernels, shards(): pl.pallas_call(main_kernel, grid=(blocks,), in_specs=[pl.BlockSpec((VOL,...  9.29 us
    pallas_call x1, Pallas kernels, shards(): pl.pallas_call(functools.partial(halo_kernel, scale), out_shape=(sds((PAY...  6.11 us
    ppermute x1, starting transfers between devices, shards(): rest = lax.ppermute(whole, 'core', swap)  5.42 us
    ppermute x3, starting transfers between devices, both_ways(): down = lax.ppermute(low, axis, [(i + 1, i) for i in range(n - 1)])  5.06 us
    ppermute x3, waiting for transfers between devices, both_ways(): down = lax.ppermute(low, axis, [(i + 1, i) for i in range(n - 1)])  3.73 us
  transfers between devices with their start and end apart: 8, of which 6 were waited for; matrix products, arithmetic and copies ran while one was open for 0% of the time, Pallas kernels for 7%

profile of v1, /device:TPU:1, one launch (start us, length us, event | category | flops | bytes accessed | tf_op | source)
XLA Modules:
  0.0 130.9 jit_solution(6095884730361394367)
XLA Ops:
  0.6 2.7 %prep.1 = (f32[2048,128]{1,0:T(8,128)}, f32[2,192,128]{2,1,0:T(8,128)}, f32[2,192,128]{2,1,0:T(8,128)}, f32[2,192,128]{2,1,0:T(8,128)}) custom-call(s32[3]{0:T(128)} %send.1, f32[4,64,512]{2,1,0:T(8,128)} %cot.1, f32[4,64,512]{2,1,0:T(8,128)} %pre.1, s32[4,512]{1,0:T(4,128)} %act.5), custom_call_target="tpu_custom_call" | custom-call | tf_op jit(solution)/shard_map/prep/pallas_call | solution.py:365
  3.3 1.0 slice_bitcast_fusion
  4.3 1.3 collective-permute-start.1
  5.6 4.6 %collective-permute-start = (f32[192,128]{1,0:T(8,128)S(1)}, f32[192,128]{1,0:T(8,128)S(1)}, u32[]{:S(2)}, u32[]{:S(2)}) collective-permute-start(f32[192,128]{1,0:T(8,128)S(1)} %get-tuple-element.40), channel_id=1, source_target_pairs={{0,64},{64,128},{128,192},{192,256},{256,320},{320,384},{384,448},... | collective-permute-start | bytes 294920 | tf_op jit(solution)/shard_map/ppermute | solution.py:350
  10.2 1.6 %collective-permute-done.rx0 = f32[192,128]{1,0:T(8,128)S(1)} collective-permute-done((f32[192,128]{1,0:T(8,128)S(1)}, f32[192,128]{1,0:T(8,128)S(1)}, u32[]{:S(2)}, u32[]{:S(2)}) %collective-permute-start) | collective-permute-done | bytes 98336 | tf_op jit(solution)/shard_map/ppermute | solution.py:350
  12.4 1.7 %pack_y.1 = (f32[240,128]{1,0:T(8,128)}, f32[240,128]{1,0:T(8,128)}) custom-call(f32[2,192,128]{2,1,0:T(8,128)} %get-tuple-element.23.ys, f32[192,128]{1,0:T(8,128)} %copy-done.2, f32[192,128]{1,0:T(8,128)} %copy-done.1), custom_call_target="tpu_custom_call" | custom-call | tf_op jit(solution)/shard_map/pack_y/pallas_call | solution.py:403
  14.2 3.4 %collective-permute-start.2 = (f32[240,128]{1,0:T(8,128)}, f32[240,128]{1,0:T(8,128)S(1)}, u32[]{:S(2)}, u32[]{:S(2)}) collective-permute-start(f32[240,128]{1,0:T(8,128)} %get-tuple-element.24), channel_id=1, source_target_pairs={{0,8},{8,16},{16,24},{24,32},{32,40},{40,48},{48,56},{1,9},{9,17},... | collective-permute-start | bytes 368648 | tf_op jit(solution)/shard_map/ppermute | solution.py:350
  17.6 1.3 collective-permute-start.3
  18.9 0.9 collective-permute-done.2.ry0
  19.8 3.7 %collective-permute-done.3.ry1 = f32[240,128]{1,0:T(8,128)S(1)} collective-permute-done((f32[240,128]{1,0:T(8,128)}, f32[240,128]{1,0:T(8,128)S(1)}, u32[]{:S(2)}, u32[]{:S(2)}) %collective-permute-start.3) | collective-permute-done | bytes 122912 | tf_op jit(solution)/shard_map/ppermute | solution.py:351
  24.1 1.9 %pack_z.1 = (f32[320,128]{1,0:T(8,128)}, f32[320,128]{1,0:T(8,128)}) custom-call(f32[2,192,128]{2,1,0:T(8,128)} %get-tuple-element.26.zs, f32[192,128]{1,0:T(8,128)} %copy-done.2, f32[192,128]{1,0:T(8,128)} %copy-done.1, f32[240,128]{1,0:T(8,128)} %copy-done.3, f32[240,128]{1,0:T(8,128)} %copy-done.4), custom_call_target="tpu_custom_call" | custom-call | tf_op jit(solution)/shard_map/pack_z/pallas_call | solution.py:408
  26.0 7.1 %collective-permute-start.4 = (f32[320,128]{1,0:T(8,128)}, f32[320,128]{1,0:T(8,128)S(1)}, u32[]{:S(2)}, u32[]{:S(2)}) collective-permute-start(f32[320,128]{1,0:T(8,128)} %get-tuple-element.27), channel_id=1, source_target_pairs={{0,1},{1,2},{2,3},{3,4},{4,5},{5,6},{6,7},{8,9},{9,10},{10,11},{11... | collective-permute-start | bytes 491528 | tf_op jit(solution)/shard_map/ppermute | solution.py:350
  33.1 2.5 %collective-permute-start.5 = (f32[320,128]{1,0:T(8,128)}, f32[320,128]{1,0:T(8,128)S(1)}, u32[]{:S(2)}, u32[]{:S(2)}) collective-permute-start(f32[320,128]{1,0:T(8,128)} %get-tuple-element.28), channel_id=1, source_target_pairs={{1,0},{2,1},{3,2},{4,3},{5,4},{6,5},{7,6},{9,8},{10,9},{11,10},{12... | collective-permute-start | bytes 491528 | tf_op jit(solution)/shard_map/ppermute | solution.py:351
  35.6 9.3 %interior.1 = (f32[2048,128]{1,0:T(8,128)}, f32[2048,128]{1,0:T(8,128)}, f32[384,1152]{1,0:T(8,128)}, bf16[384,1152]{1,0:T(8,128)(2,1)}, f32[8,128]{1,0:T(8,128)}) custom-call(f32[2048,128]{1,0:T(8,128)} %get-tuple-element.21.gd, f32[4,64,512]{2,1,0:T(8,128)} %feat.1, s32[4,512]{1,0:T(4,128)} %act.5, f32[27,64,64]{2,1,0:T(8,128)} %kern.1), custom_call_target="tpu_custom_call" | custom-call | tf_op jit(solution)/shard_map/interior/pallas_call | solution.py:376
  45.6 6.1 %halo.1 = (f32[512,128]{1,0:T(8,128)}, f32[512,128]{1,0:T(8,128)}, f32[4,64,512]{2,1,0:T(8,128)}) custom-call(s32[4,27]{1,0:T(4,128)} %od.1, s32[4,27]{1,0:T(4,128)} %os_.1, s32[756]{0:T(1024)} %constant.8.clone.tb, s32[1]{0:T(128)} %bitcast.core, f32[2048,128]{1,0:T(8,128)} %get-tuple-element.21.gd, f32[192,128]{1,0:T(8,128)} %copy-done.2, ...), custom_call_target="tpu_custom_call" | custom-call | tf_op jit(solution)/shard_map/halo/pallas_call | solution.py:415
  51.8 1.9 %collective-permute-start.6 = (f32[512,128]{1,0:T(8,128)}, f32[512,128]{1,0:T(8,128)S(1)}, u32[]{:S(2)}, u32[]{:S(2)}) collective-permute-start(f32[512,128]{1,0:T(8,128)} %get-tuple-element.36), channel_id=1, source_target_pairs={{0,1},{1,0},{2,3},{3,2},{4,5},{5,4},{6,7},{7,6},{8,9},{9,8},{10,11... | collective-permute-start | bytes 786440 | tf_op jit(solution)/shard_map/ppermute | solution.py:434
  53.7 1.7 %collective-permute-done.6 = f32[512,128]{1,0:T(8,128)S(1)} collective-permute-done((f32[512,128]{1,0:T(8,128)}, f32[512,128]{1,0:T(8,128)S(1)}, u32[]{:S(2)}, u32[]{:S(2)}) %collective-permute-start.6) | collective-permute-done | bytes 262176 | tf_op jit(solution)/shard_map/ppermute | solution.py:434
  55.4 1.0 add.3
  56.4 42.0 %all_to_all.10 = f32[256,2,128]{2,1,0:T(2,128)S(1)} all-to-all(f32[256,2,128]{2,1,0:T(2,128)S(1)} %bitcast.8), channel_id=1, replica_groups=mesh['gx'=8,'gy'=8,'zl'=4,'core'=2] {'gx','gy','zl'}, dimensions={0} | all-to-all | bytes 524288 | tf_op jit(solution)/shard_map/all_to_all | solution.py:435
  98.7 22.8 %all_to_all.11 = f32[256,2,128]{2,1,0:T(2,128)S(1)} all-to-all(f32[256,2,128]{2,1,0:T(2,128)S(1)} %broadcast_in_dim.2), channel_id=1, replica_groups=mesh['gx'=8,'gy'=8,'zl'=4,'core'=2] {'gx','gy','zl'}, dimensions={0} | all-to-all | bytes 524288 | tf_op jit(solution)/shard_map/all_to_all | solution.py:438
  121.5 5.4 %collective-permute-start.7 = (f32[512,128]{1,0:T(8,128)S(1)}, f32[512,128]{1,0:T(8,128)S(1)}, u32[]{:S(2)}, u32[]{:S(2)}) collective-permute-start(f32[512,128]{1,0:T(8,128)S(1)} %bitcast.9), channel_id=1, source_target_pairs={{0,1},{1,0},{2,3},{3,2},{4,5},{5,4},{6,7},{7,6},{8,9},{9,8},{10,11... | collective-permute-start | bytes 786440 | tf_op jit(solution)/shard_map/ppermute | solution.py:439
  126.9 1.1 collective-permute-done.7.other
  128.0 0.7 copy-done.5
  128.7 2.2 %unpack.1 = (f32[27,64,64]{2,1,0:T(8,128)}, f32[1,64]{1,0:T(1,128)}) custom-call(s32[1]{0:T(128)} %bitcast.core, f32[512,128]{1,0:T(8,128)} %bitcast.10, f32[512,128]{1,0:T(8,128)} %copy-done.5), custom_call_target="tpu_custom_call" | custom-call | tf_op jit(solution)/shard_map/unpack/pallas_call | solution.py:441
  (20 shorter events, 2.4 us)
Async XLA Ops:
  4.3 5.9 %collective-permute-start.1 = (f32[192,128]{1,0:T(8,128)S(1)}, f32[192,128]{1,0:T(8,128)S(1)}, u32[]{:S(2)}, u32[]{:S(2)}) collective-permute-start(f32[192,128]{1,0:T(8,128)S(1)} %get-tuple-element.39), channel_id=1, source_target_pairs={{64,0},{128,64},{192,128},{256,192},{320,256},{384,320},{448,384},... | collective-permute-start | bytes 294920 | tf_op jit(solution)/shard_map/ppermute | solution.py:351
  5.6 6.2 %collective-permute-start = (f32[192,128]{1,0:T(8,128)S(1)}, f32[192,128]{1,0:T(8,128)S(1)}, u32[]{:S(2)}, u32[]{:S(2)}) collective-permute-start(f32[192,128]{1,0:T(8,128)S(1)} %get-tuple-element.40), channel_id=1, source_target_pairs={{0,64},{64,128},{128,192},{192,256},{256,320},{320,384},{384,448},... | collective-permute-start | bytes 294920 | tf_op jit(solution)/shard_map/ppermute | solution.py:350
  10.2 1.6 %copy-start.1 = (f32[192,128]{1,0:T(8,128)}, f32[192,128]{1,0:T(8,128)S(1)}, u32[]{:S(2)}) copy-start(f32[192,128]{1,0:T(8,128)S(1)} %collective-permute-done.1.rx1) | copy-start | bytes 294916
  11.8 0.6 copy-start.2
  14.2 5.6 %collective-permute-start.2 = (f32[240,128]{1,0:T(8,128)}, f32[240,128]{1,0:T(8,128)S(1)}, u32[]{:S(2)}, u32[]{:S(2)}) collective-permute-start(f32[240,128]{1,0:T(8,128)} %get-tuple-element.24), channel_id=1, source_target_pairs={{0,8},{8,16},{16,24},{24,32},{32,40},{40,48},{48,56},{1,9},{9,17},... | collective-permute-start | bytes 368648 | tf_op jit(solution)/shard_map/ppermute | solution.py:350
  17.6 5.8 %collective-permute-start.3 = (f32[240,128]{1,0:T(8,128)}, f32[240,128]{1,0:T(8,128)S(1)}, u32[]{:S(2)}, u32[]{:S(2)}) collective-permute-start(f32[240,128]{1,0:T(8,128)} %get-tuple-element.25), channel_id=1, source_target_pairs={{8,0},{16,8},{24,16},{32,24},{40,32},{48,40},{56,48},{9,1},{17,9},... | collective-permute-start | bytes 368648 | tf_op jit(solution)/shard_map/ppermute | solution.py:351
  19.8 3.7 %copy-start.3 = (f32[240,128]{1,0:T(8,128)}, f32[240,128]{1,0:T(8,128)S(1)}, u32[]{:S(2)}) copy-start(f32[240,128]{1,0:T(8,128)S(1)} %collective-permute-done.2.ry0) | copy-start | bytes 368644
  23.5 0.7 copy-start.4
  26.0 18.9 %collective-permute-start.4 = (f32[320,128]{1,0:T(8,128)}, f32[320,128]{1,0:T(8,128)S(1)}, u32[]{:S(2)}, u32[]{:S(2)}) collective-permute-start(f32[320,128]{1,0:T(8,128)} %get-tuple-element.27), channel_id=1, source_target_pairs={{0,1},{1,2},{2,3},{3,4},{4,5},{5,6},{6,7},{8,9},{9,10},{10,11},{11... | collective-permute-start | bytes 491528 | tf_op jit(solution)/shard_map/ppermute | solution.py:350
  33.1 11.8 %collective-permute-start.5 = (f32[320,128]{1,0:T(8,128)}, f32[320,128]{1,0:T(8,128)S(1)}, u32[]{:S(2)}, u32[]{:S(2)}) collective-permute-start(f32[320,128]{1,0:T(8,128)} %get-tuple-element.28), channel_id=1, source_target_pairs={{1,0},{2,1},{3,2},{4,3},{5,4},{6,5},{7,6},{9,8},{10,9},{11,10},{12... | collective-permute-start | bytes 491528 | tf_op jit(solution)/shard_map/ppermute | solution.py:351
  44.9 0.7 copy-start.6
  44.9 0.7 copy-start.7
  51.8 3.6 %collective-permute-start.6 = (f32[512,128]{1,0:T(8,128)}, f32[512,128]{1,0:T(8,128)S(1)}, u32[]{:S(2)}, u32[]{:S(2)}) collective-permute-start(f32[512,128]{1,0:T(8,128)} %get-tuple-element.36), channel_id=1, source_target_pairs={{0,1},{1,0},{2,3},{3,2},{4,5},{5,4},{6,7},{7,6},{8,9},{9,8},{10,11... | collective-permute-start | bytes 786440 | tf_op jit(solution)/shard_map/ppermute | solution.py:434
  121.5 6.6 %copy-start = (f32[256,2,128]{2,1,0:T(2,128)}, f32[256,2,128]{2,1,0:T(2,128)S(1)}, u32[]{:S(2)}) copy-start(f32[256,2,128]{2,1,0:T(2,128)S(1)} %all_to_all.11) | copy-start | bytes 786436
  121.5 6.6 %collective-permute-start.7 = (f32[512,128]{1,0:T(8,128)S(1)}, f32[512,128]{1,0:T(8,128)S(1)}, u32[]{:S(2)}, u32[]{:S(2)}) collective-permute-start(f32[512,128]{1,0:T(8,128)S(1)} %bitcast.9), channel_id=1, source_target_pairs={{0,1},{1,0},{2,3},{3,2},{4,5},{5,4},{6,7},{7,6},{8,9},{9,8},{10,11... | collective-permute-start | bytes 786440 | tf_op jit(solution)/shard_map/ppermute | solution.py:439
  128.0 0.7 copy-start.5

commit v2 on v1

--- a/solution.py
+++ b/solution.py
@@ -14,20 +14,20 @@
 VOL = 512
 LANES = 128
 PAY = 1024
-AX = ("gx", "gy", "zl", "core")
+AX = ("zh", "x", "gy", "zl", "core")
+AXX = ("zh", "x")
 AXZ = ("zl", "core")
 
 FACE = 64
 
 
 def layout_of(blocks, listed):
-    own = blocks * VOL
     face = listed * FACE
     edge = listed * BS
     corner = -(-listed // 8) * 8
     y_rows = face + 2 * edge
     z_rows = face + 4 * edge + 4 * corner
-    starts = [own]
+    starts = [0]
     for size in (face, face, y_rows, y_rows, z_rows):
         starts.append(starts[-1] + size)
     total = starts[-1] + z_rows
@@ -94,26 +94,39 @@
     return jnp.where(mask, high, value - high)
 
 
-def prep_kernel(send, cot, pre, act, gd, xs, ys, zs):
+def prep_kernel(core, send_h, cot_h, pre_h, act_h, gd, xs0, xs1, ys, zs, send, cot, pre, act, sems, asem, ssem):
     blocks = cot.shape[0]
     listed = send.shape[0]
+    pairs = ((cot_h, cot, 0), (pre_h, pre, 1))
+    copies = [[pltpu.make_async_copy(h.at[b], v.at[b], sems.at[b, i]) for h, v, i in pairs] for b in range(blocks)]
+    act_copy = pltpu.make_async_copy(act_h, act, asem)
+    send_copy = pltpu.make_async_copy(send_h, send, ssem)
+    act_copy.start()
+    for pair in copies:
+        for copy in pair:
+            copy.start()
+    send_copy.start()
+    act_copy.wait()
     for b in range(blocks):
+        for copy in copies[b]:
+            copy.wait()
         p = pre[b]
         s = 1.0 / (1.0 + jnp.exp(-p))
         m = act[b : b + 1, :].astype(F32)
         g = cot[b] * (s * (1.0 + p * (1.0 - s))) * m
         gd[b * VOL : (b + 1) * VOL, :] = jnp.concatenate([g, g], axis=0).T
+    send_copy.wait()
     for i in range(listed):
         r0 = pl.multiple_of(jnp.minimum(send[i], blocks - 1) * VOL, VOL)
         for side in range(2):
             f = 7 * side
-            xs[side, i * 64 : (i + 1) * 64, :] = gd[pl.ds(r0 + f * 64, 64), :]
+            (xs0, xs1)[side][i * 64 : (i + 1) * 64, :] = gd[pl.ds(r0 + f * 64, 64), :]
             for x in range(8):
                 ys[side, i * 64 + x * 8 : i * 64 + x * 8 + 8, :] = gd[pl.ds(r0 + x * 64 + f * 8, 8), :]
             zs[side, i * 64 : (i + 1) * 64, :] = gd[pl.ds(r0 + f, 64, stride=8), :]
 
 
-def pack_y_kernel(ys, rx0, rx1, out0, out1):
+def pack_y_kernel(ys, rx0, rx1, after, out0, out1):
     face = ys.shape[1]
     listed = face // 64
     for side, out in ((0, out0), (1, out1)):
@@ -125,7 +138,7 @@
                 out[row : row + 8, :] = rx[s * 64 + f * 8 : s * 64 + f * 8 + 8, :]
 
 
-def pack_z_kernel(zs, rx0, rx1, ry0, ry1, out0, out1):
+def pack_z_kernel(zs, rx0, rx1, ry0, ry1, after, out0, out1):
     face = zs.shape[1]
     listed = face // 64
     edge = listed * 8
@@ -145,25 +158,12 @@
                     out[row + s : row + s + 1, :] = src[at : at + 1, :]
 
 
-def main_kernel(gd, feat, act, kern, at, p, kg, rt, bias, z):
-    b = pl.program_id(0)
+def interior_block(b, r0, gd, feat, act, at, p, kg_in, kg, rt, bias_in, bias, z):
     lane = lax.broadcasted_iota(jnp.int32, (VOL, LANES), 1) < 64
-
-    @pl.when(b == 0)
-    def _():
-        kg[...] = jnp.zeros(kg.shape, F32)
-        bias[...] = jnp.zeros(bias.shape, F32)
-        for k in range(27):
-            kx, c = k // 9, k % 9
-            w = kern[k]
-            wd = jnp.concatenate([w, w], axis=1)
-            high = wd.astype(BF16)
-            low = (wd - high.astype(F32)).astype(BF16)
-            rt[kx * 128 : kx * 128 + 64, c * 128 : (c + 1) * 128] = high
-            rt[kx * 128 + 64 : kx * 128 + 128, c * 128 : (c + 1) * 128] = low
-
-    g = gd[...]
-    bias[0:1, :] += jnp.sum(g, axis=0, keepdims=True)
+    rows = slice(r0, r0 + VOL)
+    g = gd[b * VOL : (b + 1) * VOL, :]
+    total = jnp.broadcast_to(jnp.sum(g, axis=0, keepdims=True), bias.shape)
+    bias[...] = total if bias_in is None else bias_in[...] + total
     hl = split_hl(g, lane)
     row = lax.broadcasted_iota(jnp.int32, (VOL, LANES), 0)
     vy = (row // 8) % 8
@@ -185,20 +185,65 @@
             c = (ky + 1) * 3 + kz + 1
             z[:, c * 128 : (c + 1) * 128] = sy.astype(BF16)
 
-    f = feat[0] * act[pl.ds(b, 1), :].astype(F32)
+    f = feat * act[b : b + 1, :].astype(F32)
     ff = jnp.concatenate([f, f], axis=0)
     half = lax.broadcasted_iota(jnp.int32, (LANES, VOL), 0) < 64
     a = split_hl(ff, half)
-    at[...] = a.T
+    at[rows, :] = a.T
     zero = jnp.zeros((LANES, 64), F32)
     up = jnp.concatenate([zero, a[:, : VOL - 64]], axis=1)
     down = jnp.concatenate([a[:, 64:], zero], axis=1)
     a3 = jnp.concatenate([up, a, down], axis=0).astype(BF16)
-    kg[...] += jnp.dot(a3, z[...], preferred_element_type=F32)
+    term = jnp.dot(a3, z[...], preferred_element_type=F32)
+    kg[...] = term if kg_in is None else kg_in[...] + term
     p3 = lax.dot_general(z[...], rt[...], (((1,), (1,)), ((), ())), preferred_element_type=F32)
-    p[...] = p3[:, 128:256]
-    p[64:VOL, :] += p3[: VOL - 64, 256:384]
-    p[0 : VOL - 64, :] += p3[64:, 0:128]
+    p[rows, :] = p3[:, 128:256]
+    p[r0 + 64 : r0 + VOL, :] += p3[: VOL - 64, 256:384]
+    p[r0 : r0 + VOL - 64, :] += p3[64:, 0:128]
+
+
+def fetch(part, feat_h, feat, sems):
+    return [pltpu.make_async_copy(feat_h.at[b], feat.at[i], sems.at[i]) for i, b in enumerate(part)]
+
+
+def first_kernel(part, gd, feat_h, act, kern_h, at, p, kg, rt, bias, z, feat, sems, kern, ksem):
+    kern_copy = pltpu.make_async_copy(kern_h, kern, ksem)
+    kern_copy.start()
+    copies = fetch(part, feat_h, feat, sems)
+    for copy in copies:
+        copy.start()
+    kern_copy.wait()
+    for k in range(27):
+        kx, c = k // 9, k % 9
+        w = kern[k]
+        wd = jnp.concatenate([w, w], axis=1)
+        high = wd.astype(BF16)
+        low = (wd - high.astype(F32)).astype(BF16)
+        rt[kx * 128 : kx * 128 + 64, c * 128 : (c + 1) * 128] = high
+        rt[kx * 128 + 64 : kx * 128 + 128, c * 128 : (c + 1) * 128] = low
+    for i, b in enumerate(part):
+        copies[i].wait()
+        kgi, bi = (None, None) if i == 0 else (kg, bias)
+        interior_block(b, i * VOL, gd, feat[i], act, at, p, kgi, kg, rt, bi, bias, z)
+
+
+def next_kernel(part, held, *refs):
+    gd, feat_h, act, rt, kg0, bias0 = refs[:6]
+    earlier = refs[6 : 6 + 2 * held]
+    at, p, kg, bias, z, feat, sems = refs[7 + 2 * held :]
+    copies = fetch(part, feat_h, feat, sems)
+    for copy in copies:
+        copy.start()
+    row = 0
+    for i in range(held):
+        n = earlier[2 * i].shape[0]
+        at[row : row + n, :] = earlier[2 * i][...]
+        p[row : row + n, :] = earlier[2 * i + 1][...]
+        row += n
+    for i, b in enumerate(part):
+        copies[i].wait()
+        kgi, bi = (kg0, bias0) if i == 0 else (kg, bias)
+        interior_block(b, row + i * VOL, gd, feat[i], act, at, p, kgi, kg, rt, bi, bias, z)
 
 
 def nt(a, b):
@@ -219,15 +264,15 @@
     return out
 
 
-def halo_kernel(scale, od, os_, tb, core, gd, rx0, rx1, ry0, ry1, rz0, rz1, at, rt, kgm, bias, p, act,
-                mine, other, ig, src, pb, pw, kg, pa, pay):
+def halo_kernel(scale, od, os_, tb, core, gd, rx0, rx1, ry0, ry1, rz0, rz1, at, rt, bias, p0, kg0,
+                mine, other, pa, src, pb, pw, pay, kg):
     blocks = od.shape[0]
     row = 0
-    for ref in (gd, rx0, rx1, ry0, ry1, rz0, rz1):
+    for ref in (rx0, rx1, ry0, ry1, rz0, rz1):
         src[row : row + ref.shape[0], :] = ref[...]
         row += ref.shape[0]
-    kg[...] = kgm[...]
-    pa[...] = p[...]
+    pa[...] = p0[...]
+    kg[...] = kg0[...]
     lane64 = lax.broadcasted_iota(jnp.int32, (64, LANES), 1) < 64
 
     def plane(b, axis, sign):
@@ -242,12 +287,17 @@
                 base = (code & 4095) + (os_[b, o] << ((code >> 12) & 15))
                 sr = (code >> 16) & 15
                 sq = (code >> 20) & 15
-                for i in range(8 if r == 0 else 1):
-                    for j in range(8 if q == 0 else 1):
-                        at_r = i + 1 if r == 0 else (0 if r == -1 else 9)
-                        at_q = 8 + j if q == 0 else (7 if q == -1 else 16)
-                        row = base + (i << sr) + (j << sq)
-                        pb[at_r, at_q : at_q + 1, :] = src[pl.ds(row, 1), :]
+
+                def fill(ref):
+                    for i in range(8 if r == 0 else 1):
+                        for j in range(8 if q == 0 else 1):
+                            at_r = i + 1 if r == 0 else (0 if r == -1 else 9)
+                            at_q = 8 + j if q == 0 else (7 if q == -1 else 16)
+                            row = base + (i << sr) + (j << sq)
+                            pb[at_r, at_q : at_q + 1, :] = ref[pl.ds(row, 1), :]
+
+                pl.when(d == 13)(lambda: fill(gd))
+                pl.when(d != 13)(lambda: fill(src))
 
         for kr in (-1, 0, 1):
             for kq in (-1, 0, 1):
@@ -317,7 +367,10 @@
     me = core[0]
     mine[...] = pay[pl.ds(pl.multiple_of(me * (PAY // 2), PAY // 2), PAY // 2), :]
     other[...] = pay[pl.ds(pl.multiple_of((1 - me) * (PAY // 2), PAY // 2), PAY // 2), :]
-    for b in range(blocks):
+
+
+def finish_kernel(pa, act, ig):
+    for b in range(act.shape[0]):
         og = pa[b * VOL : (b + 1) * VOL, :]
         og = (og + pltpu.roll(og, 64, 1)).T
         ig[b] = og[:64, :] * act[b : b + 1, :].astype(F32)
@@ -339,6 +392,8 @@
 
 VM = pl.BlockSpec(memory_space=pltpu.VMEM)
 SM = pl.BlockSpec(memory_space=pltpu.SMEM)
+ANY = pl.BlockSpec(memory_space=pl.ANY)
+ROOM = pltpu.CompilerParams(vmem_limit_bytes=32 * 2**20)
 
 
 def sds(shape, dtype=F32):
@@ -352,90 +407,121 @@
     return up, down
 
 
+def vm(shape, dtype=F32):
+    return pltpu.VMEM(shape, dtype)
+
+
+def local(x):
+    return pltpu.with_memory_space_constraint(x, pltpu.VMEM)
+
+
+def far(x):
+    return pltpu.with_memory_space_constraint(x, pltpu.HBM)
+
+
 def shards(features, preact, cotangent, kernel, active, owner_dir, owner_slot, send_list):
     blocks, channels, volume = features.shape
     listed = send_list.shape[0]
     lay = layout_of(blocks, listed)
     face, yr, zr = lay["face"], lay["y_rows"], lay["z_rows"]
+    rows = blocks * VOL
     devices = lax.axis_size(AX)
-    me = lax.axis_index("core").astype(jnp.int32)
-    core = me.reshape(1)
+    core = lax.axis_index("core").astype(jnp.int32).reshape(1)
     scale = float((volume * blocks * devices) ** -0.5)
 
-    gd, xs, ys, zs = pl.pallas_call(
+    gd, xs0, xs1, ys, zs = pl.pallas_call(
         prep_kernel,
-        out_shape=(sds((blocks * VOL, LANES)),) + (sds((2, face, LANES)),) * 3,
-        in_specs=[SM, VM, VM, VM],
-        out_specs=(VM,) * 4,
-        name="prep",
-    )(send_list, cotangent, preact, active)
-
-    rx0, rx1 = both_ways(xs[0], xs[1], "gx")
-
-    full = lambda shape: pl.BlockSpec(shape, lambda b: (0,) * len(shape))
-    at, p, kgm, rt, bias = pl.pallas_call(
-        main_kernel,
-        grid=(blocks,),
-        in_specs=[
-            pl.BlockSpec((VOL, LANES), lambda b: (b, 0)),
-            pl.BlockSpec((1, channels, VOL), lambda b: (b, 0, 0)),
-            full((blocks, VOL)),
-            full((27, channels, channels)),
+        out_shape=(vm((rows, LANES)), vm((face, LANES)), vm((face, LANES)), vm((2, face, LANES)), vm((2, face, LANES))),
+        in_specs=[SM] + [ANY] * 4,
+        out_specs=(VM,) * 5,
+        scratch_shapes=[
+            pltpu.SMEM((listed,), jnp.int32),
+            pltpu.VMEM((blocks, channels, VOL), F32),
+            pltpu.VMEM((blocks, channels, VOL), F32),
+            pltpu.VMEM((blocks, VOL), jnp.int32),
+            pltpu.SemaphoreType.DMA((blocks, 2)),
+            pltpu.SemaphoreType.DMA,
+            pltpu.SemaphoreType.DMA,
         ],
-        out_specs=(
-            pl.BlockSpec((VOL, LANES), lambda b: (b, 0)),
-            pl.BlockSpec((VOL, LANES), lambda b: (b, 0)),
-            full((384, 1152)),
-            full((384, 1152)),
-            full((8, LANES)),
-        ),
-        out_shape=(
-            sds((blocks * VOL, LANES)),
-            sds((blocks * VOL, LANES)),
-            sds((384, 1152)),
-            sds((384, 1152), BF16),
-            sds((8, LANES)),
-        ),
-        scratch_shapes=[pltpu.VMEM((VOL, 1152), BF16)],
-        name="interior",
-    )(gd, features, active, kernel)
+        name="prep", compiler_params=ROOM,
+    )(core, far(send_list), far(cotangent), far(preact), far(active))
+    rx0, rx1 = both_ways(xs0, xs1, AXX)
+
+    third = max(blocks // 4, 1)
+    parts = (range(third), range(third, 2 * third), range(2 * third, blocks))
+
+    def scratch(part):
+        return [
+            pltpu.VMEM((VOL, 1152), BF16),
+            pltpu.VMEM((max(len(part), 1), channels, VOL), F32),
+            pltpu.SemaphoreType.DMA((max(len(part), 1),)),
+        ]
+
+    wide = (384, 1152)
+    n0 = len(parts[0]) * VOL
+    at0, p0, kg, rt, bias = pl.pallas_call(
+        functools.partial(first_kernel, parts[0]),
+        in_specs=[VM, ANY, VM, ANY],
+        out_specs=(VM,) * 5,
+        out_shape=(vm((n0, LANES)), vm((n0, LANES)), vm(wide), vm(wide, BF16), vm((8, LANES))),
+        scratch_shapes=scratch(parts[0]) + [pltpu.VMEM((27, channels, channels), F32), pltpu.SemaphoreType.DMA],
+        name="interior0", compiler_params=ROOM,
+    )(local(gd), far(features), active, far(kernel))
+
+    def more(part, earlier, kg, bias, after, name):
+        n = len(part) * VOL + sum(e.shape[0] for e in earlier[::2])
+        return pl.pallas_call(
+            functools.partial(next_kernel, part, len(earlier) // 2),
+            in_specs=[VM, ANY] + [VM] * (4 + len(earlier)) + [ANY],
+            out_specs=(VM,) * 4,
+            out_shape=(vm((n, LANES)), vm((n, LANES)), vm(wide), vm((8, LANES))),
+            scratch_shapes=scratch(part),
+            name=name, compiler_params=ROOM,
+        )(local(gd), far(features), active, local(rt), local(kg), local(bias), *[local(e) for e in earlier], after)
 
     ys0, ys1 = pl.pallas_call(
-        pack_y_kernel, out_shape=(sds((yr, LANES)),) * 2, in_specs=[VM] * 3, out_specs=(VM,) * 2,
-        name="pack_y",
-    )(ys, rx0, rx1)
+        pack_y_kernel, out_shape=(vm((yr, LANES)),) * 2, in_specs=[VM] * 3 + [ANY], out_specs=(VM,) * 2,
+        name="pack_y", compiler_params=ROOM,
+    )(local(ys), local(rx0), local(rx1), bias)
     ry0, ry1 = both_ways(ys0, ys1, "gy")
+    at1, p1, kg, bias = more(parts[1], (), kg, bias, ys0, "interior1")
     zs0, zs1 = pl.pallas_call(
-        pack_z_kernel, out_shape=(sds((zr, LANES)),) * 2, in_specs=[VM] * 5, out_specs=(VM,) * 2,
-        name="pack_z",
-    )(zs, rx0, rx1, ry0, ry1)
+        pack_z_kernel, out_shape=(vm((zr, LANES)),) * 2, in_specs=[VM] * 5 + [ANY], out_specs=(VM,) * 2,
+        name="pack_z", compiler_params=ROOM,
+    )(local(zs), local(rx0), local(rx1), local(ry0), local(ry1), bias)
     rz0, rz1 = both_ways(zs0, zs1, AXZ)
+    at, p, kg, bias = more(parts[2], (at0, p0, at1, p1), kg, bias, zs0, "interior2")
 
     table = jnp.asarray(piece_table(blocks, listed))
-    mine, other, input_grad = pl.pallas_call(
+    mine, other, p = pl.pallas_call(
         functools.partial(halo_kernel, scale),
-        out_shape=(sds((PAY // 2, LANES)), sds((PAY // 2, LANES)), sds((blocks, channels, VOL))),
-        in_specs=[SM] * 4 + [VM] * 13,
+        out_shape=(vm((PAY // 2, LANES)), vm((PAY // 2, LANES)), vm((rows, LANES))),
+        in_specs=[SM] * 4 + [VM] * 12,
         out_specs=(VM,) * 3,
         scratch_shapes=[
             pltpu.VMEM((lay["total"], LANES), F32),
             pltpu.VMEM((10, 24, LANES), F32),
             pltpu.VMEM((64, 1152), BF16),
+            pltpu.VMEM((PAY, LANES), F32),
             pltpu.VMEM((384, 1152), F32),
-            pltpu.VMEM((blocks * VOL, LANES), F32),
-            pltpu.VMEM((PAY, LANES), F32),
         ],
-        name="halo",
-    )(owner_dir, owner_slot, table, core, gd, rx0, rx1, ry0, ry1, rz0, rz1, at, rt, kgm, bias, p, active)
+        name="halo", compiler_params=ROOM,
+    )(owner_dir, owner_slot, table, core, local(gd), local(rx0), local(rx1), local(ry0), local(ry1),
+      local(rz0), local(rz1), local(at), local(rt), local(bias), local(p), local(kg))
 
     swap = [(0, 1), (1, 0)]
-    peers_ax = ("gx", "gy", "zl")
-    peers = lax.axis_size(peers_ax)
-    half = mine + lax.ppermute(other, "core", swap)
-    spread = lax.all_to_all(half.reshape(peers, PAY // 2 // peers, LANES), peers_ax, 0, 0, tiled=True)
+    arrived = lax.ppermute(other, "core", swap)
+    input_grad = pl.pallas_call(
+        finish_kernel, out_shape=sds((blocks, channels, VOL)), in_specs=[VM] * 2, out_specs=VM, name="finish", compiler_params=ROOM,
+    )(local(p), active)
+    half = mine + arrived
+    plane, depth = lax.axis_size(("x", "gy")), lax.axis_size(("zh", "zl"))
+    spread = lax.all_to_all(half.reshape(plane, PAY // 2 // plane, LANES), ("x", "gy"), 0, 0, tiled=True)
     share = jnp.sum(spread, axis=0)
-    copies = jnp.broadcast_to(share[None], spread.shape)
-    whole = lax.all_to_all(copies, peers_ax, 0, 0, tiled=True).reshape(PAY // 2, LANES)
+    share = lax.all_to_all(jnp.broadcast_to(share[None], (depth,) + share.shape), ("zh", "zl"), 0, 0, tiled=True)
+    share = jnp.sum(share, axis=0)
+    whole = lax.all_to_all(jnp.broadcast_to(share[None], spread.shape), ("x", "gy"), 0, 0, tiled=True)
+    whole = whole.reshape(PAY // 2, LANES)
     rest = lax.ppermute(whole, "core", swap)
 
     kernel_grad, bias_grad = pl.pallas_call(
@@ -444,14 +530,14 @@
         in_specs=[SM, VM, VM],
         out_specs=(VM,) * 2,
         scratch_shapes=[pltpu.VMEM((PAY, LANES), F32)],
-        name="unpack",
-    )(core, whole, rest)
+        name="unpack", compiler_params=ROOM,
+    )(core, local(whole), local(rest))
     return input_grad, kernel_grad, bias_grad.reshape(channels)
 
 
 def solution(mesh):
     shape = mesh.devices.shape
-    fine = Mesh(mesh.devices.reshape(shape[0], shape[1], shape[2] // 2, 2), AX)
+    fine = Mesh(mesh.devices.reshape(2, shape[0] // 2, shape[1], shape[2] // 2, 2), AX)
     placed = (
         P(AX, None, None),
         P(AX, None, None),

time: 132 us -> 110 us (0.83); the launches traced: 131 us -> 110 us
  Pallas kernels: 23.9 us -> 15.9 us
  waiting for transfers between devices: 9 us -> 1.59 us
  local copies, waits for them, and re-layouts: 3.74 us -> 0.74 us
  blocking collectives: 64.7 us -> 62.7 us
    pallas_call x5 -> x8, Pallas kernels: 21.7 us -> 14.8 us  [the longest x2 6.41 us: more(): pl.pallas_call(functools.partial(next_kernel, part, len(earlier) // 2), i...]
    ppermute x3, waiting for transfers between devices: 3.73 us -> 0.44 us  [both_ways(): down = lax.ppermute(low, axis, [(i + 1, i) for i in range(n - 1)])]
    ppermute x3, waiting for transfers between devices: 2.42 us -> 0.01 us  [both_ways(): up = lax.ppermute(high, axis, [(i, i + 1) for i in range(n - 1)])]
    all_to_all x2 -> x3, blocking collectives: 64.7 us -> 62.7 us  [the longest x1 37 us: shards(): lax.all_to_all(half.reshape(plane, PAY // 2 // plane, LANES), ('x', 'gy')...]
    unnamed x16 -> x10, local copies, waits for them, and re-layouts: 2.71 us -> 0.72 us
  transfers between devices with their start and end apart: 8 -> 8, of which waited for: 6 -> 2; matrix products, arithmetic and copies ran while one was open for 0% -> 0% of each run, Pallas kernels for 7% -> 10%
where the time goes in v2:
time: 110 us
  blocking collectives  62.7 us (57%)
  starting transfers between devices  28.5 us (26%)
  Pallas kernels  15.9 us (14%)
  waiting for transfers between devices  1.59 us (1%)
    all_to_all x1, blocking collectives, shards(): lax.all_to_all(half.reshape(plane, PAY // 2 // plane, LANES), ('x', 'gy')...  37 us
    all_to_all x1, blocking collectives, shards(): lax.all_to_all(jnp.broadcast_to(share[None], spread.shape), ('x', 'gy'),...  16.1 us
    ppermute x3, starting transfers between devices, both_ways(): up = lax.ppermute(high, axis, [(i, i + 1) for i in range(n - 1)])  14.5 us
    all_to_all x1, blocking collectives, shards(): lax.all_to_all(jnp.broadcast_to(share[None], (depth,) + share.shape), ('z...  9.6 us
    pallas_call x2, Pallas kernels, more(): pl.pallas_call(functools.partial(next_kernel, part, len(earlier) // 2), i...  6.41 us
    ppermute x1, starting transfers between devices, shards(): rest = lax.ppermute(whole, 'core', swap)  5.81 us
    ppermute x3, starting transfers between devices, both_ways(): down = lax.ppermute(low, axis, [(i + 1, i) for i in range(n - 1)])  5.15 us
    ppermute x1, starting transfers between devices, shards(): arrived = lax.ppermute(other, 'core', swap)  3.02 us
  transfers between devices with their start and end apart: 8, of which 2 were waited for; matrix products, arithmetic and copies ran while one was open for 0% of the time, Pallas kernels for 10%

profile of v2, /device:TPU:1, one launch (start us, length us, event | category | flops | bytes accessed | tf_op | source)
XLA Modules:
  0.0 110.3 jit_solution(2124889766990397373)
XLA Ops:
  0.6 0.0 copy-start.1
  0.6 1.9 %prep.1 = (f32[2048,128]{1,0:T(8,128)S(1)}, f32[192,128]{1,0:T(8,128)S(1)}, f32[192,128]{1,0:T(8,128)S(1)}, f32[2,192,128]{2,1,0:T(8,128)S(1)}, f32[2,192,128]{2,1,0:T(8,128)S(1)}) custom-call(s32[1]{0:T(128)} %bitcast.core, s32[3]{0:T(128)} %send_h.1, f32[4,64,512]{2,1,0:T(8,128)} %cot_h.1, f32[4,64,512]{2,1,0:T(8,128)} %pre_h.1, s32[4,512]{1,0:T(4,128)} %act.3), custom_call_target="tpu_custom_call" | custom-call | tf_op jit(solution)/shard_map/prep/pallas_call | solution.py:432
  2.5 3.9 %collective-permute-start = (f32[192,128]{1,0:T(8,128)S(1)}, f32[192,128]{1,0:T(8,128)S(1)}, u32[]{:S(2)}, u32[]{:S(2)}) collective-permute-start(f32[192,128]{1,0:T(8,128)S(1)} %get-tuple-element.31), channel_id=1, source_target_pairs={{0,64},{64,128},{128,192},{192,256},{256,320},{320,384},{384,448},... | collective-permute-start | bytes 294920 | tf_op jit(solution)/shard_map/ppermute | solution.py:405
  6.5 1.3 %collective-permute-start.1 = (f32[192,128]{1,0:T(8,128)S(1)}, f32[192,128]{1,0:T(8,128)S(1)}, u32[]{:S(2)}, u32[]{:S(2)}) collective-permute-start(f32[192,128]{1,0:T(8,128)S(1)} %get-tuple-element.32), channel_id=1, source_target_pairs={{64,0},{128,64},{192,128},{256,192},{320,256},{384,320},{448,384},... | collective-permute-start | bytes 294920 | tf_op jit(solution)/shard_map/ppermute | solution.py:406
  7.8 0.7 copy-done
  8.5 3.0 %interior0.1 = (f32[512,128]{1,0:T(8,128)S(1)}, f32[512,128]{1,0:T(8,128)S(1)}, f32[384,1152]{1,0:T(8,128)S(1)}, bf16[384,1152]{1,0:T(8,128)(2,1)S(1)}, f32[8,128]{1,0:T(8,128)S(1)}) custom-call(f32[2048,128]{1,0:T(8,128)S(1)} %get-tuple-element.30.gd.refs_0_, f32[4,64,512]{2,1,0:T(8,128)} %refs_1_.3, s32[4,512]{1,0:T(4,128)S(1)} %copy-done, ...), custom_call_target="tpu_custom_call" | custom-call | tf_op jit(solution)/shard_map/interior0/pallas_call | solution.py:462
  11.5 0.4 collective-permute-done.1.rx1
  11.9 1.3 %collective-permute-start.3 = (f32[240,128]{1,0:T(8,128)S(1)}, f32[240,128]{1,0:T(8,128)S(1)}, u32[]{:S(2)}, u32[]{:S(2)}) collective-permute-start(f32[240,128]{1,0:T(8,128)S(1)} %get-tuple-element.36.refs_6_), channel_id=1, source_target_pairs={{8,0},{16,8},{24,16},{32,24},{40,32},{48,40},{56,48},{9,1},{17,9},... | collective-permute-start | bytes 368648 | tf_op jit(solution)/shard_map/ppermute | solution.py:406
  13.2 4.0 %collective-permute-start.2 = (f32[240,128]{1,0:T(8,128)S(1)}, f32[240,128]{1,0:T(8,128)S(1)}, u32[]{:S(2)}, u32[]{:S(2)}) collective-permute-start(f32[240,128]{1,0:T(8,128)S(1)} %get-tuple-element.35), channel_id=1, source_target_pairs={{0,8},{8,16},{16,24},{24,32},{32,40},{40,48},{48,56},{1,9},{9,17},... | collective-permute-start | bytes 368648 | tf_op jit(solution)/shard_map/ppermute | solution.py:405
  17.2 2.4 %interior1.1 = (f32[512,128]{1,0:T(8,128)S(1)}, f32[512,128]{1,0:T(8,128)S(1)}, f32[384,1152]{1,0:T(8,128)S(1)}, f32[8,128]{1,0:T(8,128)S(1)}) custom-call(f32[2048,128]{1,0:T(8,128)S(1)} %get-tuple-element.30.gd.refs_0_, f32[4,64,512]{2,1,0:T(8,128)} %refs_1_.3, s32[4,512]{1,0:T(4,128)S(1)} %copy-done.1, ...), custom_call_target="tpu_custom_call" | custom-call | tf_op jit(solution)/shard_map/interior1/pallas_call | solution.py:473
  19.7 6.5 %collective-permute-start.4 = (f32[320,128]{1,0:T(8,128)S(1)}, f32[320,128]{1,0:T(8,128)S(1)}, u32[]{:S(2)}, u32[]{:S(2)}) collective-permute-start(f32[320,128]{1,0:T(8,128)S(1)} %get-tuple-element.41), channel_id=1, source_target_pairs={{0,1},{1,2},{2,3},{3,4},{4,5},{5,6},{6,7},{8,9},{9,10},{10,11},{11... | collective-permute-start | bytes 491528 | tf_op jit(solution)/shard_map/ppermute | solution.py:405
  26.3 2.6 %collective-permute-start.5 = (f32[320,128]{1,0:T(8,128)S(1)}, f32[320,128]{1,0:T(8,128)S(1)}, u32[]{:S(2)}, u32[]{:S(2)}) collective-permute-start(f32[320,128]{1,0:T(8,128)S(1)} %get-tuple-element.42.refs_10_), channel_id=1, source_target_pairs={{1,0},{2,1},{3,2},{4,3},{5,4},{6,5},{7,6},{9,8},{10,9},{11,10},{12... | collective-permute-start | bytes 491528 | tf_op jit(solution)/shard_map/ppermute | solution.py:406
  28.8 0.0 copy-start.2
  28.9 4.0 %interior2.1 = (f32[2048,128]{1,0:T(8,128)S(1)}, f32[2048,128]{1,0:T(8,128)S(1)}, f32[384,1152]{1,0:T(8,128)S(1)}, f32[8,128]{1,0:T(8,128)S(1)}) custom-call(f32[2048,128]{1,0:T(8,128)S(1)} %get-tuple-element.30.gd.refs_0_, f32[4,64,512]{2,1,0:T(8,128)} %refs_1_.3, s32[4,512]{1,0:T(4,128)S(1)} %copy-done.1, ...), custom_call_target="tpu_custom_call" | custom-call | tf_op jit(solution)/shard_map/interior2/pallas_call | solution.py:473
  32.9 0.0 collective-permute-done.5.rz1
  32.9 2.1 %halo.1 = (f32[512,128]{1,0:T(8,128)S(1)}, f32[512,128]{1,0:T(8,128)S(1)}, f32[2048,128]{1,0:T(8,128)S(1)}) custom-call(s32[4,27]{1,0:T(4,128)S(1)} %copy-done.3, s32[4,27]{1,0:T(4,128)S(1)} %copy-done.4, s32[756]{0:T(1024)S(1)} %copy-done.2, s32[1]{0:T(128)} %bitcast.core, f32[2048,128]{1,0:T(8,128)S(1)} %get-tuple-element.30.gd.refs_0_, ...), custom_call_target="tpu_custom_call" | custom-call | tf_op jit(solution)/shard_map/halo/pallas_call | solution.py:496
  35.0 3.0 %collective-permute-start.6 = (f32[512,128]{1,0:T(8,128)S(1)}, f32[512,128]{1,0:T(8,128)S(1)}, u32[]{:S(2)}, u32[]{:S(2)}) collective-permute-start(f32[512,128]{1,0:T(8,128)S(1)} %get-tuple-element.54), channel_id=1, source_target_pairs={{0,1},{1,0},{2,3},{3,2},{4,5},{5,4},{6,7},{7,6},{8,9},{9,8},{10,11... | collective-permute-start | bytes 786440 | tf_op jit(solution)/shard_map/ppermute | solution.py:513
  38.0 1.1 %collective-permute-done.6 = f32[512,128]{1,0:T(8,128)S(1)} collective-permute-done((f32[512,128]{1,0:T(8,128)S(1)}, f32[512,128]{1,0:T(8,128)S(1)}, u32[]{:S(2)}, u32[]{:S(2)}) %collective-permute-start.6) | collective-permute-done | bytes 262176 | tf_op jit(solution)/shard_map/ppermute | solution.py:513
  39.2 37.0 %all_to_all.15 = f32[32,16,128]{2,1,0:T(8,128)S(1)} all-to-all(f32[32,16,128]{2,1,0:T(8,128)S(1)} %bitcast.6), channel_id=1, replica_groups=mesh['zh'=2,'x'=4,'gy'=8,'zl'=4,'core'=2] {'x','gy'}, dimensions={0} | all-to-all | bytes 524288 | tf_op jit(solution)/shard_map/all_to_all | solution.py:519
  76.2 9.6 %all_to_all.16 = f32[8,16,128]{2,1,0:T(8,128)S(1)} all-to-all(f32[8,16,128]{2,1,0:T(8,128)S(1)} %broadcast_in_dim.4), channel_id=1, replica_groups=mesh['zh'=2,'x'=4,'gy'=8,'zl'=4,'core'=2] {'zh','zl'}, dimensions={0} | all-to-all | bytes 131072 | tf_op jit(solution)/shard_map/all_to_all | solution.py:521
  85.9 16.1 %all_to_all.17 = f32[32,16,128]{2,1,0:T(8,128)S(1)} all-to-all(f32[32,16,128]{2,1,0:T(8,128)S(1)} %broadcast_in_dim.5), channel_id=1, replica_groups=mesh['zh'=2,'x'=4,'gy'=8,'zl'=4,'core'=2] {'x','gy'}, dimensions={0} | all-to-all | bytes 524288 | tf_op jit(solution)/shard_map/all_to_all | solution.py:523
  102.0 5.8 %collective-permute-start.7 = (f32[512,128]{1,0:T(8,128)S(1)}, f32[512,128]{1,0:T(8,128)S(1)}, u32[]{:S(2)}, u32[]{:S(2)}) collective-permute-start(f32[512,128]{1,0:T(8,128)S(1)} %bitcast.4), channel_id=1, source_target_pairs={{0,1},{1,0},{2,3},{3,2},{4,5},{5,4},{6,7},{7,6},{8,9},{9,8},{10,11... | collective-permute-start | bytes 786440 | tf_op jit(solution)/shard_map/ppermute | solution.py:525
  107.8 1.4 %finish.1 = f32[4,64,512]{2,1,0:T(8,128)} custom-call(f32[2048,128]{1,0:T(8,128)S(1)} %get-tuple-element.52.pa, s32[4,512]{1,0:T(4,128)S(1)} %copy-done.1), custom_call_target="tpu_custom_call" | custom-call | tf_op jit(solution)/shard_map/finish/pallas_call | solution.py:514
  109.2 1.1 %unpack.1 = (f32[27,64,64]{2,1,0:T(8,128)}, f32[1,64]{1,0:T(1,128)}) custom-call(s32[1]{0:T(128)} %bitcast.core, f32[512,128]{1,0:T(8,128)S(1)} %bitcast.5, f32[512,128]{1,0:T(8,128)S(1)} %collective-permute-done.7.other), custom_call_target="tpu_custom_call" | custom-call | tf_op jit(solution)/shard_map/unpack/pallas_call | solution.py:527
  (19 shorter events, 0.2 us)
Async XLA Ops:
  0.6 16.5 %copy-start.1 = (s32[4,512]{1,0:T(4,128)S(1)}, s32[4,512]{1,0:T(4,128)}, u32[]{:S(2)}) copy-start(s32[4,512]{1,0:T(4,128)} %act.3) | copy-start | bytes 24580
  2.5 8.9 %collective-permute-start = (f32[192,128]{1,0:T(8,128)S(1)}, f32[192,128]{1,0:T(8,128)S(1)}, u32[]{:S(2)}, u32[]{:S(2)}) collective-permute-start(f32[192,128]{1,0:T(8,128)S(1)} %get-tuple-element.31), channel_id=1, source_target_pairs={{0,64},{64,128},{128,192},{192,256},{256,320},{320,384},{384,448},... | collective-permute-start | bytes 294920 | tf_op jit(solution)/shard_map/ppermute | solution.py:405
  6.5 5.4 %collective-permute-start.1 = (f32[192,128]{1,0:T(8,128)S(1)}, f32[192,128]{1,0:T(8,128)S(1)}, u32[]{:S(2)}, u32[]{:S(2)}) collective-permute-start(f32[192,128]{1,0:T(8,128)S(1)} %get-tuple-element.32), channel_id=1, source_target_pairs={{64,0},{128,64},{192,128},{256,192},{320,256},{384,320},{448,384},... | collective-permute-start | bytes 294920 | tf_op jit(solution)/shard_map/ppermute | solution.py:406
  7.8 0.7 copy-start
  11.9 7.8 %collective-permute-start.3 = (f32[240,128]{1,0:T(8,128)S(1)}, f32[240,128]{1,0:T(8,128)S(1)}, u32[]{:S(2)}, u32[]{:S(2)}) collective-permute-start(f32[240,128]{1,0:T(8,128)S(1)} %get-tuple-element.36.refs_6_), channel_id=1, source_target_pairs={{8,0},{16,8},{24,16},{32,24},{40,32},{48,40},{56,48},{9,1},{17,9},... | collective-permute-start | bytes 368648 | tf_op jit(solution)/shard_map/ppermute | solution.py:406
  13.2 6.5 %collective-permute-start.2 = (f32[240,128]{1,0:T(8,128)S(1)}, f32[240,128]{1,0:T(8,128)S(1)}, u32[]{:S(2)}, u32[]{:S(2)}) collective-permute-start(f32[240,128]{1,0:T(8,128)S(1)} %get-tuple-element.35), channel_id=1, source_target_pairs={{0,8},{8,16},{16,24},{24,32},{32,40},{40,48},{48,56},{1,9},{9,17},... | collective-permute-start | bytes 368648 | tf_op jit(solution)/shard_map/ppermute | solution.py:405
  19.7 13.1 %collective-permute-start.4 = (f32[320,128]{1,0:T(8,128)S(1)}, f32[320,128]{1,0:T(8,128)S(1)}, u32[]{:S(2)}, u32[]{:S(2)}) collective-permute-start(f32[320,128]{1,0:T(8,128)S(1)} %get-tuple-element.41), channel_id=1, source_target_pairs={{0,1},{1,2},{2,3},{3,4},{4,5},{5,6},{6,7},{8,9},{9,10},{10,11},{11... | collective-permute-start | bytes 491528 | tf_op jit(solution)/shard_map/ppermute | solution.py:405
  26.3 6.6 %collective-permute-start.5 = (f32[320,128]{1,0:T(8,128)S(1)}, f32[320,128]{1,0:T(8,128)S(1)}, u32[]{:S(2)}, u32[]{:S(2)}) collective-permute-start(f32[320,128]{1,0:T(8,128)S(1)} %get-tuple-element.42.refs_10_), channel_id=1, source_target_pairs={{1,0},{2,1},{3,2},{4,3},{5,4},{6,5},{7,6},{9,8},{10,9},{11,10},{12... | collective-permute-start | bytes 491528 | tf_op jit(solution)/shard_map/ppermute | solution.py:406
  28.8 4.1 %copy-start.2 = (s32[756]{0:T(1024)S(1)}, s32[756]{0:T(1024)}, u32[]{:S(2)}) copy-start(s32[756]{0:T(1024)} %constant.8.clone.tb) | copy-start | bytes 9076
  28.8 4.1 %copy-start.3 = (s32[4,27]{1,0:T(4,128)S(1)}, s32[4,27]{1,0:T(4,128)}, u32[]{:S(2)}) copy-start(s32[4,27]{1,0:T(4,128)} %od.1) | copy-start | bytes 1300
  28.9 4.1 %copy-start.4 = (s32[4,27]{1,0:T(4,128)S(1)}, s32[4,27]{1,0:T(4,128)}, u32[]{:S(2)}) copy-start(s32[4,27]{1,0:T(4,128)} %os_.1) | copy-start | bytes 1300
  35.0 4.2 %collective-permute-start.6 = (f32[512,128]{1,0:T(8,128)S(1)}, f32[512,128]{1,0:T(8,128)S(1)}, u32[]{:S(2)}, u32[]{:S(2)}) collective-permute-start(f32[512,128]{1,0:T(8,128)S(1)} %get-tuple-element.54), channel_id=1, source_target_pairs={{0,1},{1,0},{2,3},{3,2},{4,5},{5,4},{6,7},{7,6},{8,9},{9,8},{10,11... | collective-permute-start | bytes 786440 | tf_op jit(solution)/shard_map/ppermute | solution.py:513
  102.0 7.2 %collective-permute-start.7 = (f32[512,128]{1,0:T(8,128)S(1)}, f32[512,128]{1,0:T(8,128)S(1)}, u32[]{:S(2)}, u32[]{:S(2)}) collective-permute-start(f32[512,128]{1,0:T(8,128)S(1)} %bitcast.4), channel_id=1, source_target_pairs={{0,1},{1,0},{2,3},{3,2},{4,5},{5,4},{6,7},{7,6},{8,9},{9,8},{10,11... | collective-permute-start | bytes 786440 | tf_op jit(solution)/shard_map/ppermute | solution.py:525

commit v3 on v2

--- a/solution.py
+++ b/solution.py
@@ -13,7 +13,7 @@
 BS = 8
 VOL = 512
 LANES = 128
-PAY = 1024
+PAY = 896
 AX = ("zh", "x", "gy", "zl", "core")
 AXX = ("zh", "x")
 AXZ = ("zl", "core")
@@ -94,7 +94,22 @@
     return jnp.where(mask, high, value - high)
 
 
-def prep_kernel(core, send_h, cot_h, pre_h, act_h, gd, xs0, xs1, ys, zs, send, cot, pre, act, sems, asem, ssem):
+def pack_rows(ref, out):
+    n = out.shape[0]
+    left = lax.broadcasted_iota(jnp.int32, (n, LANES), 1) < 64
+    out[...] = jnp.where(left, ref[0:n, :], ref[n : 2 * n, :])
+
+
+def unpack_rows(ref, out, start=0):
+    n = ref.shape[0]
+    left = lax.broadcasted_iota(jnp.int32, (n, LANES), 1) < 64
+    v = ref[...]
+    w = pltpu.roll(v, 64, 1)
+    out[start : start + n, :] = jnp.where(left, v, w)
+    out[start + n : start + 2 * n, :] = jnp.where(left, w, v)
+
+
+def prep_kernel(core, send_h, cot_h, pre_h, act_h, gd, xs0, xs1, ys, zs, send, cot, pre, act, sems, asem, ssem, xf):
     blocks = cot.shape[0]
     listed = send.shape[0]
     pairs = ((cot_h, cot, 0), (pre_h, pre, 1))
@@ -120,42 +135,50 @@
         r0 = pl.multiple_of(jnp.minimum(send[i], blocks - 1) * VOL, VOL)
         for side in range(2):
             f = 7 * side
-            (xs0, xs1)[side][i * 64 : (i + 1) * 64, :] = gd[pl.ds(r0 + f * 64, 64), :]
+            xf[side, i * 64 : (i + 1) * 64, :] = gd[pl.ds(r0 + f * 64, 64), :]
             for x in range(8):
                 ys[side, i * 64 + x * 8 : i * 64 + x * 8 + 8, :] = gd[pl.ds(r0 + x * 64 + f * 8, 8), :]
             zs[side, i * 64 : (i + 1) * 64, :] = gd[pl.ds(r0 + f, 64, stride=8), :]
-
-
-def pack_y_kernel(ys, rx0, rx1, after, out0, out1):
+    pack_rows(xf.at[0], xs0)
+    pack_rows(xf.at[1], xs1)
+
+
+def pack_y_kernel(ys, rx0, rx1, after, out0, out1, xf, yf):
     face = ys.shape[1]
     listed = face // 64
+    unpack_rows(rx0, xf.at[0])
+    unpack_rows(rx1, xf.at[1])
     for side, out in ((0, out0), (1, out1)):
         f = 7 * side
-        out[0:face, :] = ys[side]
-        for j, rx in enumerate((rx0, rx1)):
+        yf[0:face, :] = ys[side]
+        for j in range(2):
             for s in range(listed):
                 row = face + (j * listed + s) * 8
-                out[row : row + 8, :] = rx[s * 64 + f * 8 : s * 64 + f * 8 + 8, :]
-
-
-def pack_z_kernel(zs, rx0, rx1, ry0, ry1, after, out0, out1):
+                yf[row : row + 8, :] = xf[j, s * 64 + f * 8 : s * 64 + f * 8 + 8, :]
+        pack_rows(yf, out)
+
+
+def pack_z_kernel(zs, rx0, rx1, ry0, ry1, after, out0, out1, x0, x1, y0, y1, zf):
     face = zs.shape[1]
     listed = face // 64
     edge = listed * 8
     corner = -(-listed // 8) * 8
+    for src, full in ((rx0, x0), (rx1, x1), (ry0, y0), (ry1, y1)):
+        unpack_rows(src, full)
     for side, out in ((0, out0), (1, out1)):
         f = 7 * side
-        out[0:face, :] = zs[side]
-        for j, src in enumerate((rx0, rx1, ry0, ry1)):
+        zf[0:face, :] = zs[side]
+        for j, src in enumerate((x0, x1, y0, y1)):
             row = face + j * edge
-            out[row : row + edge, :] = src[pl.ds(f, edge, stride=8), :]
-        for j, src in enumerate((ry0, ry1)):
+            zf[row : row + edge, :] = src[pl.ds(f, edge, stride=8), :]
+        for j, src in enumerate((y0, y1)):
             for i in range(2):
                 row = face + 4 * edge + corner * (2 * j + i)
-                out[row : row + corner, :] = jnp.zeros((corner, LANES), F32)
+                zf[row : row + corner, :] = jnp.zeros((corner, LANES), F32)
                 for s in range(listed):
                     at = face + i * edge + s * 8 + f
-                    out[row + s : row + s + 1, :] = src[at : at + 1, :]
+                    zf[row + s : row + s + 1, :] = src[at : at + 1, :]
+        pack_rows(zf, out)
 
 
 def interior_block(b, r0, gd, feat, act, at, p, kg_in, kg, rt, bias_in, bias, z):
@@ -269,8 +292,8 @@
     blocks = od.shape[0]
     row = 0
     for ref in (rx0, rx1, ry0, ry1, rz0, rz1):
-        src[row : row + ref.shape[0], :] = ref[...]
-        row += ref.shape[0]
+        unpack_rows(ref, src, row)
+        row += 2 * ref.shape[0]
     pa[...] = p0[...]
     kg[...] = kg0[...]
     lane64 = lax.broadcasted_iota(jnp.int32, (64, LANES), 1) < 64
@@ -363,7 +386,6 @@
         if odd:
             pay[t * 64 : (t + 1) * 64, :] = jnp.where(lane64, held, u) * scale
         held = u
-    pay[14 * 64 :, :] = jnp.zeros((PAY - 14 * 64, LANES), F32)
     me = core[0]
     mine[...] = pay[pl.ds(pl.multiple_of(me * (PAY // 2), PAY // 2), PAY // 2), :]
     other[...] = pay[pl.ds(pl.multiple_of((1 - me) * (PAY // 2), PAY // 2), PAY // 2), :]
@@ -431,7 +453,7 @@
 
     gd, xs0, xs1, ys, zs = pl.pallas_call(
         prep_kernel,
-        out_shape=(vm((rows, LANES)), vm((face, LANES)), vm((face, LANES)), vm((2, face, LANES)), vm((2, face, LANES))),
+        out_shape=(vm((rows, LANES)), vm((face // 2, LANES)), vm((face // 2, LANES)), vm((2, face, LANES)), vm((2, face, LANES))),
         in_specs=[SM] + [ANY] * 4,
         out_specs=(VM,) * 5,
         scratch_shapes=[
@@ -442,6 +464,7 @@
             pltpu.SemaphoreType.DMA((blocks, 2)),
             pltpu.SemaphoreType.DMA,
             pltpu.SemaphoreType.DMA,
+            pltpu.VMEM((2, face, LANES), F32),
         ],
         name="prep", compiler_params=ROOM,
     )(core, far(send_list), far(cotangent), far(preact), far(active))
@@ -480,13 +503,17 @@
         )(local(gd), far(features), active, local(rt), local(kg), local(bias), *[local(e) for e in earlier], after)
 
     ys0, ys1 = pl.pallas_call(
-        pack_y_kernel, out_shape=(vm((yr, LANES)),) * 2, in_specs=[VM] * 3 + [ANY], out_specs=(VM,) * 2,
+        pack_y_kernel, out_shape=(vm((yr // 2, LANES)),) * 2,
+        scratch_shapes=[pltpu.VMEM((2, face, LANES), F32), pltpu.VMEM((yr, LANES), F32)],
+        in_specs=[VM] * 3 + [ANY], out_specs=(VM,) * 2,
         name="pack_y", compiler_params=ROOM,
     )(local(ys), local(rx0), local(rx1), bias)
     ry0, ry1 = both_ways(ys0, ys1, "gy")
     at1, p1, kg, bias = more(parts[1], (), kg, bias, ys0, "interior1")
     zs0, zs1 = pl.pallas_call(
-        pack_z_kernel, out_shape=(vm((zr, LANES)),) * 2, in_specs=[VM] * 5 + [ANY], out_specs=(VM,) * 2,
+        pack_z_kernel, out_shape=(vm((zr // 2, LANES)),) * 2,
+        scratch_shapes=[pltpu.VMEM((n, LANES), F32) for n in (face, face, yr, yr, zr)],
+        in_specs=[VM] * 5 + [ANY], out_specs=(VM,) * 2,
         name="pack_z", compiler_params=ROOM,
     )(local(zs), local(rx0), local(rx1), local(ry0), local(ry1), bias)
     rz0, rz1 = both_ways(zs0, zs1, AXZ)
@@ -516,11 +543,18 @@
     )(local(p), active)
     half = mine + arrived
     plane, depth = lax.axis_size(("x", "gy")), lax.axis_size(("zh", "zl"))
-    spread = lax.all_to_all(half.reshape(plane, PAY // 2 // plane, LANES), ("x", "gy"), 0, 0, tiled=True)
-    share = jnp.sum(spread, axis=0)
-    share = lax.all_to_all(jnp.broadcast_to(share[None], (depth,) + share.shape), ("zh", "zl"), 0, 0, tiled=True)
-    share = jnp.sum(share, axis=0)
-    whole = lax.all_to_all(jnp.broadcast_to(share[None], spread.shape), ("x", "gy"), 0, 0, tiled=True)
+    chunk = PAY // 2 // plane // 2
+
+    def trade(x, count, axes):
+        x = lax.all_to_all(x.reshape(count * chunk, 2, LANES), axes, 0, 0, tiled=True)
+        return x.reshape(count, chunk, 2, LANES)
+
+    def copies(x, count):
+        return jnp.broadcast_to(x[None], (count,) + x.shape)
+
+    share = jnp.sum(trade(half, plane, ("x", "gy")), axis=0)
+    share = jnp.sum(trade(copies(share, depth), depth, ("zh", "zl")), axis=0)
+    whole = trade(copies(share, plane), plane, ("x", "gy"))
     whole = whole.reshape(PAY // 2, LANES)
     rest = lax.ppermute(whole, "core", swap)
 

time: 110 us -> 107 us (0.973)
  blocking collectives: 62.7 us -> 59.3 us
    all_to_all x3, blocking collectives: 62.7 us -> 59.3 us  [trade(): lax.all_to_all(x.reshape(count * chunk, 2, LANES), axes, 0, 0, tiled=True)]
    ppermute x1, starting transfers between devices: 3.02 us -> 1.92 us  [shards(): arrived = lax.ppermute(other, 'core', swap)]
  transfers between devices with their start and end apart: 8 -> 8, of which waited for: 2 -> 1; matrix products, arithmetic and copies ran while one was open for 0% -> 0% of each run, Pallas kernels for 10% -> 10%
where the time goes in v3:
time: 107 us; the launch traced here: 106 us
  blocking collectives  59.3 us (55%)
  starting transfers between devices  27.6 us (26%)
  Pallas kernels  16.2 us (15%)
  waiting for transfers between devices  1.47 us (1%)
    all_to_all x3, blocking collectives, trade(): lax.all_to_all(x.reshape(count * chunk, 2, LANES), axes, 0, 0, tiled=True)  59.3 us
    ppermute x3, starting transfers between devices, both_ways(): up = lax.ppermute(high, axis, [(i, i + 1) for i in range(n - 1)])  14.3 us
    pallas_call x2, Pallas kernels, more(): pl.pallas_call(functools.partial(next_kernel, part, len(earlier) // 2), i...  6.42 us
    ppermute x1, starting transfers between devices, shards(): rest = lax.ppermute(whole, 'core', swap)  6.19 us
    ppermute x3, starting transfers between devices, both_ways(): down = lax.ppermute(low, axis, [(i + 1, i) for i in range(n - 1)])  5.14 us
    pallas_call x1, Pallas kernels, shards(): pl.pallas_call(functools.partial(first_kernel, parts[0]), in_specs=[VM, A...  2.96 us
    pallas_call x1, Pallas kernels, shards(): pl.pallas_call(functools.partial(halo_kernel, scale), out_shape=(vm((PAY...  2.16 us
  transfers between devices with their start and end apart: 8, of which 1 were waited for; matrix products, arithmetic and copies ran while one was open for 0% of the time, Pallas kernels for 10%

profile of v3, /device:TPU:1, one launch (start us, length us, event | category | flops | bytes accessed | tf_op | source)
XLA Modules:
  0.0 106.3 jit_solution(16228225157995782127)
XLA Ops:
  0.6 1.9 %prep.1 = (f32[2048,128]{1,0:T(8,128)S(1)}, f32[96,128]{1,0:T(8,128)S(1)}, f32[96,128]{1,0:T(8,128)S(1)}, f32[2,192,128]{2,1,0:T(8,128)S(1)}, f32[2,192,128]{2,1,0:T(8,128)S(1)}) custom-call(s32[1]{0:T(128)} %bitcast.core, s32[3]{0:T(128)} %send_h.1, f32[4,64,512]{2,1,0:T(8,128)} %cot_h.1, f32[4,64,512]{2,1,0:T(8,128)} %pre_h.1, s32[4,512]{1,0:T(4,128)} %act.3), custom_call_target="tpu_custom_call" | custom-call | tf_op jit(solution)/shard_map/prep/pallas_call | solution.py:454
  2.5 3.9 %collective-permute-start = (f32[96,128]{1,0:T(8,128)S(1)}, f32[96,128]{1,0:T(8,128)S(1)}, u32[]{:S(2)}, u32[]{:S(2)}) collective-permute-start(f32[96,128]{1,0:T(8,128)S(1)} %get-tuple-element.31), channel_id=1, source_target_pairs={{0,64},{64,128},{128,192},{192,256},{256,320},{320,384},{384,448},... | collective-permute-start | bytes 147464 | tf_op jit(solution)/shard_map/ppermute | solution.py:427
  6.5 1.3 %collective-permute-start.1 = (f32[96,128]{1,0:T(8,128)S(1)}, f32[96,128]{1,0:T(8,128)S(1)}, u32[]{:S(2)}, u32[]{:S(2)}) collective-permute-start(f32[96,128]{1,0:T(8,128)S(1)} %get-tuple-element.32), channel_id=1, source_target_pairs={{64,0},{128,64},{192,128},{256,192},{320,256},{384,320},{448,384},... | collective-permute-start | bytes 147464 | tf_op jit(solution)/shard_map/ppermute | solution.py:428
  7.8 0.7 copy-done
  8.5 3.0 %interior0.1 = (f32[512,128]{1,0:T(8,128)S(1)}, f32[512,128]{1,0:T(8,128)S(1)}, f32[384,1152]{1,0:T(8,128)S(1)}, bf16[384,1152]{1,0:T(8,128)(2,1)S(1)}, f32[8,128]{1,0:T(8,128)S(1)}) custom-call(f32[2048,128]{1,0:T(8,128)S(1)} %get-tuple-element.30.gd.refs_0_, f32[4,64,512]{2,1,0:T(8,128)} %refs_1_.3, s32[4,512]{1,0:T(4,128)S(1)} %copy-done, ...), custom_call_target="tpu_custom_call" | custom-call | tf_op jit(solution)/shard_map/interior0/pallas_call | solution.py:485
  11.5 0.1 pack_y.1
  11.5 1.3 %collective-permute-start.3 = (f32[120,128]{1,0:T(8,128)S(1)}, f32[120,128]{1,0:T(8,128)S(1)}, u32[]{:S(2)}, u32[]{:S(2)}) collective-permute-start(f32[120,128]{1,0:T(8,128)S(1)} %get-tuple-element.36.refs_6_), channel_id=1, source_target_pairs={{8,0},{16,8},{24,16},{32,24},{40,32},{48,40},{56,48},{9,1},{17,9},... | collective-permute-start | bytes 184328 | tf_op jit(solution)/shard_map/ppermute | solution.py:428
  12.8 4.0 %collective-permute-start.2 = (f32[120,128]{1,0:T(8,128)S(1)}, f32[120,128]{1,0:T(8,128)S(1)}, u32[]{:S(2)}, u32[]{:S(2)}) collective-permute-start(f32[120,128]{1,0:T(8,128)S(1)} %get-tuple-element.35), channel_id=1, source_target_pairs={{0,8},{8,16},{16,24},{24,32},{32,40},{40,48},{48,56},{1,9},{9,17},... | collective-permute-start | bytes 184328 | tf_op jit(solution)/shard_map/ppermute | solution.py:427
  16.9 2.5 %interior1.1 = (f32[512,128]{1,0:T(8,128)S(1)}, f32[512,128]{1,0:T(8,128)S(1)}, f32[384,1152]{1,0:T(8,128)S(1)}, f32[8,128]{1,0:T(8,128)S(1)}) custom-call(f32[2048,128]{1,0:T(8,128)S(1)} %get-tuple-element.30.gd.refs_0_, f32[4,64,512]{2,1,0:T(8,128)} %refs_1_.3, s32[4,512]{1,0:T(4,128)S(1)} %copy-done.1, ...), custom_call_target="tpu_custom_call" | custom-call | tf_op jit(solution)/shard_map/interior1/pallas_call | solution.py:496
  19.3 0.2 pack_z.1
  19.5 6.4 %collective-permute-start.4 = (f32[160,128]{1,0:T(8,128)S(1)}, f32[160,128]{1,0:T(8,128)S(1)}, u32[]{:S(2)}, u32[]{:S(2)}) collective-permute-start(f32[160,128]{1,0:T(8,128)S(1)} %get-tuple-element.41), channel_id=1, source_target_pairs={{0,1},{1,2},{2,3},{3,4},{4,5},{5,6},{6,7},{8,9},{9,10},{10,11},{11... | collective-permute-start | bytes 245768 | tf_op jit(solution)/shard_map/ppermute | solution.py:427
  25.9 2.6 %collective-permute-start.5 = (f32[160,128]{1,0:T(8,128)S(1)}, f32[160,128]{1,0:T(8,128)S(1)}, u32[]{:S(2)}, u32[]{:S(2)}) collective-permute-start(f32[160,128]{1,0:T(8,128)S(1)} %get-tuple-element.42.refs_10_), channel_id=1, source_target_pairs={{1,0},{2,1},{3,2},{4,3},{5,4},{6,5},{7,6},{9,8},{10,9},{11,10},{12... | collective-permute-start | bytes 245768 | tf_op jit(solution)/shard_map/ppermute | solution.py:428
  28.5 4.0 %interior2.1 = (f32[2048,128]{1,0:T(8,128)S(1)}, f32[2048,128]{1,0:T(8,128)S(1)}, f32[384,1152]{1,0:T(8,128)S(1)}, f32[8,128]{1,0:T(8,128)S(1)}) custom-call(f32[2048,128]{1,0:T(8,128)S(1)} %get-tuple-element.30.gd.refs_0_, f32[4,64,512]{2,1,0:T(8,128)} %refs_1_.3, s32[4,512]{1,0:T(4,128)S(1)} %copy-done.1, ...), custom_call_target="tpu_custom_call" | custom-call | tf_op jit(solution)/shard_map/interior2/pallas_call | solution.py:496
  32.5 2.2 %halo.1 = (f32[448,128]{1,0:T(8,128)S(1)}, f32[448,128]{1,0:T(8,128)S(1)}, f32[2048,128]{1,0:T(8,128)S(1)}) custom-call(s32[4,27]{1,0:T(4,128)S(1)} %copy-done.3, s32[4,27]{1,0:T(4,128)S(1)} %copy-done.4, s32[756]{0:T(1024)S(1)} %copy-done.2, s32[1]{0:T(128)} %bitcast.core, f32[2048,128]{1,0:T(8,128)S(1)} %get-tuple-element.30.gd.refs_0_, ...), custom_call_target="tpu_custom_call" | custom-call | tf_op jit(solution)/shard_map/halo/pallas_call | solution.py:523
  34.7 1.9 %collective-permute-start.6 = (f32[448,128]{1,0:T(8,128)S(1)}, f32[448,128]{1,0:T(8,128)S(1)}, u32[]{:S(2)}, u32[]{:S(2)}) collective-permute-start(f32[448,128]{1,0:T(8,128)S(1)} %get-tuple-element.54), channel_id=1, source_target_pairs={{0,1},{1,0},{2,3},{3,2},{4,5},{5,4},{6,7},{7,6},{8,9},{9,8},{10,11... | collective-permute-start | bytes 688136 | tf_op jit(solution)/shard_map/ppermute | solution.py:540
  36.6 1.5 %collective-permute-done.6 = f32[448,128]{1,0:T(8,128)S(1)} collective-permute-done((f32[448,128]{1,0:T(8,128)S(1)}, f32[448,128]{1,0:T(8,128)S(1)}, u32[]{:S(2)}, u32[]{:S(2)}) %collective-permute-start.6) | collective-permute-done | bytes 229408 | tf_op jit(solution)/shard_map/ppermute | solution.py:540
  38.1 33.6 %all_to_all.15 = f32[224,2,128]{2,1,0:T(2,128)S(1)} all-to-all(f32[224,2,128]{2,1,0:T(2,128)S(1)} %bitcast.12), channel_id=1, replica_groups=mesh['zh'=2,'x'=4,'gy'=8,'zl'=4,'core'=2] {'x','gy'}, dimensions={0} | all-to-all | bytes 458752 | tf_op jit(solution)/shard_map/all_to_all | solution.py:549
  71.7 0.1 reduce_sum.18
  71.8 10.4 %all_to_all.16 = f32[56,2,128]{2,1,0:T(2,128)S(1)} all-to-all(f32[56,2,128]{2,1,0:T(2,128)S(1)} %bitcast.14), channel_id=1, replica_groups=mesh['zh'=2,'x'=4,'gy'=8,'zl'=4,'core'=2] {'zh','zl'}, dimensions={0} | all-to-all | bytes 114688 | tf_op jit(solution)/shard_map/all_to_all | solution.py:549
  82.2 0.1 broadcast_in_dim.5
  82.2 15.3 %all_to_all.17 = f32[224,2,128]{2,1,0:T(2,128)S(1)} all-to-all(f32[224,2,128]{2,1,0:T(2,128)S(1)} %bitcast.11), channel_id=1, replica_groups=mesh['zh'=2,'x'=4,'gy'=8,'zl'=4,'core'=2] {'x','gy'}, dimensions={0} | all-to-all | bytes 458752 | tf_op jit(solution)/shard_map/all_to_all | solution.py:549
  97.6 6.2 %collective-permute-start.7 = (f32[448,128]{1,0:T(8,128)S(1)}, f32[448,128]{1,0:T(8,128)S(1)}, u32[]{:S(2)}, u32[]{:S(2)}) collective-permute-start(f32[448,128]{1,0:T(8,128)S(1)} %bitcast.8), channel_id=1, source_target_pairs={{0,1},{1,0},{2,3},{3,2},{4,5},{5,4},{6,7},{7,6},{8,9},{9,8},{10,11... | collective-permute-start | bytes 688136 | tf_op jit(solution)/shard_map/ppermute | solution.py:559
  103.8 1.4 %finish.1 = f32[4,64,512]{2,1,0:T(8,128)} custom-call(f32[2048,128]{1,0:T(8,128)S(1)} %get-tuple-element.52.pa, s32[4,512]{1,0:T(4,128)S(1)} %copy-done.1), custom_call_target="tpu_custom_call" | custom-call | tf_op jit(solution)/shard_map/finish/pallas_call | solution.py:541
  105.2 1.1 %unpack.1 = (f32[27,64,64]{2,1,0:T(8,128)}, f32[1,64]{1,0:T(1,128)}) custom-call(s32[1]{0:T(128)} %bitcast.core, f32[448,128]{1,0:T(8,128)S(1)} %bitcast.9, f32[448,128]{1,0:T(8,128)S(1)} %collective-permute-done.7.other), custom_call_target="tpu_custom_call" | custom-call | tf_op jit(solution)/shard_map/unpack/pallas_call | solution.py:561
  (19 shorter events, 0.1 us)
Async XLA Ops:
  0.6 16.2 %copy-start.1 = (s32[4,512]{1,0:T(4,128)S(1)}, s32[4,512]{1,0:T(4,128)}, u32[]{:S(2)}) copy-start(s32[4,512]{1,0:T(4,128)} %act.3) | copy-start | bytes 24580
  2.5 8.9 %collective-permute-start = (f32[96,128]{1,0:T(8,128)S(1)}, f32[96,128]{1,0:T(8,128)S(1)}, u32[]{:S(2)}, u32[]{:S(2)}) collective-permute-start(f32[96,128]{1,0:T(8,128)S(1)} %get-tuple-element.31), channel_id=1, source_target_pairs={{0,64},{64,128},{128,192},{192,256},{256,320},{320,384},{384,448},... | collective-permute-start | bytes 147464 | tf_op jit(solution)/shard_map/ppermute | solution.py:427
  6.5 5.0 %collective-permute-start.1 = (f32[96,128]{1,0:T(8,128)S(1)}, f32[96,128]{1,0:T(8,128)S(1)}, u32[]{:S(2)}, u32[]{:S(2)}) collective-permute-start(f32[96,128]{1,0:T(8,128)S(1)} %get-tuple-element.32), channel_id=1, source_target_pairs={{64,0},{128,64},{192,128},{256,192},{320,256},{384,320},{448,384},... | collective-permute-start | bytes 147464 | tf_op jit(solution)/shard_map/ppermute | solution.py:428
  7.8 0.7 copy-start
  11.5 7.8 %collective-permute-start.3 = (f32[120,128]{1,0:T(8,128)S(1)}, f32[120,128]{1,0:T(8,128)S(1)}, u32[]{:S(2)}, u32[]{:S(2)}) collective-permute-start(f32[120,128]{1,0:T(8,128)S(1)} %get-tuple-element.36.refs_6_), channel_id=1, source_target_pairs={{8,0},{16,8},{24,16},{32,24},{40,32},{48,40},{56,48},{9,1},{17,9},... | collective-permute-start | bytes 184328 | tf_op jit(solution)/shard_map/ppermute | solution.py:428
  12.8 6.5 %collective-permute-start.2 = (f32[120,128]{1,0:T(8,128)S(1)}, f32[120,128]{1,0:T(8,128)S(1)}, u32[]{:S(2)}, u32[]{:S(2)}) collective-permute-start(f32[120,128]{1,0:T(8,128)S(1)} %get-tuple-element.35), channel_id=1, source_target_pairs={{0,8},{8,16},{16,24},{24,32},{32,40},{40,48},{48,56},{1,9},{9,17},... | collective-permute-start | bytes 184328 | tf_op jit(solution)/shard_map/ppermute | solution.py:427
  19.5 13.0 %collective-permute-start.4 = (f32[160,128]{1,0:T(8,128)S(1)}, f32[160,128]{1,0:T(8,128)S(1)}, u32[]{:S(2)}, u32[]{:S(2)}) collective-permute-start(f32[160,128]{1,0:T(8,128)S(1)} %get-tuple-element.41), channel_id=1, source_target_pairs={{0,1},{1,2},{2,3},{3,4},{4,5},{5,6},{6,7},{8,9},{9,10},{10,11},{11... | collective-permute-start | bytes 245768 | tf_op jit(solution)/shard_map/ppermute | solution.py:427
  25.9 6.6 %collective-permute-start.5 = (f32[160,128]{1,0:T(8,128)S(1)}, f32[160,128]{1,0:T(8,128)S(1)}, u32[]{:S(2)}, u32[]{:S(2)}) collective-permute-start(f32[160,128]{1,0:T(8,128)S(1)} %get-tuple-element.42.refs_10_), channel_id=1, source_target_pairs={{1,0},{2,1},{3,2},{4,3},{5,4},{6,5},{7,6},{9,8},{10,9},{11,10},{12... | collective-permute-start | bytes 245768 | tf_op jit(solution)/shard_map/ppermute | solution.py:428
  28.5 4.0 %copy-start.2 = (s32[756]{0:T(1024)S(1)}, s32[756]{0:T(1024)}, u32[]{:S(2)}) copy-start(s32[756]{0:T(1024)} %constant.8.clone.tb) | copy-start | bytes 9076
  28.5 4.0 %copy-start.3 = (s32[4,27]{1,0:T(4,128)S(1)}, s32[4,27]{1,0:T(4,128)}, u32[]{:S(2)}) copy-start(s32[4,27]{1,0:T(4,128)} %od.1) | copy-start | bytes 1300
  28.5 4.0 %copy-start.4 = (s32[4,27]{1,0:T(4,128)S(1)}, s32[4,27]{1,0:T(4,128)}, u32[]{:S(2)}) copy-start(s32[4,27]{1,0:T(4,128)} %os_.1) | copy-start | bytes 1300
  34.7 3.4 %collective-permute-start.6 = (f32[448,128]{1,0:T(8,128)S(1)}, f32[448,128]{1,0:T(8,128)S(1)}, u32[]{:S(2)}, u32[]{:S(2)}) collective-permute-start(f32[448,128]{1,0:T(8,128)S(1)} %get-tuple-element.54), channel_id=1, source_target_pairs={{0,1},{1,0},{2,3},{3,2},{4,5},{5,4},{6,7},{7,6},{8,9},{9,8},{10,11... | collective-permute-start | bytes 688136 | tf_op jit(solution)/shard_map/ppermute | solution.py:540
  97.6 7.6 %collective-permute-start.7 = (f32[448,128]{1,0:T(8,128)S(1)}, f32[448,128]{1,0:T(8,128)S(1)}, u32[]{:S(2)}, u32[]{:S(2)}) collective-permute-start(f32[448,128]{1,0:T(8,128)S(1)} %bitcast.8), channel_id=1, source_target_pairs={{0,1},{1,0},{2,3},{3,2},{4,5},{5,4},{6,7},{7,6},{8,9},{9,8},{10,11... | collective-permute-start | bytes 688136 | tf_op jit(solution)/shard_map/ppermute | solution.py:559

commit v4 on v3

--- a/solution.py
+++ b/solution.py
@@ -14,9 +14,7 @@
 VOL = 512
 LANES = 128
 PAY = 896
-AX = ("zh", "x", "gy", "zl", "core")
-AXX = ("zh", "x")
-AXZ = ("zl", "core")
+AX = "d"
 
 FACE = 64
 
@@ -287,19 +285,75 @@
     return out
 
 
-def halo_kernel(scale, od, os_, tb, core, gd, rx0, rx1, ry0, ry1, rz0, rz1, at, rt, bias, p0, kg0,
-                mine, other, pa, src, pb, pw, pay, kg):
+def plane_slot(b, axis, sign):
+    return b * 6 + 2 * axis + (sign + 1) // 2
+
+
+def for_planes(od, visit):
+    def block(b, carry):
+        for axis in range(3):
+            for sign in (-1, 1):
+                pieces = plane_pieces(axis, sign)
+                found = od[b, pieces[0][0]] != 27
+                for o, _, _ in pieces[1:]:
+                    found = found | (od[b, o] != 27)
+
+                @pl.when(found)
+                def _(axis=axis, sign=sign):
+                    visit(b, axis, sign)
+
+        return carry
+
+    lax.fori_loop(0, od.shape[0], block, 0)
+
+
+def edges_kernel(od, pws, rt, p, pa):
+    pa[...] = p[...]
+
+    def plane(b, axis, sign):
+        face = 0 if sign == -1 else 7
+        pw = pws.at[plane_slot(b, axis, sign)]
+        r0 = b * VOL
+        k = 1 - sign
+        if axis == 0:
+            rows = pl.ds(pl.multiple_of(r0 + face * 64, 64), 64)
+            pa[rows, :] += nt(pw[...], rt[k * 128 : (k + 1) * 128, :])
+        elif axis == 1:
+            acc = jnp.zeros((64, LANES), F32)
+            for i in range(3):
+                acc = acc + nt(pw[:, i * 384 : (i + 1) * 384], rt[i * 128 : (i + 1) * 128, k * 384 : (k + 1) * 384])
+            for x in range(8):
+                rows = pl.ds(pl.multiple_of(r0 + x * 64 + face * 8, 8), 8)
+                pa[rows, :] += acc[x * 8 : x * 8 + 8, :]
+        else:
+            acc = jnp.zeros((64, LANES), F32)
+            for i in range(3):
+                for j in range(3):
+                    part = pw[:, (i * 3 + j) * 128 : (i * 3 + j + 1) * 128]
+                    acc = acc + nt(part, rt[i * 128 : (i + 1) * 128, (j * 3 + k) * 128 : (j * 3 + k + 1) * 128])
+            rows = pl.ds(r0 + face, 64, stride=8)
+            pa[rows, :] = pa[rows, :] + acc
+
+    for_planes(od, plane)
+
+
+def join_kernel(mine, arrived, after, half):
+    half[...] = mine[...] + arrived[...]
+
+
+def halo_kernel(scale, od, os_, tb, core, gd, rx0, rx1, ry0, ry1, rz0, rz1, at, bias, kg0,
+                mine, other, pws, src, pb, pay, kg):
     blocks = od.shape[0]
     row = 0
     for ref in (rx0, rx1, ry0, ry1, rz0, rz1):
         unpack_rows(ref, src, row)
         row += 2 * ref.shape[0]
-    pa[...] = p0[...]
     kg[...] = kg0[...]
     lane64 = lax.broadcasted_iota(jnp.int32, (64, LANES), 1) < 64
 
     def plane(b, axis, sign):
         face = 0 if sign == -1 else 7
+        pw = pws.at[plane_slot(b, axis, sign)]
         pb[...] = jnp.zeros(pb.shape, F32)
         for o, r, q in plane_pieces(axis, sign):
             d = od[b, o]
@@ -330,48 +384,21 @@
         r0 = b * VOL
         k = 1 - sign
         if axis == 0:
-            rows = pl.ds(pl.multiple_of(r0 + face * 64, 64), 64)
-            ap = at[rows, :].astype(BF16)
-            span = slice(k * 128, (k + 1) * 128)
-            kg[span, :] += tn(ap, pw[...])
-            pa[rows, :] += nt(pw[...], rt[span, :])
+            ap = at[pl.ds(pl.multiple_of(r0 + face * 64, 64), 64), :].astype(BF16)
+            kg[k * 128 : (k + 1) * 128, :] += tn(ap, pw[...])
         elif axis == 1:
             starts = [pl.multiple_of(r0 + x * 64 + face * 8, 8) for x in range(8)]
             ap = jnp.concatenate([at[pl.ds(s, 8), :] for s in starts], axis=0).astype(BF16)
-            acc = jnp.zeros((64, LANES), F32)
-            cols = slice(k * 384, (k + 1) * 384)
             for i in range(3):
-                part = pw[:, i * 384 : (i + 1) * 384]
-                kg[i * 128 : (i + 1) * 128, cols] += tn(ap, part)
-                acc = acc + nt(part, rt[i * 128 : (i + 1) * 128, cols])
-            for x, s in enumerate(starts):
-                pa[pl.ds(s, 8), :] += acc[x * 8 : x * 8 + 8, :]
+                kg[i * 128 : (i + 1) * 128, k * 384 : (k + 1) * 384] += tn(ap, pw[:, i * 384 : (i + 1) * 384])
         else:
-            rows = pl.ds(r0 + face, 64, stride=8)
-            ap = at[rows, :].astype(BF16)
-            acc = jnp.zeros((64, LANES), F32)
+            ap = at[pl.ds(r0 + face, 64, stride=8), :].astype(BF16)
             for i in range(3):
                 for j in range(3):
                     part = pw[:, (i * 3 + j) * 128 : (i * 3 + j + 1) * 128]
-                    cols = slice((j * 3 + k) * 128, (j * 3 + k + 1) * 128)
-                    kg[i * 128 : (i + 1) * 128, cols] += tn(ap, part)
-                    acc = acc + nt(part, rt[i * 128 : (i + 1) * 128, cols])
-            pa[rows, :] = pa[rows, :] + acc
-
-    def block(b, carry):
-        for axis in range(3):
-            for sign in (-1, 1):
-                found = od[b, plane_pieces(axis, sign)[0][0]] != 27
-                for o, _, _ in plane_pieces(axis, sign)[1:]:
-                    found = found | (od[b, o] != 27)
-
-                @pl.when(found)
-                def _(axis=axis, sign=sign):
-                    plane(b, axis, sign)
-
-        return carry
-
-    lax.fori_loop(0, blocks, block, 0)
+                    kg[i * 128 : (i + 1) * 128, (j * 3 + k) * 128 : (j * 3 + k + 1) * 128] += tn(ap, part)
+
+    for_planes(od, plane)
 
     for n in range(28):
         t, odd = n // 2, n % 2
@@ -422,11 +449,26 @@
     return jax.ShapeDtypeStruct(shape, dtype)
 
 
-def both_ways(low, high, axis):
-    n = lax.axis_size(axis)
-    up = lax.ppermute(high, axis, [(i, i + 1) for i in range(n - 1)])
-    down = lax.ppermute(low, axis, [(i + 1, i) for i in range(n - 1)])
+def both_ways(low, high, ids, axis):
+    lines = np.moveaxis(ids, axis, -1)
+    steps = [(int(a), int(b)) for a, b in zip(lines[..., :-1].ravel(), lines[..., 1:].ravel())]
+    up = lax.ppermute(high, AX, steps)
+    down = lax.ppermute(low, AX, [(b, a) for a, b in steps])
     return up, down
+
+
+def sum_groups(ids):
+    zh, x, y, zl, _ = ids.shape
+    first, second = [], []
+    for core in range(2):
+        part = ids[..., core]
+        if core == 0 or y != zh * zl:
+            first += part.transpose(0, 3, 1, 2).reshape(zh * zl, x * y).tolist()
+            second += part.transpose(1, 2, 0, 3).reshape(x * y, zh * zl).tolist()
+        else:
+            first += part.transpose(2, 1, 0, 3).reshape(y, x * zh * zl).tolist()
+            second += part.transpose(1, 0, 3, 2).reshape(x * zh * zl, y).tolist()
+    return first, second
 
 
 def vm(shape, dtype=F32):
@@ -441,14 +483,15 @@
     return pltpu.with_memory_space_constraint(x, pltpu.HBM)
 
 
-def shards(features, preact, cotangent, kernel, active, owner_dir, owner_slot, send_list):
+def shards(grid, features, preact, cotangent, kernel, active, owner_dir, owner_slot, send_list):
     blocks, channels, volume = features.shape
     listed = send_list.shape[0]
     lay = layout_of(blocks, listed)
     face, yr, zr = lay["face"], lay["y_rows"], lay["z_rows"]
     rows = blocks * VOL
-    devices = lax.axis_size(AX)
-    core = lax.axis_index("core").astype(jnp.int32).reshape(1)
+    devices = int(np.prod(grid))
+    ids = np.arange(devices).reshape(grid)
+    core = (lax.axis_index(AX) & 1).astype(jnp.int32).reshape(1)
     scale = float((volume * blocks * devices) ** -0.5)
 
     gd, xs0, xs1, ys, zs = pl.pallas_call(
@@ -468,7 +511,7 @@
         ],
         name="prep", compiler_params=ROOM,
     )(core, far(send_list), far(cotangent), far(preact), far(active))
-    rx0, rx1 = both_ways(xs0, xs1, AXX)
+    rx0, rx1 = both_ways(xs0, xs1, ids, 0)
 
     third = max(blocks // 4, 1)
     parts = (range(third), range(third, 2 * third), range(2 * third, blocks))
@@ -508,7 +551,7 @@
         in_specs=[VM] * 3 + [ANY], out_specs=(VM,) * 2,
         name="pack_y", compiler_params=ROOM,
     )(local(ys), local(rx0), local(rx1), bias)
-    ry0, ry1 = both_ways(ys0, ys1, "gy")
+    ry0, ry1 = both_ways(ys0, ys1, ids, 1)
     at1, p1, kg, bias = more(parts[1], (), kg, bias, ys0, "interior1")
     zs0, zs1 = pl.pallas_call(
         pack_z_kernel, out_shape=(vm((zr // 2, LANES)),) * 2,
@@ -516,47 +559,56 @@
         in_specs=[VM] * 5 + [ANY], out_specs=(VM,) * 2,
         name="pack_z", compiler_params=ROOM,
     )(local(zs), local(rx0), local(rx1), local(ry0), local(ry1), bias)
-    rz0, rz1 = both_ways(zs0, zs1, AXZ)
+    rz0, rz1 = both_ways(zs0, zs1, ids, 2)
     at, p, kg, bias = more(parts[2], (at0, p0, at1, p1), kg, bias, zs0, "interior2")
 
     table = jnp.asarray(piece_table(blocks, listed))
-    mine, other, p = pl.pallas_call(
+    mine, other, pws = pl.pallas_call(
         functools.partial(halo_kernel, scale),
-        out_shape=(vm((PAY // 2, LANES)), vm((PAY // 2, LANES)), vm((rows, LANES))),
-        in_specs=[SM] * 4 + [VM] * 12,
+        out_shape=(vm((PAY // 2, LANES)), vm((PAY // 2, LANES)), vm((6 * blocks, 64, 1152), BF16)),
+        in_specs=[SM] * 4 + [VM] * 10,
         out_specs=(VM,) * 3,
         scratch_shapes=[
             pltpu.VMEM((lay["total"], LANES), F32),
             pltpu.VMEM((10, 24, LANES), F32),
-            pltpu.VMEM((64, 1152), BF16),
             pltpu.VMEM((PAY, LANES), F32),
             pltpu.VMEM((384, 1152), F32),
         ],
         name="halo", compiler_params=ROOM,
     )(owner_dir, owner_slot, table, core, local(gd), local(rx0), local(rx1), local(ry0), local(ry1),
-      local(rz0), local(rz1), local(at), local(rt), local(bias), local(p), local(kg))
-
-    swap = [(0, 1), (1, 0)]
-    arrived = lax.ppermute(other, "core", swap)
-    input_grad = pl.pallas_call(
-        finish_kernel, out_shape=sds((blocks, channels, VOL)), in_specs=[VM] * 2, out_specs=VM, name="finish", compiler_params=ROOM,
-    )(local(p), active)
-    half = mine + arrived
-    plane, depth = lax.axis_size(("x", "gy")), lax.axis_size(("zh", "zl"))
+      local(rz0), local(rz1), local(at), local(bias), local(kg))
+
+    swap = [(i, i ^ 1) for i in range(devices)]
+    arrived = lax.ppermute(other, AX, swap)
+    p = pl.pallas_call(
+        edges_kernel, out_shape=vm((rows, LANES)), in_specs=[SM] + [VM] * 3, out_specs=VM,
+        name="edges", compiler_params=ROOM,
+    )(owner_dir, local(pws), local(rt), local(p))
+    half = pl.pallas_call(
+        join_kernel, out_shape=vm((PAY // 2, LANES)), in_specs=[VM, VM, ANY], out_specs=VM,
+        name="join", compiler_params=ROOM,
+    )(local(mine), local(arrived), p)
+    over, along = sum_groups(ids.reshape(2, grid[0] // 2, grid[1], grid[2] // 2, 2))
+    plane, depth = len(over[0]), len(along[0])
     chunk = PAY // 2 // plane // 2
 
-    def trade(x, count, axes):
-        x = lax.all_to_all(x.reshape(count * chunk, 2, LANES), axes, 0, 0, tiled=True)
-        return x.reshape(count, chunk, 2, LANES)
+    def trade(x, groups):
+        x = x.reshape(len(groups[0]) * chunk, 2, LANES)
+        x = lax.all_to_all(x, AX, 0, 0, tiled=True, axis_index_groups=groups)
+        return x.reshape(len(groups[0]), chunk, 2, LANES)
 
     def copies(x, count):
         return jnp.broadcast_to(x[None], (count,) + x.shape)
 
-    share = jnp.sum(trade(half, plane, ("x", "gy")), axis=0)
-    share = jnp.sum(trade(copies(share, depth), depth, ("zh", "zl")), axis=0)
-    whole = trade(copies(share, plane), plane, ("x", "gy"))
+    share = jnp.sum(trade(half, over), axis=0)
+    share = jnp.sum(trade(copies(share, depth), along), axis=0)
+    whole = trade(copies(share, plane), over)
     whole = whole.reshape(PAY // 2, LANES)
-    rest = lax.ppermute(whole, "core", swap)
+    rest = lax.ppermute(whole, AX, swap)
+    input_grad = pl.pallas_call(
+        finish_kernel, out_shape=sds((blocks, channels, VOL)), in_specs=[VM] * 2, out_specs=VM,
+        name="finish", compiler_params=ROOM,
+    )(local(p), active)
 
     kernel_grad, bias_grad = pl.pallas_call(
         unpack_kernel,
@@ -570,8 +622,8 @@
 
 
 def solution(mesh):
-    shape = mesh.devices.shape
-    fine = Mesh(mesh.devices.reshape(2, shape[0] // 2, shape[1], shape[2] // 2, 2), AX)
+    grid = mesh.devices.shape
+    flat = Mesh(mesh.devices.reshape(-1), (AX,))
     placed = (
         P(AX, None, None),
         P(AX, None, None),
@@ -583,8 +635,8 @@
         P(AX),
     )
     return jax.shard_map(
-        shards,
-        mesh=fine,
+        functools.partial(shards, grid),
+        mesh=flat,
         in_specs=placed,
         out_specs=(P(AX, None, None), P(), P()),
         check_vma=False,

time: 107 us -> 107 us (level)
  blocking collectives: 59.3 us -> 57.5 us
    all_to_all x3, blocking collectives: 59.3 us -> 57.5 us  [trade(): x = lax.all_to_all(x, AX, 0, 0, tiled=True, axis_index_groups=groups)]
    pallas_call x0 -> x2, Pallas kernels: none -> 1.25 us  [the longest x1 1.21 us: shards(): pl.pallas_call(edges_kernel, out_shape=vm((rows, LANES)), in_specs=[SM] +...]
  transfers between devices with their start and end apart: 8 -> 8, of which waited for: 1 -> 2; matrix products, arithmetic and copies ran while one was open for 0% -> 0% of each run, Pallas kernels for 10% -> 11%
where the time goes in v4:
time: 107 us; the launch traced here: 106 us
  blocking collectives  57.5 us (54%)
  starting transfers between devices  28.1 us (26%)
  Pallas kernels  17.2 us (16%)
  waiting for transfers between devices  1.43 us (1%)
    all_to_all x3, blocking collectives, trade(): x = lax.all_to_all(x, AX, 0, 0, tiled=True, axis_index_groups=groups)  57.5 us
    ppermute x3, starting transfers between devices, both_ways(): up = lax.ppermute(high, AX, steps)  14.4 us
    ppermute x1, starting transfers between devices, shards(): rest = lax.ppermute(whole, AX, swap)  7.3 us
    pallas_call x2, Pallas kernels, more(): pl.pallas_call(functools.partial(next_kernel, part, len(earlier) // 2), i...  6.42 us
    ppermute x3, starting transfers between devices, both_ways(): down = lax.ppermute(low, AX, [(b, a) for a, b in steps])  4.5 us
    pallas_call x1, Pallas kernels, shards(): pl.pallas_call(functools.partial(first_kernel, parts[0]), in_specs=[VM, A...  2.96 us
  transfers between devices with their start and end apart: 8, of which 2 were waited for; matrix products, arithmetic and copies ran while one was open for 0% of the time, Pallas kernels for 11%

profile of v4, /device:TPU:1, one launch (start us, length us, event | category | flops | bytes accessed | tf_op | source)
XLA Modules:
  0.0 106.0 jit_solution(1952454278967435583)
XLA Ops:
  0.6 1.9 %prep.1 = (f32[2048,128]{1,0:T(8,128)S(1)}, f32[96,128]{1,0:T(8,128)S(1)}, f32[96,128]{1,0:T(8,128)S(1)}, f32[2,192,128]{2,1,0:T(8,128)S(1)}, f32[2,192,128]{2,1,0:T(8,128)S(1)}) custom-call(s32[1]{0:T(128)} %bitcast.core, s32[3]{0:T(128)} %send_h.1, f32[4,64,512]{2,1,0:T(8,128)} %cot_h.1, f32[4,64,512]{2,1,0:T(8,128)} %pre_h.1, s32[4,512]{1,0:T(4,128)} %act.3), custom_call_target="tpu_custom_call" | custom-call | tf_op jit(solution)/shard_map/prep/pallas_call | solution.py:497
  2.5 3.9 %collective-permute-start = (f32[96,128]{1,0:T(8,128)S(1)}, f32[96,128]{1,0:T(8,128)S(1)}, u32[]{:S(2)}, u32[]{:S(2)}) collective-permute-start(f32[96,128]{1,0:T(8,128)S(1)} %get-tuple-element.31), channel_id=1, source_target_pairs={{0,64},{64,128},{128,192},{192,256},{256,320},{320,384},{384,448},... | collective-permute-start | bytes 147464 | tf_op jit(solution)/shard_map/ppermute | solution.py:455
  6.5 1.3 %collective-permute-start.1 = (f32[96,128]{1,0:T(8,128)S(1)}, f32[96,128]{1,0:T(8,128)S(1)}, u32[]{:S(2)}, u32[]{:S(2)}) collective-permute-start(f32[96,128]{1,0:T(8,128)S(1)} %get-tuple-element.32), channel_id=1, source_target_pairs={{64,0},{128,64},{192,128},{256,192},{320,256},{384,320},{448,384},... | collective-permute-start | bytes 147464 | tf_op jit(solution)/shard_map/ppermute | solution.py:456
  7.8 0.7 copy-done
  8.5 3.0 %interior0.1 = (f32[512,128]{1,0:T(8,128)S(1)}, f32[512,128]{1,0:T(8,128)S(1)}, f32[384,1152]{1,0:T(8,128)S(1)}, bf16[384,1152]{1,0:T(8,128)(2,1)S(1)}, f32[8,128]{1,0:T(8,128)S(1)}) custom-call(f32[2048,128]{1,0:T(8,128)S(1)} %get-tuple-element.30.gd.refs_0_, f32[4,64,512]{2,1,0:T(8,128)} %refs_1_.3, s32[4,512]{1,0:T(4,128)S(1)} %copy-done, ...), custom_call_target="tpu_custom_call" | custom-call | tf_op jit(solution)/shard_map/interior0/pallas_call | solution.py:528
  11.5 3.2 %collective-permute-start.2 = (f32[120,128]{1,0:T(8,128)S(1)}, f32[120,128]{1,0:T(8,128)S(1)}, u32[]{:S(2)}, u32[]{:S(2)}) collective-permute-start(f32[120,128]{1,0:T(8,128)S(1)} %get-tuple-element.35), channel_id=1, source_target_pairs={{0,8},{8,16},{16,24},{24,32},{32,40},{40,48},{48,56},{1,9},{9,17},... | collective-permute-start | bytes 184328 | tf_op jit(solution)/shard_map/ppermute | solution.py:455
  14.8 1.3 %collective-permute-start.3 = (f32[120,128]{1,0:T(8,128)S(1)}, f32[120,128]{1,0:T(8,128)S(1)}, u32[]{:S(2)}, u32[]{:S(2)}) collective-permute-start(f32[120,128]{1,0:T(8,128)S(1)} %get-tuple-element.36.refs_6_), channel_id=1, source_target_pairs={{8,0},{16,8},{24,16},{32,24},{40,32},{48,40},{56,48},{9,1},{17,9},... | collective-permute-start | bytes 184328 | tf_op jit(solution)/shard_map/ppermute | solution.py:456
  16.1 2.5 %interior1.1 = (f32[512,128]{1,0:T(8,128)S(1)}, f32[512,128]{1,0:T(8,128)S(1)}, f32[384,1152]{1,0:T(8,128)S(1)}, f32[8,128]{1,0:T(8,128)S(1)}) custom-call(f32[2048,128]{1,0:T(8,128)S(1)} %get-tuple-element.30.gd.refs_0_, f32[4,64,512]{2,1,0:T(8,128)} %refs_1_.3, s32[4,512]{1,0:T(4,128)S(1)} %copy-done.1, ...), custom_call_target="tpu_custom_call" | custom-call | tf_op jit(solution)/shard_map/interior1/pallas_call | solution.py:539
  18.5 1.2 %collective-permute-done.3.ry1 = f32[120,128]{1,0:T(8,128)S(1)} collective-permute-done((f32[120,128]{1,0:T(8,128)S(1)}, f32[120,128]{1,0:T(8,128)S(1)}, u32[]{:S(2)}, u32[]{:S(2)}) %collective-permute-start.3) | collective-permute-done | bytes 61472 | tf_op jit(solution)/shard_map/ppermute | solution.py:456
  19.7 0.2 pack_z.1
  19.9 7.3 %collective-permute-start.4 = (f32[160,128]{1,0:T(8,128)S(1)}, f32[160,128]{1,0:T(8,128)S(1)}, u32[]{:S(2)}, u32[]{:S(2)}) collective-permute-start(f32[160,128]{1,0:T(8,128)S(1)} %get-tuple-element.41), channel_id=1, source_target_pairs={{0,1},{1,2},{2,3},{3,4},{4,5},{5,6},{6,7},{8,9},{9,10},{10,11},{11... | collective-permute-start | bytes 245768 | tf_op jit(solution)/shard_map/ppermute | solution.py:455
  27.2 1.9 %collective-permute-start.5 = (f32[160,128]{1,0:T(8,128)S(1)}, f32[160,128]{1,0:T(8,128)S(1)}, u32[]{:S(2)}, u32[]{:S(2)}) collective-permute-start(f32[160,128]{1,0:T(8,128)S(1)} %get-tuple-element.42.refs_10_), channel_id=1, source_target_pairs={{1,0},{2,1},{3,2},{4,3},{5,4},{6,5},{7,6},{9,8},{10,9},{11,10},{12... | collective-permute-start | bytes 245768 | tf_op jit(solution)/shard_map/ppermute | solution.py:456
  29.1 4.0 %interior2.1 = (f32[2048,128]{1,0:T(8,128)S(1)}, f32[2048,128]{1,0:T(8,128)S(1)}, f32[384,1152]{1,0:T(8,128)S(1)}, f32[8,128]{1,0:T(8,128)S(1)}) custom-call(f32[2048,128]{1,0:T(8,128)S(1)} %get-tuple-element.30.gd.refs_0_, f32[4,64,512]{2,1,0:T(8,128)} %refs_1_.3, s32[4,512]{1,0:T(4,128)S(1)} %copy-done.1, ...), custom_call_target="tpu_custom_call" | custom-call | tf_op jit(solution)/shard_map/interior2/pallas_call | solution.py:539
  33.1 1.9 %halo.1 = (f32[448,128]{1,0:T(8,128)S(1)}, f32[448,128]{1,0:T(8,128)S(1)}, bf16[24,64,1152]{2,1,0:T(8,128)(2,1)S(1)}) custom-call(s32[4,27]{1,0:T(4,128)S(1)} %copy-done.2, s32[4,27]{1,0:T(4,128)S(1)} %copy-done.4, s32[756]{0:T(1024)S(1)} %copy-done.3, s32[1]{0:T(128)} %bitcast.core, f32[2048,128]{1,0:T(8,128)S(1)} %get-tuple-element.30.gd.refs_0_, ...), custom_call_target="tpu_custom_call" | custom-call | tf_op jit(solution)/shard_map/halo/pallas_call | solution.py:566
  35.1 1.9 %collective-permute-start.6 = (f32[448,128]{1,0:T(8,128)S(1)}, f32[448,128]{1,0:T(8,128)S(1)}, u32[]{:S(2)}, u32[]{:S(2)}) collective-permute-start(f32[448,128]{1,0:T(8,128)S(1)} %get-tuple-element.54), channel_id=1, source_target_pairs={{0,1},{1,0},{2,3},{3,2},{4,5},{5,4},{6,7},{7,6},{8,9},{9,8},{10,11... | collective-permute-start | bytes 688136 | tf_op jit(solution)/shard_map/ppermute | solution.py:582
  37.0 1.2 %edges.1.pa.after = f32[2048,128]{1,0:T(8,128)S(1)} custom-call(s32[4,27]{1,0:T(4,128)S(1)} %copy-done.2, bf16[24,64,1152]{2,1,0:T(8,128)(2,1)S(1)} %get-tuple-element.51.pws, bf16[384,1152]{1,0:T(8,128)(2,1)S(1)} %get-tuple-element.38.refs_3_.rt, f32[2048,128]{1,0:T(8,128)S(1)} %get-tuple-element.52.p), custom_call_target="tpu_custom_call" | custom-call | tf_op jit(solution)/shard_map/edges/pallas_call | solution.py:583
  38.2 0.2 collective-permute-done.6.arrived
  38.5 29.2 %all_to_all.15 = f32[224,2,128]{2,1,0:T(2,128)S(1)} all-to-all(f32[224,2,128]{2,1,0:T(2,128)S(1)} %bitcast.10), channel_id=1, replica_groups={{0,8,16,24,32,40,48,56,64,72,80,88,96,104,112,120,128,136,144,152,160,1..., dimensions={0} | all-to-all | bytes 458752 | tf_op jit(solution)/shard_map/all_to_all | solution.py:597
  67.7 0.1 reduce_sum.18
  67.8 14.5 %all_to_all.16 = f32[56,2,128]{2,1,0:T(2,128)S(1)} all-to-all(f32[56,2,128]{2,1,0:T(2,128)S(1)} %bitcast.14), channel_id=1, replica_groups={{0,2,4,6,256,258,260,262},{8,10,12,14,264,266,268,270},{16,18,20,22,272..., dimensions={0} | all-to-all | bytes 114688 | tf_op jit(solution)/shard_map/all_to_all | solution.py:597
  82.4 13.8 %all_to_all.17 = f32[224,2,128]{2,1,0:T(2,128)S(1)} all-to-all(f32[224,2,128]{2,1,0:T(2,128)S(1)} %bitcast.12), channel_id=1, replica_groups={{0,8,16,24,32,40,48,56,64,72,80,88,96,104,112,120,128,136,144,152,160,1..., dimensions={0} | all-to-all | bytes 458752 | tf_op jit(solution)/shard_map/all_to_all | solution.py:597
  96.2 7.3 %collective-permute-start.7 = (f32[448,128]{1,0:T(8,128)S(1)}, f32[448,128]{1,0:T(8,128)S(1)}, u32[]{:S(2)}, u32[]{:S(2)}) collective-permute-start(f32[448,128]{1,0:T(8,128)S(1)} %bitcast.8), channel_id=1, source_target_pairs={{0,1},{1,0},{2,3},{3,2},{4,5},{5,4},{6,7},{7,6},{8,9},{9,8},{10,11... | collective-permute-start | bytes 688136 | tf_op jit(solution)/shard_map/ppermute | solution.py:607
  103.5 1.4 %finish.1 = f32[4,64,512]{2,1,0:T(8,128)} custom-call(f32[2048,128]{1,0:T(8,128)S(1)} %edges.1.pa.after, s32[4,512]{1,0:T(4,128)S(1)} %copy-done.1), custom_call_target="tpu_custom_call" | custom-call | tf_op jit(solution)/shard_map/finish/pallas_call | solution.py:608
  104.9 1.1 %unpack.1 = (f32[27,64,64]{2,1,0:T(8,128)}, f32[1,64]{1,0:T(1,128)}) custom-call(s32[1]{0:T(128)} %bitcast.core, f32[448,128]{1,0:T(8,128)S(1)} %bitcast.9, f32[448,128]{1,0:T(8,128)S(1)} %collective-permute-done.7.other), custom_call_target="tpu_custom_call" | custom-call | tf_op jit(solution)/shard_map/unpack/pallas_call | solution.py:613
  (20 shorter events, 0.3 us)
Async XLA Ops:
  0.6 15.4 %copy-start.1 = (s32[4,512]{1,0:T(4,128)S(1)}, s32[4,512]{1,0:T(4,128)}, u32[]{:S(2)}) copy-start(s32[4,512]{1,0:T(4,128)} %act.3) | copy-start | bytes 24580
  2.5 8.9 %collective-permute-start = (f32[96,128]{1,0:T(8,128)S(1)}, f32[96,128]{1,0:T(8,128)S(1)}, u32[]{:S(2)}, u32[]{:S(2)}) collective-permute-start(f32[96,128]{1,0:T(8,128)S(1)} %get-tuple-element.31), channel_id=1, source_target_pairs={{0,64},{64,128},{128,192},{192,256},{256,320},{320,384},{384,448},... | collective-permute-start | bytes 147464 | tf_op jit(solution)/shard_map/ppermute | solution.py:455
  6.5 5.0 %collective-permute-start.1 = (f32[96,128]{1,0:T(8,128)S(1)}, f32[96,128]{1,0:T(8,128)S(1)}, u32[]{:S(2)}, u32[]{:S(2)}) collective-permute-start(f32[96,128]{1,0:T(8,128)S(1)} %get-tuple-element.32), channel_id=1, source_target_pairs={{64,0},{128,64},{192,128},{256,192},{320,256},{384,320},{448,384},... | collective-permute-start | bytes 147464 | tf_op jit(solution)/shard_map/ppermute | solution.py:456
  7.8 0.7 copy-start
  11.5 7.0 %collective-permute-start.2 = (f32[120,128]{1,0:T(8,128)S(1)}, f32[120,128]{1,0:T(8,128)S(1)}, u32[]{:S(2)}, u32[]{:S(2)}) collective-permute-start(f32[120,128]{1,0:T(8,128)S(1)} %get-tuple-element.35), channel_id=1, source_target_pairs={{0,8},{8,16},{16,24},{24,32},{32,40},{40,48},{48,56},{1,9},{9,17},... | collective-permute-start | bytes 184328 | tf_op jit(solution)/shard_map/ppermute | solution.py:455
  14.8 5.0 %collective-permute-start.3 = (f32[120,128]{1,0:T(8,128)S(1)}, f32[120,128]{1,0:T(8,128)S(1)}, u32[]{:S(2)}, u32[]{:S(2)}) collective-permute-start(f32[120,128]{1,0:T(8,128)S(1)} %get-tuple-element.36.refs_6_), channel_id=1, source_target_pairs={{8,0},{16,8},{24,16},{32,24},{40,32},{48,40},{56,48},{9,1},{17,9},... | collective-permute-start | bytes 184328 | tf_op jit(solution)/shard_map/ppermute | solution.py:456
  19.9 13.2 %collective-permute-start.4 = (f32[160,128]{1,0:T(8,128)S(1)}, f32[160,128]{1,0:T(8,128)S(1)}, u32[]{:S(2)}, u32[]{:S(2)}) collective-permute-start(f32[160,128]{1,0:T(8,128)S(1)} %get-tuple-element.41), channel_id=1, source_target_pairs={{0,1},{1,2},{2,3},{3,4},{4,5},{5,6},{6,7},{8,9},{9,10},{10,11},{11... | collective-permute-start | bytes 245768 | tf_op jit(solution)/shard_map/ppermute | solution.py:455
  27.2 5.9 %collective-permute-start.5 = (f32[160,128]{1,0:T(8,128)S(1)}, f32[160,128]{1,0:T(8,128)S(1)}, u32[]{:S(2)}, u32[]{:S(2)}) collective-permute-start(f32[160,128]{1,0:T(8,128)S(1)} %get-tuple-element.42.refs_10_), channel_id=1, source_target_pairs={{1,0},{2,1},{3,2},{4,3},{5,4},{6,5},{7,6},{9,8},{10,9},{11,10},{12... | collective-permute-start | bytes 245768 | tf_op jit(solution)/shard_map/ppermute | solution.py:456
  29.1 4.0 %copy-start.2 = (s32[4,27]{1,0:T(4,128)S(1)}, s32[4,27]{1,0:T(4,128)}, u32[]{:S(2)}) copy-start(s32[4,27]{1,0:T(4,128)} %od.3) | copy-start | bytes 1300
  29.1 4.0 %copy-start.3 = (s32[756]{0:T(1024)S(1)}, s32[756]{0:T(1024)}, u32[]{:S(2)}) copy-start(s32[756]{0:T(1024)} %constant.10.clone.tb) | copy-start | bytes 9076
  29.1 4.0 %copy-start.4 = (s32[4,27]{1,0:T(4,128)S(1)}, s32[4,27]{1,0:T(4,128)}, u32[]{:S(2)}) copy-start(s32[4,27]{1,0:T(4,128)} %os_.1) | copy-start | bytes 1300
  35.1 3.4 %collective-permute-start.6 = (f32[448,128]{1,0:T(8,128)S(1)}, f32[448,128]{1,0:T(8,128)S(1)}, u32[]{:S(2)}, u32[]{:S(2)}) collective-permute-start(f32[448,128]{1,0:T(8,128)S(1)} %get-tuple-element.54), channel_id=1, source_target_pairs={{0,1},{1,0},{2,3},{3,2},{4,5},{5,4},{6,7},{7,6},{8,9},{9,8},{10,11... | collective-permute-start | bytes 688136 | tf_op jit(solution)/shard_map/ppermute | solution.py:582
  96.2 8.7 %collective-permute-start.7 = (f32[448,128]{1,0:T(8,128)S(1)}, f32[448,128]{1,0:T(8,128)S(1)}, u32[]{:S(2)}, u32[]{:S(2)}) collective-permute-start(f32[448,128]{1,0:T(8,128)S(1)} %bitcast.8), channel_id=1, source_target_pairs={{0,1},{1,0},{2,3},{3,2},{4,5},{5,4},{6,7},{7,6},{8,9},{9,8},{10,11... | collective-permute-start | bytes 688136 | tf_op jit(solution)/shard_map/ppermute | solution.py:607

commit v5 on v4

--- a/solution.py
+++ b/solution.py
@@ -248,13 +248,27 @@
         interior_block(b, i * VOL, gd, feat[i], act, at, p, kgi, kg, rt, bi, bias, z)
 
 
+def plane_weights(rt, rtp):
+    for i in range(3):
+        rows = slice(i * 128, (i + 1) * 128)
+        for s, k in enumerate((0, 2)):
+            rtp[s, :, i * 384 : (i + 1) * 384] = rt[rows, k * 384 : (k + 1) * 384]
+            for j in range(3):
+                c = i * 3 + j
+                rtp[2 + s, :, c * 128 : (c + 1) * 128] = rt[rows, (j * 3 + k) * 128 : (j * 3 + k + 1) * 128]
+
+
 def next_kernel(part, held, *refs):
     gd, feat_h, act, rt, kg0, bias0 = refs[:6]
     earlier = refs[6 : 6 + 2 * held]
-    at, p, kg, bias, z, feat, sems = refs[7 + 2 * held :]
+    at, p, kg, bias, rtp, z, feat, sems = refs[7 + 2 * held :]
     copies = fetch(part, feat_h, feat, sems)
     for copy in copies:
         copy.start()
+    if held:
+        rtp[...] = jnp.zeros(rtp.shape, rtp.dtype)
+    else:
+        plane_weights(rt, rtp)
     row = 0
     for i in range(held):
         n = earlier[2 * i].shape[0]
@@ -307,32 +321,25 @@
     lax.fori_loop(0, od.shape[0], block, 0)
 
 
-def edges_kernel(od, pws, rt, p, pa):
+def edges_kernel(od, pws, rt, rtp, p, pa):
     pa[...] = p[...]
 
     def plane(b, axis, sign):
         face = 0 if sign == -1 else 7
-        pw = pws.at[plane_slot(b, axis, sign)]
+        pw = pws[plane_slot(b, axis, sign)]
         r0 = b * VOL
         k = 1 - sign
         if axis == 0:
             rows = pl.ds(pl.multiple_of(r0 + face * 64, 64), 64)
-            pa[rows, :] += nt(pw[...], rt[k * 128 : (k + 1) * 128, :])
+            pa[rows, :] += nt(pw, rt[k * 128 : (k + 1) * 128, :])
         elif axis == 1:
-            acc = jnp.zeros((64, LANES), F32)
-            for i in range(3):
-                acc = acc + nt(pw[:, i * 384 : (i + 1) * 384], rt[i * 128 : (i + 1) * 128, k * 384 : (k + 1) * 384])
+            acc = nt(pw, rtp[k // 2])
             for x in range(8):
                 rows = pl.ds(pl.multiple_of(r0 + x * 64 + face * 8, 8), 8)
                 pa[rows, :] += acc[x * 8 : x * 8 + 8, :]
         else:
-            acc = jnp.zeros((64, LANES), F32)
-            for i in range(3):
-                for j in range(3):
-                    part = pw[:, (i * 3 + j) * 128 : (i * 3 + j + 1) * 128]
-                    acc = acc + nt(part, rt[i * 128 : (i + 1) * 128, (j * 3 + k) * 128 : (j * 3 + k + 1) * 128])
             rows = pl.ds(r0 + face, 64, stride=8)
-            pa[rows, :] = pa[rows, :] + acc
+            pa[rows, :] = pa[rows, :] + nt(pw, rtp[2 + k // 2])
 
     for_planes(od, plane)
 
@@ -350,6 +357,7 @@
         row += 2 * ref.shape[0]
     kg[...] = kg0[...]
     lane64 = lax.broadcasted_iota(jnp.int32, (64, LANES), 1) < 64
+    lane24 = lax.broadcasted_iota(jnp.int32, (10, 24, LANES), 2) < 64
 
     def plane(b, axis, sign):
         face = 0 if sign == -1 else 7
@@ -365,7 +373,16 @@
                 sr = (code >> 16) & 15
                 sq = (code >> 20) & 15
 
-                def fill(ref):
+                def fill(ref, own):
+                    if r == 0 and q == 0:
+                        for i in range(8):
+                            start = base + (i << sr)
+                            if axis == 2 and own:
+                                rows = pl.ds(start, 8, stride=8)
+                            else:
+                                rows = pl.ds(pl.multiple_of(start, 8), 8)
+                            pb[i + 1, 8:16, :] = ref[rows, :]
+                        return
                     for i in range(8 if r == 0 else 1):
                         for j in range(8 if q == 0 else 1):
                             at_r = i + 1 if r == 0 else (0 if r == -1 else 9)
@@ -373,30 +390,37 @@
                             row = base + (i << sr) + (j << sq)
                             pb[at_r, at_q : at_q + 1, :] = ref[pl.ds(row, 1), :]
 
-                pl.when(d == 13)(lambda: fill(gd))
-                pl.when(d != 13)(lambda: fill(src))
-
+                pl.when(d == 13)(lambda: fill(gd, True))
+                pl.when(d != 13)(lambda: fill(src, False))
+
+        pb[...] = split_hl(pb[...], lane24)
         for kr in (-1, 0, 1):
             for kq in (-1, 0, 1):
                 win = pb[1 - kr : 9 - kr, 8 - kq : 16 - kq, :].reshape(64, LANES)
                 c = (kr + 1) * 3 + kq + 1
-                pw[:, c * 128 : (c + 1) * 128] = split_hl(win, lane64).astype(BF16)
+                pw[:, c * 128 : (c + 1) * 128] = win.astype(BF16)
         r0 = b * VOL
         k = 1 - sign
         if axis == 0:
-            ap = at[pl.ds(pl.multiple_of(r0 + face * 64, 64), 64), :].astype(BF16)
-            kg[k * 128 : (k + 1) * 128, :] += tn(ap, pw[...])
+            ap = at[pl.ds(pl.multiple_of(r0 + face * 64, 64), 64), :]
         elif axis == 1:
             starts = [pl.multiple_of(r0 + x * 64 + face * 8, 8) for x in range(8)]
-            ap = jnp.concatenate([at[pl.ds(s, 8), :] for s in starts], axis=0).astype(BF16)
+            ap = jnp.concatenate([at[pl.ds(s, 8), :] for s in starts], axis=0)
+        else:
+            ap = at[pl.ds(r0 + face, 64, stride=8), :]
+        term = tn(ap.astype(BF16), pw[...])
+        if axis == 0:
+            kg[k * 128 : (k + 1) * 128, :] += term
+        elif axis == 1:
             for i in range(3):
-                kg[i * 128 : (i + 1) * 128, k * 384 : (k + 1) * 384] += tn(ap, pw[:, i * 384 : (i + 1) * 384])
+                kg[i * 128 : (i + 1) * 128, k * 384 : (k + 1) * 384] += term[:, i * 384 : (i + 1) * 384]
         else:
-            ap = at[pl.ds(r0 + face, 64, stride=8), :].astype(BF16)
             for i in range(3):
                 for j in range(3):
-                    part = pw[:, (i * 3 + j) * 128 : (i * 3 + j + 1) * 128]
-                    kg[i * 128 : (i + 1) * 128, (j * 3 + k) * 128 : (j * 3 + k + 1) * 128] += tn(ap, part)
+                    c = i * 3 + j
+                    kg[i * 128 : (i + 1) * 128, (j * 3 + k) * 128 : (j * 3 + k + 1) * 128] += (
+                        term[:, c * 128 : (c + 1) * 128]
+                    )
 
     for_planes(od, plane)
 
@@ -539,8 +563,9 @@
         return pl.pallas_call(
             functools.partial(next_kernel, part, len(earlier) // 2),
             in_specs=[VM, ANY] + [VM] * (4 + len(earlier)) + [ANY],
-            out_specs=(VM,) * 4,
-            out_shape=(vm((n, LANES)), vm((n, LANES)), vm(wide), vm((8, LANES))),
+            out_specs=(VM,) * 5,
+            out_shape=(vm((n, LANES)), vm((n, LANES)), vm(wide), vm((8, LANES)),
+                       vm((16, LANES) if earlier else (4, 128, 1152), BF16)),
             scratch_shapes=scratch(part),
             name=name, compiler_params=ROOM,
         )(local(gd), far(features), active, local(rt), local(kg), local(bias), *[local(e) for e in earlier], after)
@@ -552,7 +577,7 @@
         name="pack_y", compiler_params=ROOM,
     )(local(ys), local(rx0), local(rx1), bias)
     ry0, ry1 = both_ways(ys0, ys1, ids, 1)
-    at1, p1, kg, bias = more(parts[1], (), kg, bias, ys0, "interior1")
+    at1, p1, kg, bias, rtp = more(parts[1], (), kg, bias, ys0, "interior1")
     zs0, zs1 = pl.pallas_call(
         pack_z_kernel, out_shape=(vm((zr // 2, LANES)),) * 2,
         scratch_shapes=[pltpu.VMEM((n, LANES), F32) for n in (face, face, yr, yr, zr)],
@@ -560,7 +585,7 @@
         name="pack_z", compiler_params=ROOM,
     )(local(zs), local(rx0), local(rx1), local(ry0), local(ry1), bias)
     rz0, rz1 = both_ways(zs0, zs1, ids, 2)
-    at, p, kg, bias = more(parts[2], (at0, p0, at1, p1), kg, bias, zs0, "interior2")
+    at, p, kg, bias, _ = more(parts[2], (at0, p0, at1, p1), kg, bias, zs0, "interior2")
 
     table = jnp.asarray(piece_table(blocks, listed))
     mine, other, pws = pl.pallas_call(
@@ -581,9 +606,9 @@
     swap = [(i, i ^ 1) for i in range(devices)]
     arrived = lax.ppermute(other, AX, swap)
     p = pl.pallas_call(
-        edges_kernel, out_shape=vm((rows, LANES)), in_specs=[SM] + [VM] * 3, out_specs=VM,
+        edges_kernel, out_shape=vm((rows, LANES)), in_specs=[SM] + [VM] * 4, out_specs=VM,
         name="edges", compiler_params=ROOM,
-    )(owner_dir, local(pws), local(rt), local(p))
+    )(owner_dir, local(pws), local(rt), local(rtp), local(p))
     half = pl.pallas_call(
         join_kernel, out_shape=vm((PAY // 2, LANES)), in_specs=[VM, VM, ANY], out_specs=VM,
         name="join", compiler_params=ROOM,

time: 107 us -> 105 us (0.981)
  transfers between devices with their start and end apart: 8 -> 8, of which waited for: 2 -> 2; matrix products, arithmetic and copies ran while one was open for 0% -> 0% of each run, Pallas kernels for 11% -> 12%
where the time goes in v5:
time: 105 us
  blocking collectives  56.7 us (54%)
  starting transfers between devices  27.5 us (26%)
  Pallas kernels  17.5 us (17%)
  waiting for transfers between devices  1.3 us (1%)
    all_to_all x3, blocking collectives, trade(): x = lax.all_to_all(x, AX, 0, 0, tiled=True, axis_index_groups=groups)  56.7 us
    ppermute x3, starting transfers between devices, both_ways(): up = lax.ppermute(high, AX, steps)  14.4 us
    ppermute x1, starting transfers between devices, shards(): rest = lax.ppermute(whole, AX, swap)  6.71 us
    pallas_call x2, Pallas kernels, more(): pl.pallas_call(functools.partial(next_kernel, part, len(earlier) // 2), i...  6.45 us
    ppermute x3, starting transfers between devices, both_ways(): down = lax.ppermute(low, AX, [(b, a) for a, b in steps])  4.5 us
    pallas_call x1, Pallas kernels, shards(): pl.pallas_call(functools.partial(first_kernel, parts[0]), in_specs=[VM, A...  2.96 us
    pallas_call x1, Pallas kernels, shards(): pl.pallas_call(functools.partial(halo_kernel, scale), out_shape=(vm((PAY...  2.11 us
  transfers between devices with their start and end apart: 8, of which 2 were waited for; matrix products, arithmetic and copies ran while one was open for 0% of the time, Pallas kernels for 12%

profile of v5, /device:TPU:1, one launch (start us, length us, event | category | flops | bytes accessed | tf_op | source)
XLA Modules:
  0.0 104.9 jit_solution(11911182368806265686)
XLA Ops:
  0.6 1.9 %prep.1 = (f32[2048,128]{1,0:T(8,128)S(1)}, f32[96,128]{1,0:T(8,128)S(1)}, f32[96,128]{1,0:T(8,128)S(1)}, f32[2,192,128]{2,1,0:T(8,128)S(1)}, f32[2,192,128]{2,1,0:T(8,128)S(1)}) custom-call(s32[1]{0:T(128)} %bitcast.core, s32[3]{0:T(128)} %send_h.1, f32[4,64,512]{2,1,0:T(8,128)} %cot_h.1, f32[4,64,512]{2,1,0:T(8,128)} %pre_h.1, s32[4,512]{1,0:T(4,128)} %act.3), custom_call_target="tpu_custom_call" | custom-call | tf_op jit(solution)/shard_map/prep/pallas_call | solution.py:521
  2.5 3.9 %collective-permute-start = (f32[96,128]{1,0:T(8,128)S(1)}, f32[96,128]{1,0:T(8,128)S(1)}, u32[]{:S(2)}, u32[]{:S(2)}) collective-permute-start(f32[96,128]{1,0:T(8,128)S(1)} %get-tuple-element.32), channel_id=1, source_target_pairs={{0,64},{64,128},{128,192},{192,256},{256,320},{320,384},{384,448},... | collective-permute-start | bytes 147464 | tf_op jit(solution)/shard_map/ppermute | solution.py:479
  6.5 1.3 %collective-permute-start.1 = (f32[96,128]{1,0:T(8,128)S(1)}, f32[96,128]{1,0:T(8,128)S(1)}, u32[]{:S(2)}, u32[]{:S(2)}) collective-permute-start(f32[96,128]{1,0:T(8,128)S(1)} %get-tuple-element.33), channel_id=1, source_target_pairs={{64,0},{128,64},{192,128},{256,192},{320,256},{384,320},{448,384},... | collective-permute-start | bytes 147464 | tf_op jit(solution)/shard_map/ppermute | solution.py:480
  7.8 0.7 copy-done
  8.5 3.0 %interior0.1 = (f32[512,128]{1,0:T(8,128)S(1)}, f32[512,128]{1,0:T(8,128)S(1)}, f32[384,1152]{1,0:T(8,128)S(1)}, bf16[384,1152]{1,0:T(8,128)(2,1)S(1)}, f32[8,128]{1,0:T(8,128)S(1)}) custom-call(f32[2048,128]{1,0:T(8,128)S(1)} %get-tuple-element.31.gd.refs_0_, f32[4,64,512]{2,1,0:T(8,128)} %refs_1_.3, s32[4,512]{1,0:T(4,128)S(1)} %copy-done, ...), custom_call_target="tpu_custom_call" | custom-call | tf_op jit(solution)/shard_map/interior0/pallas_call | solution.py:552
  11.5 3.2 %collective-permute-start.2 = (f32[120,128]{1,0:T(8,128)S(1)}, f32[120,128]{1,0:T(8,128)S(1)}, u32[]{:S(2)}, u32[]{:S(2)}) collective-permute-start(f32[120,128]{1,0:T(8,128)S(1)} %get-tuple-element.36), channel_id=1, source_target_pairs={{0,8},{8,16},{16,24},{24,32},{32,40},{40,48},{48,56},{1,9},{9,17},... | collective-permute-start | bytes 184328 | tf_op jit(solution)/shard_map/ppermute | solution.py:479
  14.8 1.3 %collective-permute-start.3 = (f32[120,128]{1,0:T(8,128)S(1)}, f32[120,128]{1,0:T(8,128)S(1)}, u32[]{:S(2)}, u32[]{:S(2)}) collective-permute-start(f32[120,128]{1,0:T(8,128)S(1)} %get-tuple-element.37.refs_6_), channel_id=1, source_target_pairs={{8,0},{16,8},{24,16},{32,24},{40,32},{48,40},{56,48},{9,1},{17,9},... | collective-permute-start | bytes 184328 | tf_op jit(solution)/shard_map/ppermute | solution.py:480
  16.1 2.5 %interior1.1 = (f32[512,128]{1,0:T(8,128)S(1)}, f32[512,128]{1,0:T(8,128)S(1)}, f32[384,1152]{1,0:T(8,128)S(1)}, f32[8,128]{1,0:T(8,128)S(1)}, bf16[4,128,1152]{2,1,0:T(8,128)(2,1)S(1)}) custom-call(f32[2048,128]{1,0:T(8,128)S(1)} %get-tuple-element.31.gd.refs_0_, f32[4,64,512]{2,1,0:T(8,128)} %refs_1_.3, s32[4,512]{1,0:T(4,128)S(1)} %copy-done.1, ...), custom_call_target="tpu_custom_call" | custom-call | tf_op jit(solution)/shard_map/interior1/pallas_call | solution.py:563
  18.5 1.2 %collective-permute-done.3.ry1 = f32[120,128]{1,0:T(8,128)S(1)} collective-permute-done((f32[120,128]{1,0:T(8,128)S(1)}, f32[120,128]{1,0:T(8,128)S(1)}, u32[]{:S(2)}, u32[]{:S(2)}) %collective-permute-start.3) | collective-permute-done | bytes 61472 | tf_op jit(solution)/shard_map/ppermute | solution.py:480
  19.7 0.2 pack_z.1
  19.9 7.3 %collective-permute-start.4 = (f32[160,128]{1,0:T(8,128)S(1)}, f32[160,128]{1,0:T(8,128)S(1)}, u32[]{:S(2)}, u32[]{:S(2)}) collective-permute-start(f32[160,128]{1,0:T(8,128)S(1)} %get-tuple-element.42), channel_id=1, source_target_pairs={{0,1},{1,2},{2,3},{3,4},{4,5},{5,6},{6,7},{8,9},{9,10},{10,11},{11... | collective-permute-start | bytes 245768 | tf_op jit(solution)/shard_map/ppermute | solution.py:479
  27.2 1.9 %collective-permute-start.5 = (f32[160,128]{1,0:T(8,128)S(1)}, f32[160,128]{1,0:T(8,128)S(1)}, u32[]{:S(2)}, u32[]{:S(2)}) collective-permute-start(f32[160,128]{1,0:T(8,128)S(1)} %get-tuple-element.43.refs_10_), channel_id=1, source_target_pairs={{1,0},{2,1},{3,2},{4,3},{5,4},{6,5},{7,6},{9,8},{10,9},{11,10},{12... | collective-permute-start | bytes 245768 | tf_op jit(solution)/shard_map/ppermute | solution.py:480
  29.1 4.0 %interior2.1 = (f32[2048,128]{1,0:T(8,128)S(1)}, f32[2048,128]{1,0:T(8,128)S(1)}, f32[384,1152]{1,0:T(8,128)S(1)}, f32[8,128]{1,0:T(8,128)S(1)}, bf16[16,128]{1,0:T(8,128)(2,1)}) custom-call(f32[2048,128]{1,0:T(8,128)S(1)} %get-tuple-element.31.gd.refs_0_, f32[4,64,512]{2,1,0:T(8,128)} %refs_1_.3, s32[4,512]{1,0:T(4,128)S(1)} %copy-done.1, ...), custom_call_target="tpu_custom_call" | custom-call | tf_op jit(solution)/shard_map/interior2/pallas_call | solution.py:563
  33.2 2.1 %halo.1 = (f32[448,128]{1,0:T(8,128)S(1)}, f32[448,128]{1,0:T(8,128)S(1)}, bf16[24,64,1152]{2,1,0:T(8,128)(2,1)S(1)}) custom-call(s32[4,27]{1,0:T(4,128)S(1)} %copy-done.2, s32[4,27]{1,0:T(4,128)S(1)} %copy-done.4, s32[756]{0:T(1024)S(1)} %copy-done.3, s32[1]{0:T(128)} %bitcast.core, f32[2048,128]{1,0:T(8,128)S(1)} %get-tuple-element.31.gd.refs_0_, ...), custom_call_target="tpu_custom_call" | custom-call | tf_op jit(solution)/shard_map/halo/pallas_call | solution.py:591
  35.3 1.9 %collective-permute-start.6 = (f32[448,128]{1,0:T(8,128)S(1)}, f32[448,128]{1,0:T(8,128)S(1)}, u32[]{:S(2)}, u32[]{:S(2)}) collective-permute-start(f32[448,128]{1,0:T(8,128)S(1)} %get-tuple-element.56), channel_id=1, source_target_pairs={{0,1},{1,0},{2,3},{3,2},{4,5},{5,4},{6,7},{7,6},{8,9},{9,8},{10,11... | collective-permute-start | bytes 688136 | tf_op jit(solution)/shard_map/ppermute | solution.py:607
  37.2 1.3 %edges.1.pa.after = f32[2048,128]{1,0:T(8,128)S(1)} custom-call(s32[4,27]{1,0:T(4,128)S(1)} %copy-done.2, bf16[24,64,1152]{2,1,0:T(8,128)(2,1)S(1)} %get-tuple-element.52.pws, bf16[384,1152]{1,0:T(8,128)(2,1)S(1)} %get-tuple-element.39.refs_3_.rt, bf16[4,128,1152]{2,1,0:T(8,128)(2,1)S(1)} %get-tuple-element.53.rtp, f32[2048,128]{1,0:T(8,128)S(1)} %get-tuple-element.54.p), custom_call_target="tpu_custom_call" | custom-call | tf_op jit(solution)/shard_map/edges/pallas_call | solution.py:608
  38.6 0.1 collective-permute-done.6.arrived
  38.7 28.8 %all_to_all.15 = f32[224,2,128]{2,1,0:T(2,128)S(1)} all-to-all(f32[224,2,128]{2,1,0:T(2,128)S(1)} %bitcast.10), channel_id=1, replica_groups={{0,8,16,24,32,40,48,56,64,72,80,88,96,104,112,120,128,136,144,152,160,1..., dimensions={0} | all-to-all | bytes 458752 | tf_op jit(solution)/shard_map/all_to_all | solution.py:622
  67.5 0.1 reduce_sum.18
  67.6 14.3 %all_to_all.16 = f32[56,2,128]{2,1,0:T(2,128)S(1)} all-to-all(f32[56,2,128]{2,1,0:T(2,128)S(1)} %bitcast.14), channel_id=1, replica_groups={{0,2,4,6,256,258,260,262},{8,10,12,14,264,266,268,270},{16,18,20,22,272..., dimensions={0} | all-to-all | bytes 114688 | tf_op jit(solution)/shard_map/all_to_all | solution.py:622
  82.0 13.6 %all_to_all.17 = f32[224,2,128]{2,1,0:T(2,128)S(1)} all-to-all(f32[224,2,128]{2,1,0:T(2,128)S(1)} %bitcast.12), channel_id=1, replica_groups={{0,8,16,24,32,40,48,56,64,72,80,88,96,104,112,120,128,136,144,152,160,1..., dimensions={0} | all-to-all | bytes 458752 | tf_op jit(solution)/shard_map/all_to_all | solution.py:622
  95.7 6.7 %collective-permute-start.7 = (f32[448,128]{1,0:T(8,128)S(1)}, f32[448,128]{1,0:T(8,128)S(1)}, u32[]{:S(2)}, u32[]{:S(2)}) collective-permute-start(f32[448,128]{1,0:T(8,128)S(1)} %bitcast.8), channel_id=1, source_target_pairs={{0,1},{1,0},{2,3},{3,2},{4,5},{5,4},{6,7},{7,6},{8,9},{9,8},{10,11... | collective-permute-start | bytes 688136 | tf_op jit(solution)/shard_map/ppermute | solution.py:632
  102.4 1.4 %finish.1 = f32[4,64,512]{2,1,0:T(8,128)} custom-call(f32[2048,128]{1,0:T(8,128)S(1)} %edges.1.pa.after, s32[4,512]{1,0:T(4,128)S(1)} %copy-done.1), custom_call_target="tpu_custom_call" | custom-call | tf_op jit(solution)/shard_map/finish/pallas_call | solution.py:633
  103.8 1.1 %unpack.1 = (f32[27,64,64]{2,1,0:T(8,128)}, f32[1,64]{1,0:T(1,128)}) custom-call(s32[1]{0:T(128)} %bitcast.core, f32[448,128]{1,0:T(8,128)S(1)} %bitcast.9, f32[448,128]{1,0:T(8,128)S(1)} %collective-permute-done.7.other), custom_call_target="tpu_custom_call" | custom-call | tf_op jit(solution)/shard_map/unpack/pallas_call | solution.py:638
  (20 shorter events, 0.3 us)
Async XLA Ops:
  0.6 15.4 %copy-start.1 = (s32[4,512]{1,0:T(4,128)S(1)}, s32[4,512]{1,0:T(4,128)}, u32[]{:S(2)}) copy-start(s32[4,512]{1,0:T(4,128)} %act.3) | copy-start | bytes 24580
  2.5 8.9 %collective-permute-start = (f32[96,128]{1,0:T(8,128)S(1)}, f32[96,128]{1,0:T(8,128)S(1)}, u32[]{:S(2)}, u32[]{:S(2)}) collective-permute-start(f32[96,128]{1,0:T(8,128)S(1)} %get-tuple-element.32), channel_id=1, source_target_pairs={{0,64},{64,128},{128,192},{192,256},{256,320},{320,384},{384,448},... | collective-permute-start | bytes 147464 | tf_op jit(solution)/shard_map/ppermute | solution.py:479
  6.5 5.0 %collective-permute-start.1 = (f32[96,128]{1,0:T(8,128)S(1)}, f32[96,128]{1,0:T(8,128)S(1)}, u32[]{:S(2)}, u32[]{:S(2)}) collective-permute-start(f32[96,128]{1,0:T(8,128)S(1)} %get-tuple-element.33), channel_id=1, source_target_pairs={{64,0},{128,64},{192,128},{256,192},{320,256},{384,320},{448,384},... | collective-permute-start | bytes 147464 | tf_op jit(solution)/shard_map/ppermute | solution.py:480
  7.8 0.7 copy-start
  11.5 7.0 %collective-permute-start.2 = (f32[120,128]{1,0:T(8,128)S(1)}, f32[120,128]{1,0:T(8,128)S(1)}, u32[]{:S(2)}, u32[]{:S(2)}) collective-permute-start(f32[120,128]{1,0:T(8,128)S(1)} %get-tuple-element.36), channel_id=1, source_target_pairs={{0,8},{8,16},{16,24},{24,32},{32,40},{40,48},{48,56},{1,9},{9,17},... | collective-permute-start | bytes 184328 | tf_op jit(solution)/shard_map/ppermute | solution.py:479
  14.8 5.0 %collective-permute-start.3 = (f32[120,128]{1,0:T(8,128)S(1)}, f32[120,128]{1,0:T(8,128)S(1)}, u32[]{:S(2)}, u32[]{:S(2)}) collective-permute-start(f32[120,128]{1,0:T(8,128)S(1)} %get-tuple-element.37.refs_6_), channel_id=1, source_target_pairs={{8,0},{16,8},{24,16},{32,24},{40,32},{48,40},{56,48},{9,1},{17,9},... | collective-permute-start | bytes 184328 | tf_op jit(solution)/shard_map/ppermute | solution.py:480
  19.9 13.2 %collective-permute-start.4 = (f32[160,128]{1,0:T(8,128)S(1)}, f32[160,128]{1,0:T(8,128)S(1)}, u32[]{:S(2)}, u32[]{:S(2)}) collective-permute-start(f32[160,128]{1,0:T(8,128)S(1)} %get-tuple-element.42), channel_id=1, source_target_pairs={{0,1},{1,2},{2,3},{3,4},{4,5},{5,6},{6,7},{8,9},{9,10},{10,11},{11... | collective-permute-start | bytes 245768 | tf_op jit(solution)/shard_map/ppermute | solution.py:479
  27.2 6.0 %collective-permute-start.5 = (f32[160,128]{1,0:T(8,128)S(1)}, f32[160,128]{1,0:T(8,128)S(1)}, u32[]{:S(2)}, u32[]{:S(2)}) collective-permute-start(f32[160,128]{1,0:T(8,128)S(1)} %get-tuple-element.43.refs_10_), channel_id=1, source_target_pairs={{1,0},{2,1},{3,2},{4,3},{5,4},{6,5},{7,6},{9,8},{10,9},{11,10},{12... | collective-permute-start | bytes 245768 | tf_op jit(solution)/shard_map/ppermute | solution.py:480
  29.1 4.1 %copy-start.2 = (s32[4,27]{1,0:T(4,128)S(1)}, s32[4,27]{1,0:T(4,128)}, u32[]{:S(2)}) copy-start(s32[4,27]{1,0:T(4,128)} %od.3) | copy-start | bytes 1300
  29.1 4.1 %copy-start.3 = (s32[756]{0:T(1024)S(1)}, s32[756]{0:T(1024)}, u32[]{:S(2)}) copy-start(s32[756]{0:T(1024)} %constant.10.clone.tb) | copy-start | bytes 9076
  29.1 4.1 %copy-start.4 = (s32[4,27]{1,0:T(4,128)S(1)}, s32[4,27]{1,0:T(4,128)}, u32[]{:S(2)}) copy-start(s32[4,27]{1,0:T(4,128)} %os_.1) | copy-start | bytes 1300
  35.3 3.4 %collective-permute-start.6 = (f32[448,128]{1,0:T(8,128)S(1)}, f32[448,128]{1,0:T(8,128)S(1)}, u32[]{:S(2)}, u32[]{:S(2)}) collective-permute-start(f32[448,128]{1,0:T(8,128)S(1)} %get-tuple-element.56), channel_id=1, source_target_pairs={{0,1},{1,0},{2,3},{3,2},{4,5},{5,4},{6,7},{7,6},{8,9},{9,8},{10,11... | collective-permute-start | bytes 688136 | tf_op jit(solution)/shard_map/ppermute | solution.py:607
  95.7 8.1 %collective-permute-start.7 = (f32[448,128]{1,0:T(8,128)S(1)}, f32[448,128]{1,0:T(8,128)S(1)}, u32[]{:S(2)}, u32[]{:S(2)}) collective-permute-start(f32[448,128]{1,0:T(8,128)S(1)} %bitcast.8), channel_id=1, source_target_pairs={{0,1},{1,0},{2,3},{3,2},{4,5},{5,4},{6,7},{7,6},{8,9},{9,8},{10,11... | collective-permute-start | bytes 688136 | tf_op jit(solution)/shard_map/ppermute | solution.py:632

commit v6 on v5

--- a/solution.py
+++ b/solution.py
@@ -486,7 +486,7 @@
     first, second = [], []
     for core in range(2):
         part = ids[..., core]
-        if core == 0 or y != zh * zl:
+        if core == 1 or y != zh * zl:
             first += part.transpose(0, 3, 1, 2).reshape(zh * zl, x * y).tolist()
             second += part.transpose(1, 2, 0, 3).reshape(x * y, zh * zl).tolist()
         else:

time: 105 us -> 106 us (level); the launches traced: 105 us -> 105 us
  transfers between devices with their start and end apart: 8 -> 8, of which waited for: 2 -> 2; matrix products, arithmetic and copies ran while one was open for 0% -> 0% of each run, Pallas kernels for 12% -> 11%
where the time goes in v6:
time: 106 us; the launch traced here: 105 us
  blocking collectives  57.3 us (54%)
  starting transfers between devices  26.9 us (25%)
  Pallas kernels  17.1 us (16%)
  waiting for transfers between devices  1.51 us (1%)
    all_to_all x3, blocking collectives, trade(): x = lax.all_to_all(x, AX, 0, 0, tiled=True, axis_index_groups=groups)  57.3 us
    ppermute x3, starting transfers between devices, both_ways(): up = lax.ppermute(high, AX, steps)  14.4 us
    pallas_call x2, Pallas kernels, more(): pl.pallas_call(functools.partial(next_kernel, part, len(earlier) // 2), i...  6.45 us
    ppermute x1, starting transfers between devices, shards(): rest = lax.ppermute(whole, AX, swap)  6.04 us
    ppermute x3, starting transfers between devices, both_ways(): down = lax.ppermute(low, AX, [(b, a) for a, b in steps])  4.5 us
    pallas_call x1, Pallas kernels, shards(): pl.pallas_call(functools.partial(first_kernel, parts[0]), in_specs=[VM, A...  2.96 us
  transfers between devices with their start and end apart: 8, of which 2 were waited for; matrix products, arithmetic and copies ran while one was open for 0% of the time, Pallas kernels for 11%

profile of v6, /device:TPU:1, one launch (start us, length us, event | category | flops | bytes accessed | tf_op | source)
XLA Modules:
  0.0 104.6 jit_solution(10512209008258140275)
XLA Ops:
  0.6 1.9 %prep.1 = (f32[2048,128]{1,0:T(8,128)S(1)}, f32[96,128]{1,0:T(8,128)S(1)}, f32[96,128]{1,0:T(8,128)S(1)}, f32[2,192,128]{2,1,0:T(8,128)S(1)}, f32[2,192,128]{2,1,0:T(8,128)S(1)}) custom-call(s32[1]{0:T(128)} %bitcast.core, s32[3]{0:T(128)} %send_h.1, f32[4,64,512]{2,1,0:T(8,128)} %cot_h.1, f32[4,64,512]{2,1,0:T(8,128)} %pre_h.1, s32[4,512]{1,0:T(4,128)} %act.3), custom_call_target="tpu_custom_call" | custom-call | tf_op jit(solution)/shard_map/prep/pallas_call | solution.py:521
  2.5 3.9 %collective-permute-start = (f32[96,128]{1,0:T(8,128)S(1)}, f32[96,128]{1,0:T(8,128)S(1)}, u32[]{:S(2)}, u32[]{:S(2)}) collective-permute-start(f32[96,128]{1,0:T(8,128)S(1)} %get-tuple-element.32), channel_id=1, source_target_pairs={{0,64},{64,128},{128,192},{192,256},{256,320},{320,384},{384,448},... | collective-permute-start | bytes 147464 | tf_op jit(solution)/shard_map/ppermute | solution.py:479
  6.5 1.3 %collective-permute-start.1 = (f32[96,128]{1,0:T(8,128)S(1)}, f32[96,128]{1,0:T(8,128)S(1)}, u32[]{:S(2)}, u32[]{:S(2)}) collective-permute-start(f32[96,128]{1,0:T(8,128)S(1)} %get-tuple-element.33), channel_id=1, source_target_pairs={{64,0},{128,64},{192,128},{256,192},{320,256},{384,320},{448,384},... | collective-permute-start | bytes 147464 | tf_op jit(solution)/shard_map/ppermute | solution.py:480
  7.8 0.7 copy-done
  8.5 3.0 %interior0.1 = (f32[512,128]{1,0:T(8,128)S(1)}, f32[512,128]{1,0:T(8,128)S(1)}, f32[384,1152]{1,0:T(8,128)S(1)}, bf16[384,1152]{1,0:T(8,128)(2,1)S(1)}, f32[8,128]{1,0:T(8,128)S(1)}) custom-call(f32[2048,128]{1,0:T(8,128)S(1)} %get-tuple-element.31.gd.refs_0_, f32[4,64,512]{2,1,0:T(8,128)} %refs_1_.3, s32[4,512]{1,0:T(4,128)S(1)} %copy-done, ...), custom_call_target="tpu_custom_call" | custom-call | tf_op jit(solution)/shard_map/interior0/pallas_call | solution.py:552
  11.5 3.2 %collective-permute-start.2 = (f32[120,128]{1,0:T(8,128)S(1)}, f32[120,128]{1,0:T(8,128)S(1)}, u32[]{:S(2)}, u32[]{:S(2)}) collective-permute-start(f32[120,128]{1,0:T(8,128)S(1)} %get-tuple-element.36), channel_id=1, source_target_pairs={{0,8},{8,16},{16,24},{24,32},{32,40},{40,48},{48,56},{1,9},{9,17},... | collective-permute-start | bytes 184328 | tf_op jit(solution)/shard_map/ppermute | solution.py:479
  14.8 1.3 %collective-permute-start.3 = (f32[120,128]{1,0:T(8,128)S(1)}, f32[120,128]{1,0:T(8,128)S(1)}, u32[]{:S(2)}, u32[]{:S(2)}) collective-permute-start(f32[120,128]{1,0:T(8,128)S(1)} %get-tuple-element.37.refs_6_), channel_id=1, source_target_pairs={{8,0},{16,8},{24,16},{32,24},{40,32},{48,40},{56,48},{9,1},{17,9},... | collective-permute-start | bytes 184328 | tf_op jit(solution)/shard_map/ppermute | solution.py:480
  16.1 2.5 %interior1.1 = (f32[512,128]{1,0:T(8,128)S(1)}, f32[512,128]{1,0:T(8,128)S(1)}, f32[384,1152]{1,0:T(8,128)S(1)}, f32[8,128]{1,0:T(8,128)S(1)}, bf16[4,128,1152]{2,1,0:T(8,128)(2,1)S(1)}) custom-call(f32[2048,128]{1,0:T(8,128)S(1)} %get-tuple-element.31.gd.refs_0_, f32[4,64,512]{2,1,0:T(8,128)} %refs_1_.3, s32[4,512]{1,0:T(4,128)S(1)} %copy-done.1, ...), custom_call_target="tpu_custom_call" | custom-call | tf_op jit(solution)/shard_map/interior1/pallas_call | solution.py:563
  18.5 1.2 %collective-permute-done.3.ry1 = f32[120,128]{1,0:T(8,128)S(1)} collective-permute-done((f32[120,128]{1,0:T(8,128)S(1)}, f32[120,128]{1,0:T(8,128)S(1)}, u32[]{:S(2)}, u32[]{:S(2)}) %collective-permute-start.3) | collective-permute-done | bytes 61472 | tf_op jit(solution)/shard_map/ppermute | solution.py:480
  19.7 0.2 pack_z.1
  19.9 7.3 %collective-permute-start.4 = (f32[160,128]{1,0:T(8,128)S(1)}, f32[160,128]{1,0:T(8,128)S(1)}, u32[]{:S(2)}, u32[]{:S(2)}) collective-permute-start(f32[160,128]{1,0:T(8,128)S(1)} %get-tuple-element.42), channel_id=1, source_target_pairs={{0,1},{1,2},{2,3},{3,4},{4,5},{5,6},{6,7},{8,9},{9,10},{10,11},{11... | collective-permute-start | bytes 245768 | tf_op jit(solution)/shard_map/ppermute | solution.py:479
  27.2 1.9 %collective-permute-start.5 = (f32[160,128]{1,0:T(8,128)S(1)}, f32[160,128]{1,0:T(8,128)S(1)}, u32[]{:S(2)}, u32[]{:S(2)}) collective-permute-start(f32[160,128]{1,0:T(8,128)S(1)} %get-tuple-element.43.refs_10_), channel_id=1, source_target_pairs={{1,0},{2,1},{3,2},{4,3},{5,4},{6,5},{7,6},{9,8},{10,9},{11,10},{12... | collective-permute-start | bytes 245768 | tf_op jit(solution)/shard_map/ppermute | solution.py:480
  29.1 4.0 %interior2.1 = (f32[2048,128]{1,0:T(8,128)S(1)}, f32[2048,128]{1,0:T(8,128)S(1)}, f32[384,1152]{1,0:T(8,128)S(1)}, f32[8,128]{1,0:T(8,128)S(1)}, bf16[16,128]{1,0:T(8,128)(2,1)}) custom-call(f32[2048,128]{1,0:T(8,128)S(1)} %get-tuple-element.31.gd.refs_0_, f32[4,64,512]{2,1,0:T(8,128)} %refs_1_.3, s32[4,512]{1,0:T(4,128)S(1)} %copy-done.1, ...), custom_call_target="tpu_custom_call" | custom-call | tf_op jit(solution)/shard_map/interior2/pallas_call | solution.py:563
  33.2 1.9 %halo.1 = (f32[448,128]{1,0:T(8,128)S(1)}, f32[448,128]{1,0:T(8,128)S(1)}, bf16[24,64,1152]{2,1,0:T(8,128)(2,1)S(1)}) custom-call(s32[4,27]{1,0:T(4,128)S(1)} %copy-done.2, s32[4,27]{1,0:T(4,128)S(1)} %copy-done.4, s32[756]{0:T(1024)S(1)} %copy-done.3, s32[1]{0:T(128)} %bitcast.core, f32[2048,128]{1,0:T(8,128)S(1)} %get-tuple-element.31.gd.refs_0_, ...), custom_call_target="tpu_custom_call" | custom-call | tf_op jit(solution)/shard_map/halo/pallas_call | solution.py:591
  35.1 1.9 %collective-permute-start.6 = (f32[448,128]{1,0:T(8,128)S(1)}, f32[448,128]{1,0:T(8,128)S(1)}, u32[]{:S(2)}, u32[]{:S(2)}) collective-permute-start(f32[448,128]{1,0:T(8,128)S(1)} %get-tuple-element.56), channel_id=1, source_target_pairs={{0,1},{1,0},{2,3},{3,2},{4,5},{5,4},{6,7},{7,6},{8,9},{9,8},{10,11... | collective-permute-start | bytes 688136 | tf_op jit(solution)/shard_map/ppermute | solution.py:607
  37.0 1.1 %edges.1.pa.after = f32[2048,128]{1,0:T(8,128)S(1)} custom-call(s32[4,27]{1,0:T(4,128)S(1)} %copy-done.2, bf16[24,64,1152]{2,1,0:T(8,128)(2,1)S(1)} %get-tuple-element.52.pws, bf16[384,1152]{1,0:T(8,128)(2,1)S(1)} %get-tuple-element.39.refs_3_.rt, bf16[4,128,1152]{2,1,0:T(8,128)(2,1)S(1)} %get-tuple-element.53.rtp, f32[2048,128]{1,0:T(8,128)S(1)} %get-tuple-element.54.p), custom_call_target="tpu_custom_call" | custom-call | tf_op jit(solution)/shard_map/edges/pallas_call | solution.py:608
  38.1 0.3 collective-permute-done.6.arrived
  38.5 32.3 %all_to_all.15 = f32[224,2,128]{2,1,0:T(2,128)S(1)} all-to-all(f32[224,2,128]{2,1,0:T(2,128)S(1)} %bitcast.10), channel_id=1, replica_groups={{0,2,4,6,256,258,260,262,64,66,68,70,320,322,324,326,128,130,132,134,38..., dimensions={0} | all-to-all | bytes 458752 | tf_op jit(solution)/shard_map/all_to_all | solution.py:622
  70.8 0.1 reduce_sum.18
  70.9 11.1 %all_to_all.16 = f32[56,2,128]{2,1,0:T(2,128)S(1)} all-to-all(f32[56,2,128]{2,1,0:T(2,128)S(1)} %bitcast.14), channel_id=1, replica_groups={{0,8,16,24,32,40,48,56},{2,10,18,26,34,42,50,58},{4,12,20,28,36,44,52,6..., dimensions={0} | all-to-all | bytes 114688 | tf_op jit(solution)/shard_map/all_to_all | solution.py:622
  82.1 13.8 %all_to_all.17 = f32[224,2,128]{2,1,0:T(2,128)S(1)} all-to-all(f32[224,2,128]{2,1,0:T(2,128)S(1)} %bitcast.12), channel_id=1, replica_groups={{0,2,4,6,256,258,260,262,64,66,68,70,320,322,324,326,128,130,132,134,38..., dimensions={0} | all-to-all | bytes 458752 | tf_op jit(solution)/shard_map/all_to_all | solution.py:622
  96.0 6.0 %collective-permute-start.7 = (f32[448,128]{1,0:T(8,128)S(1)}, f32[448,128]{1,0:T(8,128)S(1)}, u32[]{:S(2)}, u32[]{:S(2)}) collective-permute-start(f32[448,128]{1,0:T(8,128)S(1)} %bitcast.8), channel_id=1, source_target_pairs={{0,1},{1,0},{2,3},{3,2},{4,5},{5,4},{6,7},{7,6},{8,9},{9,8},{10,11... | collective-permute-start | bytes 688136 | tf_op jit(solution)/shard_map/ppermute | solution.py:632
  102.0 1.4 %finish.1 = f32[4,64,512]{2,1,0:T(8,128)} custom-call(f32[2048,128]{1,0:T(8,128)S(1)} %edges.1.pa.after, s32[4,512]{1,0:T(4,128)S(1)} %copy-done.1), custom_call_target="tpu_custom_call" | custom-call | tf_op jit(solution)/shard_map/finish/pallas_call | solution.py:633
  103.4 1.1 %unpack.1 = (f32[27,64,64]{2,1,0:T(8,128)}, f32[1,64]{1,0:T(1,128)}) custom-call(s32[1]{0:T(128)} %bitcast.core, f32[448,128]{1,0:T(8,128)S(1)} %bitcast.9, f32[448,128]{1,0:T(8,128)S(1)} %collective-permute-done.7.other), custom_call_target="tpu_custom_call" | custom-call | tf_op jit(solution)/shard_map/unpack/pallas_call | solution.py:638
  (20 shorter events, 0.3 us)
Async XLA Ops:
  0.6 15.4 %copy-start.1 = (s32[4,512]{1,0:T(4,128)S(1)}, s32[4,512]{1,0:T(4,128)}, u32[]{:S(2)}) copy-start(s32[4,512]{1,0:T(4,128)} %act.3) | copy-start | bytes 24580
  2.5 8.9 %collective-permute-start = (f32[96,128]{1,0:T(8,128)S(1)}, f32[96,128]{1,0:T(8,128)S(1)}, u32[]{:S(2)}, u32[]{:S(2)}) collective-permute-start(f32[96,128]{1,0:T(8,128)S(1)} %get-tuple-element.32), channel_id=1, source_target_pairs={{0,64},{64,128},{128,192},{192,256},{256,320},{320,384},{384,448},... | collective-permute-start | bytes 147464 | tf_op jit(solution)/shard_map/ppermute | solution.py:479
  6.5 5.0 %collective-permute-start.1 = (f32[96,128]{1,0:T(8,128)S(1)}, f32[96,128]{1,0:T(8,128)S(1)}, u32[]{:S(2)}, u32[]{:S(2)}) collective-permute-start(f32[96,128]{1,0:T(8,128)S(1)} %get-tuple-element.33), channel_id=1, source_target_pairs={{64,0},{128,64},{192,128},{256,192},{320,256},{384,320},{448,384},... | collective-permute-start | bytes 147464 | tf_op jit(solution)/shard_map/ppermute | solution.py:480
  7.8 0.7 copy-start
  11.5 7.0 %collective-permute-start.2 = (f32[120,128]{1,0:T(8,128)S(1)}, f32[120,128]{1,0:T(8,128)S(1)}, u32[]{:S(2)}, u32[]{:S(2)}) collective-permute-start(f32[120,128]{1,0:T(8,128)S(1)} %get-tuple-element.36), channel_id=1, source_target_pairs={{0,8},{8,16},{16,24},{24,32},{32,40},{40,48},{48,56},{1,9},{9,17},... | collective-permute-start | bytes 184328 | tf_op jit(solution)/shard_map/ppermute | solution.py:479
  14.8 5.0 %collective-permute-start.3 = (f32[120,128]{1,0:T(8,128)S(1)}, f32[120,128]{1,0:T(8,128)S(1)}, u32[]{:S(2)}, u32[]{:S(2)}) collective-permute-start(f32[120,128]{1,0:T(8,128)S(1)} %get-tuple-element.37.refs_6_), channel_id=1, source_target_pairs={{8,0},{16,8},{24,16},{32,24},{40,32},{48,40},{56,48},{9,1},{17,9},... | collective-permute-start | bytes 184328 | tf_op jit(solution)/shard_map/ppermute | solution.py:480
  19.9 13.2 %collective-permute-start.4 = (f32[160,128]{1,0:T(8,128)S(1)}, f32[160,128]{1,0:T(8,128)S(1)}, u32[]{:S(2)}, u32[]{:S(2)}) collective-permute-start(f32[160,128]{1,0:T(8,128)S(1)} %get-tuple-element.42), channel_id=1, source_target_pairs={{0,1},{1,2},{2,3},{3,4},{4,5},{5,6},{6,7},{8,9},{9,10},{10,11},{11... | collective-permute-start | bytes 245768 | tf_op jit(solution)/shard_map/ppermute | solution.py:479
  27.2 6.0 %collective-permute-start.5 = (f32[160,128]{1,0:T(8,128)S(1)}, f32[160,128]{1,0:T(8,128)S(1)}, u32[]{:S(2)}, u32[]{:S(2)}) collective-permute-start(f32[160,128]{1,0:T(8,128)S(1)} %get-tuple-element.43.refs_10_), channel_id=1, source_target_pairs={{1,0},{2,1},{3,2},{4,3},{5,4},{6,5},{7,6},{9,8},{10,9},{11,10},{12... | collective-permute-start | bytes 245768 | tf_op jit(solution)/shard_map/ppermute | solution.py:480
  29.1 4.1 %copy-start.2 = (s32[4,27]{1,0:T(4,128)S(1)}, s32[4,27]{1,0:T(4,128)}, u32[]{:S(2)}) copy-start(s32[4,27]{1,0:T(4,128)} %od.3) | copy-start | bytes 1300
  29.1 4.1 %copy-start.3 = (s32[756]{0:T(1024)S(1)}, s32[756]{0:T(1024)}, u32[]{:S(2)}) copy-start(s32[756]{0:T(1024)} %constant.10.clone.tb) | copy-start | bytes 9076
  29.1 4.1 %copy-start.4 = (s32[4,27]{1,0:T(4,128)S(1)}, s32[4,27]{1,0:T(4,128)}, u32[]{:S(2)}) copy-start(s32[4,27]{1,0:T(4,128)} %os_.1) | copy-start | bytes 1300
  35.1 3.4 %collective-permute-start.6 = (f32[448,128]{1,0:T(8,128)S(1)}, f32[448,128]{1,0:T(8,128)S(1)}, u32[]{:S(2)}, u32[]{:S(2)}) collective-permute-start(f32[448,128]{1,0:T(8,128)S(1)} %get-tuple-element.56), channel_id=1, source_target_pairs={{0,1},{1,0},{2,3},{3,2},{4,5},{5,4},{6,7},{7,6},{8,9},{9,8},{10,11... | collective-permute-start | bytes 688136 | tf_op jit(solution)/shard_map/ppermute | solution.py:607
  96.0 7.5 %collective-permute-start.7 = (f32[448,128]{1,0:T(8,128)S(1)}, f32[448,128]{1,0:T(8,128)S(1)}, u32[]{:S(2)}, u32[]{:S(2)}) collective-permute-start(f32[448,128]{1,0:T(8,128)S(1)} %bitcast.8), channel_id=1, source_target_pairs={{0,1},{1,0},{2,3},{3,2},{4,5},{5,4},{6,7},{7,6},{8,9},{9,8},{10,11... | collective-permute-start | bytes 688136 | tf_op jit(solution)/shard_map/ppermute | solution.py:632
